TPU v7x, 32 devices: a whole 2x2x4 slice. The times are simulated.
32 devices in a mesh: dp: 8 (over y, x, core), grp: 4 (over z).
Axes of the slice: x: 2, y: 2, z: 4, core: 2. Of those that a mesh axis runs over, the one named last changes fastest.
Arguments:
- acts: bfloat16 [192, 32, 2048], P(('dp', 'grp')), may hold values from -6 to 6
- cotan: bfloat16 [192, 32, 1024], P(('dp', 'grp')), may hold values from -0.029907227 to 0.029907227
- lengths: int32 [192], P(('dp', 'grp')), may hold values from 0 to 32, as said below
- offsets: int32 [192], P(('dp', 'grp')), may hold values from 0 to 31, as said below
- kernel: float32 [32, 1024], replicated, may hold values from -1 to 1
- gamma: float32 [1024], replicated, may hold values from 0.1 to 1.9
- beta: float32 [1024], replicated, may hold values from -3 to 3
- w_out: bfloat16 [1024, 1024], replicated, may hold values from -0.1875 to 0.1875
Outputs:
- module_out: bfloat16 [192, 32, 1024], P(('dp', 'grp'))
- grad_w_out: float32 [1024, 1024], P('dp')
- grad_kernel: float32 [32, 1024], P(None, 'dp')
- grad_gamma: float32 [1024], replicated
- grad_beta: float32 [1024], replicated
Inputs may be any that keep to these rules, and one draw needn't show every extreme that they name: `lengths`: each device holds 6 slots; its used slots come first and the others have length 0. A device holds 2 to 6 utterances; the devices with dp indices i and i + 8/2 and the same grp index hold 8 together, and in every draw some such pair holds 6 and 2. Some slot has 32 frames. The utterance of a slot fills frames offsets to offsets + lengths - 1 of that slot.
All inputs are finite; a program needn't handle non-finite values.
Results may differ from a plain program's by a relative error of at most 0.005.
Values may be sent and summed in bfloat16 or wider, within the bound.
No kernel may reach another device: no remote copies, remote signals or barrier semaphores. Data moves between devices by JAX's collectives and lax.ppermute only.
A program may use at most 64 MiB of HBM per device.

v0:
```python
import functools

import jax
import jax.numpy as jnp
from jax import lax
from jax.experimental import pallas as pl
from jax.experimental.pallas import tpu as pltpu
from jax.sharding import PartitionSpec as P


LANES = 128
F32 = jnp.float32
BF16 = jnp.bfloat16


def convolve(block_acts, block_len, block_off, kernel):
    taps = kernel.shape[0]
    model_width = kernel.shape[1]
    frame_count = block_acts.shape[1]
    position = jnp.arange(frame_count, dtype=jnp.int32)
    valid = (
        (position[None, :] >= block_off[:, None])
        & (position[None, :] < (block_off + block_len)[:, None])
    ).astype(jnp.float32)
    wide_acts = block_acts.astype(jnp.float32)
    gated = (
        wide_acts[..., :model_width]
        * jax.nn.sigmoid(wide_acts[..., model_width:])
        * valid[..., None]
    )
    padded = jnp.pad(gated, ((0, 0), (taps // 2 - 1, taps // 2), (0, 0)))
    conv_out = padded[:, 0:frame_count] * kernel[0]
    for tap in range(1, taps):
        conv_out = conv_out + padded[:, tap : tap + frame_count] * kernel[tap]
    return (valid, padded, conv_out)


def local_general(acts, cotan, lengths, offsets, kernel, gamma, beta, w_out):
    model_width = w_out.shape[0]
    taps = kernel.shape[0]
    valid, padded, conv_out = convolve(acts, lengths, offsets, kernel)
    masked = conv_out * valid[..., None]
    sum_first, sum_second, frame_total = lax.psum(
        (
            jnp.sum(masked, axis=(0, 1)),
            jnp.sum(masked * conv_out, axis=(0, 1)),
            jnp.sum(lengths).astype(jnp.float32),
        ),
        ("dp", "grp"),
    )
    mean_value = sum_first / frame_total
    inv_std = lax.rsqrt(sum_second / frame_total - mean_value * mean_value + 1e-05)
    normed = (conv_out - mean_value) * inv_std
    shifted = gamma * normed + beta
    sig_value = jax.nn.sigmoid(shifted)
    hidden = (shifted * sig_value * valid[..., None]).astype(jnp.bfloat16)
    flat_hidden = hidden.reshape(-1, model_width)
    flat_cotan = cotan.reshape(-1, model_width)
    outputs = (
        jnp.dot(flat_hidden, w_out, preferred_element_type=jnp.float32)
        .astype(jnp.bfloat16)
        .reshape(cotan.shape)
    )
    weight_rows = lax.psum_scatter(
        lax.dot_general(
            flat_hidden, flat_cotan, (((0,), (0,)), ((), ())), preferred_element_type=jnp.float32
        ),
        "dp",
        scatter_dimension=0,
        tiled=True,
    )
    back_hidden = lax.dot_general(
        flat_cotan, w_out, (((1,), (1,)), ((), ())), preferred_element_type=jnp.float32
    ).reshape(conv_out.shape)
    slope = back_hidden * sig_value * (1.0 + shifted * (1.0 - sig_value)) * valid[..., None]
    beta_sum, gamma_sum = lax.psum(
        (jnp.sum(slope, axis=(0, 1)), jnp.sum(slope * normed, axis=(0, 1))), ("dp", "grp")
    )
    conv_grad = (
        gamma
        * inv_std
        * (slope - beta_sum / frame_total - normed * gamma_sum / frame_total)
        * valid[..., None]
    )
    frame_count = conv_out.shape[1]
    kernel_term = jnp.stack(
        [
            jnp.sum(conv_grad * padded[:, tap : tap + frame_count], axis=(0, 1))
            for tap in range(taps)
        ],
        axis=0,
    )
    kernel_rows = lax.psum_scatter(kernel_term.T, "dp", scatter_dimension=0, tiled=True)
    weight_rows, kernel_rows = lax.psum((weight_rows, kernel_rows), "grp")
    return (outputs, weight_rows, kernel_rows.T, gamma_sum, beta_sum)


def fold(value):
    total = value[0:8]
    for at in range(8, value.shape[0], 8):
        total = total + value[at : at + 8]
    return total


def row_sum(value):
    return jnp.sum(value, axis=0, keepdims=True)


def conv_body(len_hbm, off_hbm, acts_hbm, k_hbm, g_hbm, b_hbm, gp_ref, cv_ref, st_ref, ok_ref, in_ref, gb_ref,
              acc_ref, len_ref, off_ref, acts_ref, k_ref, sems, slot_sems):
    slots, frames, wide = acts_ref.shape
    blocks, _, rows, _ = gp_ref.shape
    taps = k_ref.shape[0]
    lead = taps // 2
    small = [
        pltpu.make_async_copy(source, target, sems.at[i])
        for i, (source, target) in enumerate(
            (
                (len_hbm, len_ref),
                (off_hbm, off_ref),
                (k_hbm, k_ref),
                (g_hbm, gb_ref.at[0]),
                (b_hbm, gb_ref.at[1]),
            )
        )
    ]

    def fetch(slot):
        return pltpu.make_async_copy(acts_hbm.at[slot], acts_ref.at[slot], slot_sems.at[slot])

    small[0].start()
    small[1].start()
    fetch(0).start()
    small[2].start()
    for slot in range(1, slots):
        fetch(slot).start()
    small[3].start()
    small[4].start()
    acc_ref[...] = jnp.zeros_like(acc_ref)
    position = lax.broadcasted_iota(jnp.int32, (frames, LANES), 0)
    reach = lax.broadcasted_iota(jnp.int32, (taps, frames), 1)
    reach = reach - lax.broadcasted_iota(jnp.int32, (taps, frames), 0) + (lead - 1)
    for copy in small[:3]:
        copy.wait()

    def one(slot, carry):
        low = off_ref[slot]
        high = low + len_ref[slot]
        valid = ((position >= low) & (position < high)).astype(F32)
        ok_ref[slot] = valid
        in_ref[slot] = (
            (reach >= low) & (reach < high) & (reach >= 0) & (reach < frames)
        ).astype(F32)
        fetch(slot).wait()
        for block in range(blocks):
            cols = slice(block * LANES, (block + 1) * LANES)
            gate = slice(wide // 2 + block * LANES, wide // 2 + (block + 1) * LANES)
            left, right = acts_ref[slot, :, cols].astype(F32), acts_ref[slot, :, gate].astype(F32)
            gp_ref[block, slot, 0:lead, :] = jnp.zeros((lead, LANES), F32)
            gp_ref[block, slot, lead : lead + frames, :] = left * jax.nn.sigmoid(right) * valid
            tail = jnp.zeros((rows - lead - frames, LANES), F32)
            gp_ref[block, slot, lead + frames : rows, :] = tail
        for block in range(blocks):
            cols = slice(block * LANES, (block + 1) * LANES)
            total = gp_ref[block, slot, 1 : 1 + frames, :] * k_ref[0:1, cols]
            for tap in range(1, taps):
                lag = gp_ref[block, slot, 1 + tap : 1 + tap + frames, :]
                total = total + lag * k_ref[tap : tap + 1, cols]
            cv_ref[block, slot] = total
            masked = total * valid
            acc_ref[0, block] += fold(masked)
            acc_ref[1, block] += fold(masked * total)
        return carry

    lax.fori_loop(0, slots, one, 0)
    small[3].wait()
    small[4].wait()
    for block in range(blocks):
        cols = slice(block * LANES, (block + 1) * LANES)
        st_ref[0:1, cols] = row_sum(acc_ref[0, block])
        st_ref[1:2, cols] = row_sum(acc_ref[1, block])
    count = len_ref[0]
    for other in range(1, slots):
        count = count + len_ref[other]
    st_ref[:, blocks * LANES :] = jnp.full((2, LANES), count.astype(F32), F32)


def lag_sums(gp_ref, block, weights, taps, group, put):
    frames = weights(0).shape[0]
    slots = gp_ref.shape[1]
    for low in range(0, taps, group):
        sums = [None] * group
        for slot in range(slots):
            weight = weights(slot)
            for j in range(group):
                at = 1 + low + j
                term = fold(weight * gp_ref[block, slot, at : at + frames, :])
                sums[j] = term if sums[j] is None else sums[j] + term
        for j in range(group):
            put(low + j, row_sum(sums[j]))


def aux_body(start, ok_ref, in_ref, gp_ref, cv_ref, out_ref, wt_ref):
    _, slots, frames, _ = cv_ref.shape
    many, _, taps, _ = out_ref.shape
    lead = taps // 2

    def one(i, carry):
        block = start + i
        for slot in range(slots):
            wt_ref[slot] = cv_ref[block, slot] * ok_ref[slot]

        def put(k, row):
            out_ref[i, 0, k : k + 1, :] = row

        lag_sums(gp_ref, block, lambda slot: wt_ref[slot], taps, 16, put)
        total = jnp.zeros((taps, LANES), F32)
        for slot in range(slots):
            inside = in_ref[slot].astype(BF16)
            rest = gp_ref[block, slot, lead : lead + frames, :]
            for _ in range(3):
                part = rest.astype(BF16)
                rest = rest - part.astype(F32)
                total = total + jnp.dot(inside, part, preferred_element_type=F32)
        out_ref[i, 1] = total
        return carry

    lax.fori_loop(0, many, one, 0)


def back_body(cotan_ref, w_ref, out_ref):
    for block in range(out_ref.shape[0]):
        rows = w_ref[block * LANES : (block + 1) * LANES, :]
        out_ref[block] = lax.dot_general(
            cotan_ref[...], rows, (((1,), (1,)), ((), ())), preferred_element_type=F32
        )


def scale_of(st_ref, block):
    width = st_ref.shape[1] - LANES
    cols = pl.ds(pl.multiple_of(block * LANES, LANES), LANES)
    count = st_ref[0:1, width:]
    mean = st_ref[0:1, cols] / count
    inv = lax.rsqrt(st_ref[1:2, cols] / count - mean * mean + 1e-05)
    return count, mean, inv


def hidden_body(st_ref, gb_ref, ok_ref, cv_ref, hid_ref):
    blocks, slots, frames, _ = cv_ref.shape

    def one(block, carry):
        _, mean, inv = scale_of(st_ref, block)
        gain, shift = gb_ref[0, pl.ds(block, 1), :], gb_ref[1, pl.ds(block, 1), :]
        for slot in range(slots):
            valid = ok_ref[slot]
            shifted = gain * ((cv_ref[block, slot] - mean) * inv) + shift
            hidden = shifted * jax.nn.sigmoid(shifted) * valid
            hid_ref[block, slot * frames : (slot + 1) * frames, :] = hidden.astype(BF16)
        return carry

    lax.fori_loop(0, blocks, one, 0)


def slope_body(st_ref, gb_ref, ok_ref, gp_ref, cv_ref, bk_ref, *refs):
    aux_refs, q_ref, sl_ref = refs[:-2], refs[-2], refs[-1]
    blocks, slots, frames, _ = cv_ref.shape
    taps = aux_refs[0].shape[2]
    each = aux_refs[0].shape[0]
    last = 3 * taps

    def one(block, aux_ref, i):
        _, mean, inv = scale_of(st_ref, block)
        gain, shift = gb_ref[0, pl.ds(block, 1), :], gb_ref[1, pl.ds(block, 1), :]
        first = second = jnp.zeros((8, LANES), F32)
        for slot in range(slots):
            normed = (cv_ref[block, slot] - mean) * inv
            shifted = gain * normed + shift
            sig = jax.nn.sigmoid(shifted)
            back = bk_ref[block, slot * frames : (slot + 1) * frames, :]
            slope = back * sig * (1.0 + shifted * (1.0 - sig)) * ok_ref[slot]
            sl_ref[slot] = slope
            first, second = first + fold(slope), second + fold(slope * normed)

        def put(k, row):
            q_ref[block, k : k + 1, :] = row

        lag_sums(gp_ref, block, lambda slot: sl_ref[slot], taps, 16, put)
        q_ref[block, taps : 2 * taps, :] = aux_ref[i, 1]
        q_ref[block, 2 * taps : last, :] = inv * (aux_ref[i, 0] - mean * aux_ref[i, 1])
        q_ref[0, pl.ds(last + block, 1), :] = row_sum(first)
        q_ref[0, pl.ds(last + blocks + block, 1), :] = row_sum(second)

    for part, aux_ref in enumerate(aux_refs):

        def step(i, carry, part=part, aux_ref=aux_ref):
            one(part * each + i, aux_ref, i)
            return carry

        lax.fori_loop(0, each, step, 0)
    for block in range(1, blocks):
        q_ref[block, last:, :] = q_ref[0, last:, :]


def out_body(hid_ref, w_ref, out_ref):
    blocks = hid_ref.shape[0]
    slots, frames, _ = out_ref.shape
    total = None
    for block in range(blocks):
        term = jnp.dot(
            hid_ref[block],
            w_ref[block * LANES : (block + 1) * LANES, :],
            preferred_element_type=F32,
        )
        total = term if total is None else total + term
    for slot in range(slots):
        out_ref[slot] = total[slot * frames : (slot + 1) * frames, :].astype(BF16)


def rows_body(masks, at_ref, recv_ref, *refs):
    pieces, (give_ref, keep_ref, held, sems) = refs[:-4], refs[-4:]
    me, half = at_ref[0], at_ref[1]
    copies = [
        pltpu.make_async_copy(piece, held.at[i], sems.at[i]) for i, piece in enumerate(pieces)
    ]
    for copy in copies:
        copy.start()
    many = give_ref.shape[0]
    width = many * LANES
    give = pl.ds(pl.multiple_of((1 - half) * width, width), width)
    keep = pl.ds(pl.multiple_of(half * width, width), width)
    totals = [None, None]
    for i, mask in enumerate(masks):
        left = recv_ref[jnp.bitwise_xor(me, mask)]
        copies[i].wait()
        for j, cols in enumerate((give, keep)):
            term = lax.dot_general(
                left, held[i, :, cols], (((0,), (0,)), ((), ())), preferred_element_type=F32
            )
            totals[j] = term if totals[j] is None else totals[j] + term
    for total, ref in zip(totals, (give_ref, keep_ref)):
        for block in range(many):
            ref[block] = total[:, block * LANES : (block + 1) * LANES].astype(BF16)


def add_body(own_ref, recv_ref, out_ref):
    out_ref[...] = (own_ref[...].astype(F32) + recv_ref[...].astype(F32)).astype(BF16)


def sum_body(lags_ref, out_ref):
    total = lags_ref[0]
    for source in range(1, lags_ref.shape[0]):
        total = total + lags_ref[source]
    out_ref[...] = total


def scale_body(at_ref, st_ref, gb_ref, out_ref):
    me = at_ref[0]
    count, _, inv = scale_of(st_ref, me)
    out_ref[0:1, :] = gb_ref[0, pl.ds(me, 1), :] * inv
    out_ref[1:2, :] = count


def last_body(taps, at_ref, own_ref, recv_ref, lags_ref, more_ref, sc_ref, rows_ref, gk_ref, gg_ref, gb_ref):
    me, half = at_ref[0], at_ref[1]
    many = own_ref.shape[0]
    for which, ref in ((half, own_ref), (1 - half, recv_ref)):
        for block in range(many):
            cols = pl.ds(pl.multiple_of((which * many + block) * LANES, LANES), LANES)
            rows_ref[:, cols] = ref[block].astype(F32)
    value = lags_ref[...] + more_ref[...]
    blocks = gb_ref.shape[0]
    gb_ref[...] = value[3 * taps : 3 * taps + blocks]
    gg_ref[...] = value[3 * taps + blocks : 3 * taps + 2 * blocks]
    count = sc_ref[1:2, :]
    mine = pl.ds(me, 1)
    gk_ref[...] = sc_ref[0:1, :] * (
        value[0:taps]
        - (gb_ref[mine, :] / count) * value[taps : 2 * taps]
        - (gg_ref[mine, :] / count) * value[2 * taps : 3 * taps]
    )


SMEM = pl.BlockSpec(memory_space=pltpu.SMEM)
VMEM = pl.BlockSpec(memory_space=pltpu.VMEM)
HBM = pl.BlockSpec(memory_space=pltpu.HBM)
ANY = pl.BlockSpec(memory_space=pl.ANY)


def in_hbm(value):
    return pltpu.with_memory_space_constraint(value, pltpu.HBM)


def call(body, shapes, scalars, args, flops=0, scratch=(), mib=8, **more):
    many = isinstance(shapes, list)
    moved = sum(a.size * a.dtype.itemsize for a in args)
    return pl.pallas_call(
        body,
        in_specs=more.pop("in_specs", None) or [SMEM] * len(scalars) + [VMEM] * len(args),
        out_specs=[VMEM] * len(shapes) if many else VMEM,
        out_shape=shapes,
        scratch_shapes=scratch,
        compiler_params=pltpu.CompilerParams(vmem_limit_bytes=mib << 20),
        cost_estimate=pl.CostEstimate(flops=flops, bytes_accessed=moved, transcendentals=0),
        **more,
    )(*scalars, *args)


def local_fast(n_dp, n_grp, acts, cotan, lengths, offsets, kernel, gamma, beta, w_out):
    slots, frames, wide = acts.shape
    width = wide // 2
    taps = kernel.shape[0]
    blocks = width // LANES
    tokens = slots * frames
    n_q = 3 * taps + 2 * blocks
    padded = 2 * (taps // 2) + frames
    me_dp, me_grp = lax.axis_index("dp"), lax.axis_index("grp")
    shape = jax.ShapeDtypeStruct

    def swap(value, dp_mask, grp_mask):
        pairs = [
            (d * n_grp + g, (d ^ dp_mask) * n_grp + (g ^ grp_mask))
            for d in range(n_dp)
            for g in range(n_grp)
        ]
        return lax.ppermute(value, ("dp", "grp"), pairs)

    dp_bits = [1 << i for i in range(n_dp.bit_length() - 1)]
    grp_bits = [1 << i for i in range(n_grp.bit_length() - 1)]
    at = jnp.stack([me_dp, me_grp % 2]).astype(jnp.int32)
    gamma2, beta2 = gamma.reshape(blocks, LANES), beta.reshape(blocks, LANES)

    flat_cotan = cotan.reshape(tokens, width)
    pieces = [(0, flat_cotan)]
    for bit in dp_bits[1:] + dp_bits[:1]:
        pieces += [(m | bit, swap(v, bit, 0)) for m, v in pieces]
    masks, values = tuple(m for m, _ in pieces), [v for _, v in pieces]

    gated, conv_out, stats, valid, inside, gains = call(
        conv_body,
        [
            shape((blocks, slots, padded, LANES), F32),
            shape((blocks, slots, frames, LANES), F32),
            shape((2, width + LANES), F32),
            shape((slots, frames, LANES), F32),
            shape((slots, taps, frames), F32),
            shape((2, blocks, LANES), F32),
        ],
        (),
        [in_hbm(value) for value in (lengths, offsets, acts, kernel, gamma2, beta2)],
        flops=4 * taps * tokens * width,
        scratch=[
            pltpu.VMEM((2, blocks, 8, LANES), F32),
            pltpu.SMEM((slots,), jnp.int32),
            pltpu.SMEM((slots,), jnp.int32),
            pltpu.VMEM(acts.shape, BF16),
            pltpu.VMEM(kernel.shape, F32),
            pltpu.SemaphoreType.DMA((5,)),
            pltpu.SemaphoreType.DMA((slots,)),
        ],
        in_specs=[HBM] * 6,
    )

    hops = [(m | 1, 0) for m in dp_bits[1:]] + [(1, m) for m in grp_bits] + [(1, 0)]
    for dp_mask, grp_mask in hops:
        stats = stats + swap(stats, dp_mask, grp_mask)

    back = call(
        back_body,
        shape((blocks, tokens, LANES), F32),
        (),
        (flat_cotan, w_out),
        flops=2 * tokens * width * width,
    )
    parts = 4
    each = blocks // parts
    aux = [
        call(
            functools.partial(aux_body, i * each),
            shape((each, 2, taps, LANES), F32),
            (),
            (valid, inside, gated, conv_out),
            flops=4 * taps * tokens * each * LANES,
            scratch=[pltpu.VMEM((slots, frames, LANES), F32)],
        )
        for i in range(parts)
    ]

    hidden = call(
        hidden_body, shape((blocks, tokens, LANES), BF16), (), (stats, gains, valid, conv_out)
    )
    received = lax.all_to_all(hidden, "dp", 0, 0, tiled=True)
    lags = call(
        slope_body,
        shape((blocks, n_q, LANES), F32),
        (),
        (stats, gains, valid, gated, conv_out, back, *aux),
        flops=4 * taps * tokens * width,
        scratch=[pltpu.VMEM((slots, frames, LANES), F32)],
    )
    lags = lax.all_to_all(lags, "dp", 0, 0, tiled=True)
    scale = call(scale_body, shape((2, LANES), F32), (at,), (stats, gains))
    outputs = call(out_body, shape(cotan.shape, BF16), (), (hidden, w_out))

    half_shape = shape((blocks // 2, LANES, LANES), BF16)
    given, kept = call(
        functools.partial(rows_body, masks),
        [half_shape] * 2,
        (at,),
        (received, *values),
        flops=2 * n_dp * tokens * LANES * width,
        scratch=[
            pltpu.VMEM((n_dp, tokens, width), BF16),
            pltpu.SemaphoreType.DMA((n_dp,)),
        ],
        in_specs=[SMEM, VMEM] + [ANY] * n_dp,
    )
    taken = swap(given, 0, 1)
    both = call(add_body, half_shape, (), (kept, taken))
    for mask in grp_bits[1:]:
        other = swap(both, 0, mask)
        both = call(add_body, half_shape, (), (both, other))
    rest = swap(both, 0, 1)

    lags = call(sum_body, shape((n_q, LANES), F32), (), (lags,))
    for mask in grp_bits[1:]:
        lags = lags + swap(lags, 0, mask)
    more = swap(lags, 0, 1)
    weight_rows, grad_kernel, gamma_sum, beta_sum = call(
        functools.partial(last_body, taps),
        [
            shape((LANES, width), F32),
            shape((taps, LANES), F32),
            shape((blocks, LANES), F32),
            shape((blocks, LANES), F32),
        ],
        (at,),
        (both, rest, lags, more, scale),
    )
    return (outputs, weight_rows, grad_kernel, gamma_sum.reshape(width), beta_sum.reshape(width))


def solution(mesh):
    n_dp, n_grp = mesh.shape["dp"], mesh.shape["grp"]

    def fits(width, taps, frames):
        return (
            n_dp & (n_dp - 1) == 0
            and n_grp & (n_grp - 1) == 0
            and n_dp >= 4
            and n_grp >= 4
            and width == n_dp * LANES
            and taps % 16 == 0
            and frames % 16 == 0
            and n_dp % 8 == 0
        )

    def local(acts, cotan, lengths, offsets, kernel, gamma, beta, w_out):
        args = (acts, cotan, lengths, offsets, kernel, gamma, beta, w_out)
        if not fits(w_out.shape[0], kernel.shape[0], acts.shape[1]):
            return local_general(*args)
        return local_fast(n_dp, n_grp, *args)

    placed = (
        P(("dp", "grp"), None, None),
        P(("dp", "grp"), None, None),
        P(("dp", "grp")),
        P(("dp", "grp")),
        P(),
        P(),
        P(),
        P(),
    )
    return jax.shard_map(
        local,
        mesh=mesh,
        in_specs=placed,
        out_specs=(P(("dp", "grp"), None, None), P("dp", None), P(None, "dp"), P(), P()),
        check_vma=False,
    )
```

profile of v0, /device:TPU:0, one launch (start us, length us, event | category | flops | bytes accessed | tf_op | source)
XLA Modules:
  0.0 81.2 jit_solution(15316717981211618549)
XLA Ops:
  0.6 3.0 %collective-permute-start.5 = (bf16[192,1024]{1,0:T(8,128)(2,1)}, bf16[192,1024]{1,0:T(8,128)(2,1)}, u32[]{:S(2)}, u32[]{:S(2)}) collective-permute-start(bf16[192,1024]{1,0:T(8,128)(2,1)} %bitcast.7), channel_id=1, source_target_pairs={{0,8},{1,9},{2,10},{3,11},{4,12},{5,13},{6,14},{7,15},{8,0},{9,1},... | collective-permute-start | bytes 1179656 | tf_op jit(solution)/shard_map/ppermute | solution.py:425
  3.7 1.5 %collective-permute-start.6 = (bf16[192,1024]{1,0:T(8,128)(2,1)}, bf16[192,1024]{1,0:T(8,128)(2,1)}, u32[]{:S(2)}, u32[]{:S(2)}) collective-permute-start(bf16[192,1024]{1,0:T(8,128)(2,1)} %bitcast.8), channel_id=1, source_target_pairs={{0,16},{1,17},{2,18},{3,19},{4,20},{5,21},{6,22},{7,23},{8,24},{9,... | collective-permute-start | bytes 1179656 | tf_op jit(solution)/shard_map/ppermute | solution.py:425
  5.2 7.9 %collective-permute-done.5.refs_1_ = bf16[192,1024]{1,0:T(8,128)(2,1)} collective-permute-done((bf16[192,1024]{1,0:T(8,128)(2,1)}, bf16[192,1024]{1,0:T(8,128)(2,1)}, u32[]{:S(2)}, u32[]{:S(2)}) %collective-permute-start.5) | collective-permute-done | bytes 393248 | tf_op jit(solution)/shard_map/ppermute | solution.py:425
  13.1 1.8 %collective-permute-start.7 = (bf16[192,1024]{1,0:T(8,128)(2,1)}, bf16[192,1024]{1,0:T(8,128)(2,1)}, u32[]{:S(2)}, u32[]{:S(2)}) collective-permute-start(bf16[192,1024]{1,0:T(8,128)(2,1)} %collective-permute-done.5.refs_1_), channel_id=1, source_target_pairs={{0,16},{1,17},{2,18},{3,19},{4,20},{5,21},{6,22},{7,23},{8,24},{9,... | collective-permute-start | bytes 1179656 | tf_op jit(solution)/shard_map/ppermute | solution.py:425
  14.9 3.2 %shard_map.119 = (f32[8,6,64,128]{3,2,1,0:T(8,128)S(1)}, f32[8,6,32,128]{3,2,1,0:T(8,128)S(1)}, f32[2,1152]{1,0:T(2,128)S(1)}, f32[6,32,128]{2,1,0:T(8,128)S(1)}...) custom-call(s32[6]{0:T(128)} %len_hbm.1, s32[6]{0:T(128)} %off_hbm.1, bf16[6,32,2048]{2,1,0:T(8,128)(2,1)} %acts_hbm.1, ...), custom_call_target="tpu_custom_call" | custom-call | flops 25165824 | bytes 925744 | tf_op jit(solution)/shard_map/pallas_call | solution.py:396
  18.1 0.1 collective-permute-start
  18.1 3.1 %collective-permute-done = f32[2,1152]{1,0:T(2,128)S(1)} collective-permute-done((f32[2,1152]{1,0:T(2,128)S(1)}, f32[2,1152]{1,0:T(2,128)S(1)}, u32[]{:S(2)}, u32[]{:S(2)}) %collective-permute-start) | collective-permute-done | bytes 9248 | tf_op jit(solution)/shard_map/ppermute | solution.py:425
  21.3 0.3 collective-permute-start.1
  21.6 2.8 %collective-permute-done.1 = f32[2,1152]{1,0:T(2,128)S(1)} collective-permute-done((f32[2,1152]{1,0:T(2,128)S(1)}, f32[2,1152]{1,0:T(2,128)S(1)}, u32[]{:S(2)}, u32[]{:S(2)}) %collective-permute-start.1) | collective-permute-done | bytes 9248 | tf_op jit(solution)/shard_map/ppermute | solution.py:425
  24.4 1.5 %collective-permute-start.2 = (f32[2,1152]{1,0:T(2,128)S(1)}, f32[2,1152]{1,0:T(2,128)S(1)}, u32[]{:S(2)}, u32[]{:S(2)}) collective-permute-start(f32[2,1152]{1,0:T(2,128)S(1)} %add.23), channel_id=1, source_target_pairs={{0,5},{1,4},{2,7},{3,6},{4,1},{5,0},{6,3},{7,2},{8,13},{9,12},{10,... | collective-permute-start | bytes 27656 | tf_op jit(solution)/shard_map/ppermute | solution.py:425
  25.8 1.6 %collective-permute-done.2 = f32[2,1152]{1,0:T(2,128)S(1)} collective-permute-done((f32[2,1152]{1,0:T(2,128)S(1)}, f32[2,1152]{1,0:T(2,128)S(1)}, u32[]{:S(2)}, u32[]{:S(2)}) %collective-permute-start.2) | collective-permute-done | bytes 9248 | tf_op jit(solution)/shard_map/ppermute | solution.py:425
  27.5 2.5 %collective-permute-start.3 = (f32[2,1152]{1,0:T(2,128)S(1)}, f32[2,1152]{1,0:T(2,128)S(1)}, u32[]{:S(2)}, u32[]{:S(2)}) collective-permute-start(f32[2,1152]{1,0:T(2,128)S(1)} %add.24), channel_id=1, source_target_pairs={{0,6},{1,7},{2,4},{3,5},{4,2},{5,3},{6,0},{7,1},{8,14},{9,15},{10,... | collective-permute-start | bytes 27656 | tf_op jit(solution)/shard_map/ppermute | solution.py:425
  29.9 1.5 %collective-permute-done.3 = f32[2,1152]{1,0:T(2,128)S(1)} collective-permute-done((f32[2,1152]{1,0:T(2,128)S(1)}, f32[2,1152]{1,0:T(2,128)S(1)}, u32[]{:S(2)}, u32[]{:S(2)}) %collective-permute-start.3) | collective-permute-done | bytes 9248 | tf_op jit(solution)/shard_map/ppermute | solution.py:425
  31.4 0.3 collective-permute-start.4
  31.7 0.9 %collective-permute-done.4 = f32[2,1152]{1,0:T(2,128)S(1)} collective-permute-done((f32[2,1152]{1,0:T(2,128)S(1)}, f32[2,1152]{1,0:T(2,128)S(1)}, u32[]{:S(2)}, u32[]{:S(2)}) %collective-permute-start.4) | collective-permute-done | bytes 9248 | tf_op jit(solution)/shard_map/ppermute | solution.py:425
  32.6 1.2 %shard_map.120.hid_ref = bf16[8,192,128]{2,1,0:T(8,128)(2,1)} custom-call(f32[2,1152]{1,0:T(2,128)S(1)} %add.26.st_ref, f32[2,8,128]{2,1,0:T(8,128)S(1)} %get-tuple-element.18.gb_ref, f32[6,32,128]{2,1,0:T(8,128)S(1)} %get-tuple-element.19.ok_ref, f32[8,6,32,128]{3,2,1,0:T(8,128)S(1)} %get-tuple-element.20.cv_ref), custom_call_target="tpu_custom_call" | custom-call | bytes 902144 | tf_op jit(solution)/shard_map/pallas_call | solution.py:396
  33.8 3.5 %all-to-all-start = ((bf16[8,192,128]{2,1,0:T(8,128)(2,1)}), bf16[8,192,128]{2,1,0:T(8,128)(2,1)S(1)}, u32[]{:S(2)}, u32[]{:S(2)}) async-start(bf16[8,192,128]{2,1,0:T(8,128)(2,1)} %shard_map.120.hid_ref), calls=%async_computation | async-start | bytes 786432 | tf_op jit(solution)/shard_map/all_to_all | solution.py:491
  37.3 0.4 collective-permute-start.8
  37.7 0.2 collective-permute-start.9
  37.8 0.3 collective-permute-start.10
  38.2 0.0 collective-permute-done.7.refs_3_
  38.2 0.2 collective-permute-start.11
  38.3 0.7 shard_map.129.refs_3_
  39.0 0.7 shard_map.128.refs_2_
  39.7 0.0 copy-start
  39.7 0.7 shard_map.127.refs_1_
  40.4 0.7 shard_map.126.refs_0_
  41.1 0.2 copy-done
  41.3 1.0 %shard_map.125.bk_ref = f32[8,192,128]{2,1,0:T(8,128)S(1)} custom-call(bf16[192,1024]{1,0:T(8,128)(2,1)S(1)} %bitcast.10, bf16[1024,1024]{1,0:T(8,128)(2,1)S(1)} %copy-done), custom_call_target="tpu_custom_call" | custom-call | flops 402653184 | bytes 2490368 | tf_op jit(solution)/shard_map/pallas_call | solution.py:396
  42.3 3.2 %shard_map.130 = f32[8,112,128]{2,1,0:T(8,128)} custom-call(f32[2,1152]{1,0:T(2,128)S(1)} %add.26.st_ref, f32[2,8,128]{2,1,0:T(8,128)S(1)} %get-tuple-element.18.gb_ref, f32[6,32,128]{2,1,0:T(8,128)S(1)} %get-tuple-element.19.ok_ref, f32[8,6,64,128]{3,2,1,0:T(8,128)S(1)} %get-tuple-element.23.gp_ref, f32[8,6,32,128]{3,2,1,0:T(8,128)S(1)} %get-tuple-element.20.cv_ref, ...), custom_call_target="tpu_custom_call" | custom-call | flops 25165824 | bytes 3523584 | tf_op jit(solution)/shard_map/pallas_call | solution.py:396
  45.4 0.1 all-to-all-done.recv_ref
  45.5 4.0 %all-to-all-start.1 = ((f32[8,112,128]{2,1,0:T(8,128)}), f32[8,112,128]{2,1,0:T(8,128)S(1)}, u32[]{:S(2)}, u32[]{:S(2)}) async-start(f32[8,112,128]{2,1,0:T(8,128)} %shard_map.130), calls=%async_computation.1 | async-start | bytes 917504 | tf_op jit(solution)/shard_map/all_to_all | solution.py:500
  49.5 0.1 pad_add_fusion.at_ref
  49.6 0.0 collective-permute-done.8.refs_4_
  49.6 0.0 collective-permute-done.9.refs_5_
  49.6 0.0 collective-permute-done.10.refs_6_
  49.6 2.9 %shard_map.122 = (bf16[4,128,128]{2,1,0:T(8,128)(2,1)S(1)}, bf16[4,128,128]{2,1,0:T(8,128)(2,1)S(1)}) custom-call(s32[2]{0:T(128)S(1)} %pad_add_fusion.at_ref, bf16[8,192,128]{2,1,0:T(8,128)(2,1)S(1)} %all-to-all-done.recv_ref, bf16[192,1024]{1,0:T(8,128)(2,1)S(1)} %bitcast.11, bf16[192,1024]{1,0:T(8,128)(2,1)} %collective-permute-done.5.refs_1_, ...), custom_call_target="tpu_custom_call" | custom-call | flops 402653184 | bytes 3538944 | tf_op jit(solution)/shard_map/pallas_call | solution.py:396
  52.5 1.6 %collective-permute-start.12 = (bf16[4,128,128]{2,1,0:T(8,128)(2,1)S(1)}, bf16[4,128,128]{2,1,0:T(8,128)(2,1)S(1)}, u32[]{:S(2)}, u32[]{:S(2)}) collective-permute-start(bf16[4,128,128]{2,1,0:T(8,128)(2,1)S(1)} %get-tuple-element.22), channel_id=1, source_target_pairs={{0,1},{1,0},{2,3},{3,2},{4,5},{5,4},{6,7},{7,6},{8,9},{9,8},{10,11... | collective-permute-start | bytes 393224 | tf_op jit(solution)/shard_map/ppermute | solution.py:425
  54.2 4.3 %collective-permute-done.12.recv_ref = bf16[4,128,128]{2,1,0:T(8,128)(2,1)S(1)} collective-permute-done((bf16[4,128,128]{2,1,0:T(8,128)(2,1)S(1)}, bf16[4,128,128]{2,1,0:T(8,128)(2,1)S(1)}, u32[]{:S(2)}, u32[]{:S(2)}) %collective-permute-start.12) | collective-permute-done | bytes 131104 | tf_op jit(solution)/shard_map/ppermute | solution.py:425
  58.5 2.7 %collective-permute-start.13 = (bf16[4,128,128]{2,1,0:T(8,128)(2,1)S(1)}, bf16[4,128,128]{2,1,0:T(8,128)(2,1)S(1)}, u32[]{:S(2)}, u32[]{:S(2)}) collective-permute-start(bf16[4,128,128]{2,1,0:T(8,128)(2,1)S(1)} %shard_map.123.own_ref), channel_id=1, source_target_pairs={{0,2},{1,3},{2,0},{3,1},{4,6},{5,7},{6,4},{7,5},{8,10},{9,11},{10,... | collective-permute-start | bytes 393224 | tf_op jit(solution)/shard_map/ppermute | solution.py:425
  61.2 6.2 %collective-permute-done.13.recv_ref = bf16[4,128,128]{2,1,0:T(8,128)(2,1)S(1)} collective-permute-done((bf16[4,128,128]{2,1,0:T(8,128)(2,1)S(1)}, bf16[4,128,128]{2,1,0:T(8,128)(2,1)S(1)}, u32[]{:S(2)}, u32[]{:S(2)}) %collective-permute-start.13) | collective-permute-done | bytes 131104 | tf_op jit(solution)/shard_map/ppermute | solution.py:425
  67.4 0.7 collective-permute-start.14
  68.2 3.4 %collective-permute-start.15 = (f32[112,128]{1,0:T(8,128)S(1)}, f32[112,128]{1,0:T(8,128)S(1)}, u32[]{:S(2)}, u32[]{:S(2)}) collective-permute-start(f32[112,128]{1,0:T(8,128)S(1)} %shard_map.131), channel_id=1, source_target_pairs={{0,2},{1,3},{2,0},{3,1},{4,6},{5,7},{6,4},{7,5},{8,10},{9,11},{10,... | collective-permute-start | bytes 172040 | tf_op jit(solution)/shard_map/ppermute | solution.py:425
  71.6 2.2 %collective-permute-done.15 = f32[112,128]{1,0:T(8,128)S(1)} collective-permute-done((f32[112,128]{1,0:T(8,128)S(1)}, f32[112,128]{1,0:T(8,128)S(1)}, u32[]{:S(2)}, u32[]{:S(2)}) %collective-permute-start.15) | collective-permute-done | bytes 57376 | tf_op jit(solution)/shard_map/ppermute | solution.py:425
  73.8 2.7 %collective-permute-start.16 = (f32[112,128]{1,0:T(8,128)S(1)}, f32[112,128]{1,0:T(8,128)S(1)}, u32[]{:S(2)}, u32[]{:S(2)}) collective-permute-start(f32[112,128]{1,0:T(8,128)S(1)} %add.28.lags_ref), channel_id=1, source_target_pairs={{0,1},{1,0},{2,3},{3,2},{4,5},{5,4},{6,7},{7,6},{8,9},{9,8},{10,11... | collective-permute-start | bytes 172040 | tf_op jit(solution)/shard_map/ppermute | solution.py:425
  76.5 0.6 shard_map.132.sc_ref
  77.1 2.7 %shard_map.121 = bf16[6,32,1024]{2,1,0:T(8,128)(2,1)} custom-call(bf16[8,192,128]{2,1,0:T(8,128)(2,1)} %shard_map.120.hid_ref, bf16[1024,1024]{1,0:T(8,128)(2,1)S(1)} %copy-done.1), custom_call_target="tpu_custom_call" | custom-call | bytes 2490368 | tf_op jit(solution)/shard_map/pallas_call | solution.py:396
  79.8 1.4 %shard_map.133 = (f32[128,1024]{1,0:T(8,128)}, f32[32,128]{1,0:T(8,128)}, f32[8,128]{1,0:T(8,128)}, f32[8,128]{1,0:T(8,128)}) custom-call(s32[2]{0:T(128)S(1)} %pad_add_fusion.at_ref, bf16[4,128,128]{2,1,0:T(8,128)(2,1)S(1)} %shard_map.124.own_ref, bf16[4,128,128]{2,1,0:T(8,128)(2,1)S(1)} %collective-permute-done.14.recv_ref, f32[112,128]{1,0:T(8,128)S(1)} %add.28.lags_ref, ...), custom_call_target="tpu_custom_call" | custom-call | bytes 377856 | tf_op jit(solution)/shard_map/pallas_call | solution.py:396
  (18 shorter events, 0.2 us)
Async XLA Ops:
  0.6 36.6 %copy-start.2 = (bf16[6,32,1024]{2,1,0:T(8,128)(2,1)S(1)}, bf16[6,32,1024]{2,1,0:T(8,128)(2,1)}, u32[]{:S(2)}) copy-start(bf16[6,32,1024]{2,1,0:T(8,128)(2,1)} %param.9) | copy-start | bytes 1179652
  0.6 12.5 %collective-permute-start.5 = (bf16[192,1024]{1,0:T(8,128)(2,1)}, bf16[192,1024]{1,0:T(8,128)(2,1)}, u32[]{:S(2)}, u32[]{:S(2)}) collective-permute-start(bf16[192,1024]{1,0:T(8,128)(2,1)} %bitcast.7), channel_id=1, source_target_pairs={{0,8},{1,9},{2,10},{3,11},{4,12},{5,13},{6,14},{7,15},{8,0},{9,1},... | collective-permute-start | bytes 1179656 | tf_op jit(solution)/shard_map/ppermute | solution.py:425
  3.7 34.2 %collective-permute-start.6 = (bf16[192,1024]{1,0:T(8,128)(2,1)}, bf16[192,1024]{1,0:T(8,128)(2,1)}, u32[]{:S(2)}, u32[]{:S(2)}) collective-permute-start(bf16[192,1024]{1,0:T(8,128)(2,1)} %bitcast.8), channel_id=1, source_target_pairs={{0,16},{1,17},{2,18},{3,19},{4,20},{5,21},{6,22},{7,23},{8,24},{9,... | collective-permute-start | bytes 1179656 | tf_op jit(solution)/shard_map/ppermute | solution.py:425
  13.1 25.1 %collective-permute-start.7 = (bf16[192,1024]{1,0:T(8,128)(2,1)}, bf16[192,1024]{1,0:T(8,128)(2,1)}, u32[]{:S(2)}, u32[]{:S(2)}) collective-permute-start(bf16[192,1024]{1,0:T(8,128)(2,1)} %collective-permute-done.5.refs_1_), channel_id=1, source_target_pairs={{0,16},{1,17},{2,18},{3,19},{4,20},{5,21},{6,22},{7,23},{8,24},{9,... | collective-permute-start | bytes 1179656 | tf_op jit(solution)/shard_map/ppermute | solution.py:425
  18.1 3.2 %collective-permute-start = (f32[2,1152]{1,0:T(2,128)S(1)}, f32[2,1152]{1,0:T(2,128)S(1)}, u32[]{:S(2)}, u32[]{:S(2)}) collective-permute-start(f32[2,1152]{1,0:T(2,128)S(1)} %get-tuple-element.17), channel_id=1, source_target_pairs={{0,12},{1,13},{2,14},{3,15},{4,8},{5,9},{6,10},{7,11},{8,4},{9,5},... | collective-permute-start | bytes 27656 | tf_op jit(solution)/shard_map/ppermute | solution.py:425
  21.3 3.1 %collective-permute-start.1 = (f32[2,1152]{1,0:T(2,128)S(1)}, f32[2,1152]{1,0:T(2,128)S(1)}, u32[]{:S(2)}, u32[]{:S(2)}) collective-permute-start(f32[2,1152]{1,0:T(2,128)S(1)} %add.22), channel_id=1, source_target_pairs={{0,20},{1,21},{2,22},{3,23},{4,16},{5,17},{6,18},{7,19},{8,28},{9,... | collective-permute-start | bytes 27656 | tf_op jit(solution)/shard_map/ppermute | solution.py:425
  24.4 3.1 %collective-permute-start.2 = (f32[2,1152]{1,0:T(2,128)S(1)}, f32[2,1152]{1,0:T(2,128)S(1)}, u32[]{:S(2)}, u32[]{:S(2)}) collective-permute-start(f32[2,1152]{1,0:T(2,128)S(1)} %add.23), channel_id=1, source_target_pairs={{0,5},{1,4},{2,7},{3,6},{4,1},{5,0},{6,3},{7,2},{8,13},{9,12},{10,... | collective-permute-start | bytes 27656 | tf_op jit(solution)/shard_map/ppermute | solution.py:425
  27.5 4.0 %collective-permute-start.3 = (f32[2,1152]{1,0:T(2,128)S(1)}, f32[2,1152]{1,0:T(2,128)S(1)}, u32[]{:S(2)}, u32[]{:S(2)}) collective-permute-start(f32[2,1152]{1,0:T(2,128)S(1)} %add.24), channel_id=1, source_target_pairs={{0,6},{1,7},{2,4},{3,5},{4,2},{5,3},{6,0},{7,1},{8,14},{9,15},{10,... | collective-permute-start | bytes 27656 | tf_op jit(solution)/shard_map/ppermute | solution.py:425
  31.4 1.2 %collective-permute-start.4 = (f32[2,1152]{1,0:T(2,128)S(1)}, f32[2,1152]{1,0:T(2,128)S(1)}, u32[]{:S(2)}, u32[]{:S(2)}) collective-permute-start(f32[2,1152]{1,0:T(2,128)S(1)} %add.25), channel_id=1, source_target_pairs={{0,4},{1,5},{2,6},{3,7},{4,0},{5,1},{6,2},{7,3},{8,12},{9,13},{10,... | collective-permute-start | bytes 27656 | tf_op jit(solution)/shard_map/ppermute | solution.py:425
  33.8 11.7 %all-to-all-start = ((bf16[8,192,128]{2,1,0:T(8,128)(2,1)}), bf16[8,192,128]{2,1,0:T(8,128)(2,1)S(1)}, u32[]{:S(2)}, u32[]{:S(2)}) async-start(bf16[8,192,128]{2,1,0:T(8,128)(2,1)} %shard_map.120.hid_ref), calls=%async_computation | async-start | bytes 786432 | tf_op jit(solution)/shard_map/all_to_all | solution.py:491
  37.3 12.3 %collective-permute-start.8 = (bf16[192,1024]{1,0:T(8,128)(2,1)S(1)}, bf16[192,1024]{1,0:T(8,128)(2,1)}, u32[]{:S(2)}, u32[]{:S(2)}) collective-permute-start(bf16[192,1024]{1,0:T(8,128)(2,1)S(1)} %bitcast.9), channel_id=1, source_target_pairs={{0,4},{1,5},{2,6},{3,7},{4,0},{5,1},{6,2},{7,3},{8,12},{9,13},{10,... | collective-permute-start | bytes 1179656 | tf_op jit(solution)/shard_map/ppermute | solution.py:425
  37.7 11.9 %collective-permute-start.9 = (bf16[192,1024]{1,0:T(8,128)(2,1)}, bf16[192,1024]{1,0:T(8,128)(2,1)}, u32[]{:S(2)}, u32[]{:S(2)}) collective-permute-start(bf16[192,1024]{1,0:T(8,128)(2,1)} %collective-permute-done.5.refs_1_), channel_id=1, source_target_pairs={{0,4},{1,5},{2,6},{3,7},{4,0},{5,1},{6,2},{7,3},{8,12},{9,13},{10,... | collective-permute-start | bytes 1179656 | tf_op jit(solution)/shard_map/ppermute | solution.py:425
  37.8 11.7 %collective-permute-start.10 = (bf16[192,1024]{1,0:T(8,128)(2,1)}, bf16[192,1024]{1,0:T(8,128)(2,1)}, u32[]{:S(2)}, u32[]{:S(2)}) collective-permute-start(bf16[192,1024]{1,0:T(8,128)(2,1)} %collective-permute-done.6.refs_2_), channel_id=1, source_target_pairs={{0,4},{1,5},{2,6},{3,7},{4,0},{5,1},{6,2},{7,3},{8,12},{9,13},{10,... | collective-permute-start | bytes 1179656 | tf_op jit(solution)/shard_map/ppermute | solution.py:425
  38.2 11.4 %collective-permute-start.11 = (bf16[192,1024]{1,0:T(8,128)(2,1)}, bf16[192,1024]{1,0:T(8,128)(2,1)}, u32[]{:S(2)}, u32[]{:S(2)}) collective-permute-start(bf16[192,1024]{1,0:T(8,128)(2,1)} %collective-permute-done.7.refs_3_), channel_id=1, source_target_pairs={{0,4},{1,5},{2,6},{3,7},{4,0},{5,1},{6,2},{7,3},{8,12},{9,13},{10,... | collective-permute-start | bytes 1179656 | tf_op jit(solution)/shard_map/ppermute | solution.py:425
  39.7 1.6 %copy-start = (bf16[1024,1024]{1,0:T(8,128)(2,1)S(1)}, bf16[1024,1024]{1,0:T(8,128)(2,1)}, u32[]{:S(2)}) copy-start(bf16[1024,1024]{1,0:T(8,128)(2,1)} %w_ref.3) | copy-start | bytes 6291460
  45.5 22.6 %all-to-all-start.1 = ((f32[8,112,128]{2,1,0:T(8,128)}), f32[8,112,128]{2,1,0:T(8,128)S(1)}, u32[]{:S(2)}, u32[]{:S(2)}) async-start(f32[8,112,128]{2,1,0:T(8,128)} %shard_map.130), calls=%async_computation.1 | async-start | bytes 917504 | tf_op jit(solution)/shard_map/all_to_all | solution.py:500
  49.6 27.5 %copy-start.1 = (bf16[1024,1024]{1,0:T(8,128)(2,1)S(1)}, bf16[1024,1024]{1,0:T(8,128)(2,1)}, u32[]{:S(2)}) copy-start(bf16[1024,1024]{1,0:T(8,128)(2,1)} %w_ref.3) | copy-start | bytes 6291460
  52.5 6.0 %collective-permute-start.12 = (bf16[4,128,128]{2,1,0:T(8,128)(2,1)S(1)}, bf16[4,128,128]{2,1,0:T(8,128)(2,1)S(1)}, u32[]{:S(2)}, u32[]{:S(2)}) collective-permute-start(bf16[4,128,128]{2,1,0:T(8,128)(2,1)S(1)} %get-tuple-element.22), channel_id=1, source_target_pairs={{0,1},{1,0},{2,3},{3,2},{4,5},{5,4},{6,7},{7,6},{8,9},{9,8},{10,11... | collective-permute-start | bytes 393224 | tf_op jit(solution)/shard_map/ppermute | solution.py:425
  58.5 8.8 %collective-permute-start.13 = (bf16[4,128,128]{2,1,0:T(8,128)(2,1)S(1)}, bf16[4,128,128]{2,1,0:T(8,128)(2,1)S(1)}, u32[]{:S(2)}, u32[]{:S(2)}) collective-permute-start(bf16[4,128,128]{2,1,0:T(8,128)(2,1)S(1)} %shard_map.123.own_ref), channel_id=1, source_target_pairs={{0,2},{1,3},{2,0},{3,1},{4,6},{5,7},{6,4},{7,5},{8,10},{9,11},{10,... | collective-permute-start | bytes 393224 | tf_op jit(solution)/shard_map/ppermute | solution.py:425
  67.4 12.4 %collective-permute-start.14 = (bf16[4,128,128]{2,1,0:T(8,128)(2,1)S(1)}, bf16[4,128,128]{2,1,0:T(8,128)(2,1)S(1)}, u32[]{:S(2)}, u32[]{:S(2)}) collective-permute-start(bf16[4,128,128]{2,1,0:T(8,128)(2,1)S(1)} %shard_map.124.own_ref), channel_id=1, source_target_pairs={{0,1},{1,0},{2,3},{3,2},{4,5},{5,4},{6,7},{7,6},{8,9},{9,8},{10,11... | collective-permute-start | bytes 393224 | tf_op jit(solution)/shard_map/ppermute | solution.py:425
  68.2 5.6 %collective-permute-start.15 = (f32[112,128]{1,0:T(8,128)S(1)}, f32[112,128]{1,0:T(8,128)S(1)}, u32[]{:S(2)}, u32[]{:S(2)}) collective-permute-start(f32[112,128]{1,0:T(8,128)S(1)} %shard_map.131), channel_id=1, source_target_pairs={{0,2},{1,3},{2,0},{3,1},{4,6},{5,7},{6,4},{7,5},{8,10},{9,11},{10,... | collective-permute-start | bytes 172040 | tf_op jit(solution)/shard_map/ppermute | solution.py:425
  73.8 6.0 %collective-permute-start.16 = (f32[112,128]{1,0:T(8,128)S(1)}, f32[112,128]{1,0:T(8,128)S(1)}, u32[]{:S(2)}, u32[]{:S(2)}) collective-permute-start(f32[112,128]{1,0:T(8,128)S(1)} %add.28.lags_ref), channel_id=1, source_target_pairs={{0,1},{1,0},{2,3},{3,2},{4,5},{5,4},{6,7},{7,6},{8,9},{9,8},{10,11... | collective-permute-start | bytes 172040 | tf_op jit(solution)/shard_map/ppermute | solution.py:425
where the time goes:
time: 81.6 us; the launch traced here: 81.2 us
  starting transfers between devices  30.6 us (38%)
  waiting for transfers between devices  30.6 us (38%)
  Pallas kernels  18.8 us (23%)
    ppermute x17, waiting for transfers between devices, swap(): return lax.ppermute(value, ('dp', 'grp'), pairs)  30.5 us
    ppermute x17, starting transfers between devices, swap(): return lax.ppermute(value, ('dp', 'grp'), pairs)  23.2 us
    pallas_call x15, Pallas kernels, call(): pl.pallas_call(body, in_specs=more.pop('in_specs', None) or [SMEM] * len(...  18.8 us
    all_to_all x1, starting transfers between devices, local_fast(): lags = lax.all_to_all(lags, 'dp', 0, 0, tiled=True)  4 us
    all_to_all x1, starting transfers between devices, local_fast(): received = lax.all_to_all(hidden, 'dp', 0, 0, tiled=True)  3.45 us
  transfers between devices with their start and end apart: 19, of which 10 were waited for; matrix products, arithmetic and copies ran while one was open for 0% of the time, Pallas kernels for 21%

commit v1 on v0

--- a/solution.py
+++ b/solution.py
@@ -261,14 +261,15 @@
     lax.fori_loop(0, blocks, one, 0)
 
 
-def slope_body(st_ref, gb_ref, ok_ref, gp_ref, cv_ref, bk_ref, *refs):
-    aux_refs, q_ref, sl_ref = refs[:-2], refs[-2], refs[-1]
+def slope_body(at_ref, st_ref, gb_ref, ok_ref, gp_ref, cv_ref, bk_ref, *refs):
+    aux_refs, (give_ref, keep_ref, sl_ref) = refs[:-3], refs[-3:]
     blocks, slots, frames, _ = cv_ref.shape
     taps = aux_refs[0].shape[2]
-    each = aux_refs[0].shape[0]
     last = 3 * taps
-
-    def one(block, aux_ref, i):
+    bit = at_ref[0] & 1
+
+    def one(i, aux_ref, odd, q_ref):
+        block = 2 * i + odd
         _, mean, inv = scale_of(st_ref, block)
         gain, shift = gb_ref[0, pl.ds(block, 1), :], gb_ref[1, pl.ds(block, 1), :]
         first = second = jnp.zeros((8, LANES), F32)
@@ -282,23 +283,28 @@
             first, second = first + fold(slope), second + fold(slope * normed)
 
         def put(k, row):
-            q_ref[block, k : k + 1, :] = row
+            q_ref[i, k : k + 1, :] = row
 
         lag_sums(gp_ref, block, lambda slot: sl_ref[slot], taps, 16, put)
-        q_ref[block, taps : 2 * taps, :] = aux_ref[i, 1]
-        q_ref[block, 2 * taps : last, :] = inv * (aux_ref[i, 0] - mean * aux_ref[i, 1])
-        q_ref[0, pl.ds(last + block, 1), :] = row_sum(first)
-        q_ref[0, pl.ds(last + blocks + block, 1), :] = row_sum(second)
-
-    for part, aux_ref in enumerate(aux_refs):
-
-        def step(i, carry, part=part, aux_ref=aux_ref):
-            one(part * each + i, aux_ref, i)
-            return carry
-
-        lax.fori_loop(0, each, step, 0)
-    for block in range(1, blocks):
-        q_ref[block, last:, :] = q_ref[0, last:, :]
+        q_ref[i, taps : 2 * taps, :] = aux_ref[odd, 1]
+        q_ref[i, 2 * taps : last, :] = inv * (aux_ref[odd, 0] - mean * aux_ref[odd, 1])
+        keep_ref[0, pl.ds(last + block, 1), :] = row_sum(first)
+        keep_ref[0, pl.ds(last + blocks + block, 1), :] = row_sum(second)
+
+    for i, aux_ref in enumerate(aux_refs):
+        one(i, aux_ref, 1 - bit, give_ref)
+        one(i, aux_ref, bit, keep_ref)
+    for i in range(len(aux_refs)):
+        give_ref[i, last:, :] = keep_ref[0, last:, :]
+        if i:
+            keep_ref[i, last:, :] = keep_ref[0, last:, :]
+
+
+def halve_body(level, at_ref, own_ref, recv_ref, give_ref, keep_ref):
+    bit = (at_ref[0] >> level) & 1
+    for i in range(give_ref.shape[0]):
+        for odd, ref in ((1 - bit, give_ref), (bit, keep_ref)):
+            ref[i] = own_ref[2 * i + odd] + recv_ref[2 * i + odd]
 
 
 def out_body(hid_ref, w_ref, out_ref):
@@ -346,13 +352,6 @@
     out_ref[...] = (own_ref[...].astype(F32) + recv_ref[...].astype(F32)).astype(BF16)
 
 
-def sum_body(lags_ref, out_ref):
-    total = lags_ref[0]
-    for source in range(1, lags_ref.shape[0]):
-        total = total + lags_ref[source]
-    out_ref[...] = total
-
-
 def scale_body(at_ref, st_ref, gb_ref, out_ref):
     me = at_ref[0]
     count, _, inv = scale_of(st_ref, me)
@@ -460,7 +459,7 @@
         in_specs=[HBM] * 6,
     )
 
-    hops = [(m | 1, 0) for m in dp_bits[1:]] + [(1, m) for m in grp_bits] + [(1, 0)]
+    hops = [(1, m) for m in grp_bits] + [(m | 1, 0) for m in dp_bits[1:]] + [(1, 0)]
     for dp_mask, grp_mask in hops:
         stats = stats + swap(stats, dp_mask, grp_mask)
 
@@ -471,8 +470,8 @@
         (flat_cotan, w_out),
         flops=2 * tokens * width * width,
     )
-    parts = 4
-    each = blocks // parts
+    parts = blocks // 2
+    each = 2
     aux = [
         call(
             functools.partial(aux_body, i * each),
@@ -489,15 +488,23 @@
         hidden_body, shape((blocks, tokens, LANES), BF16), (), (stats, gains, valid, conv_out)
     )
     received = lax.all_to_all(hidden, "dp", 0, 0, tiled=True)
-    lags = call(
+    give, lags = call(
         slope_body,
-        shape((blocks, n_q, LANES), F32),
-        (),
+        [shape((parts, n_q, LANES), F32)] * 2,
+        (at,),
         (stats, gains, valid, gated, conv_out, back, *aux),
         flops=4 * taps * tokens * width,
         scratch=[pltpu.VMEM((slots, frames, LANES), F32)],
     )
-    lags = lax.all_to_all(lags, "dp", 0, 0, tiled=True)
+    for level in range(1, len(dp_bits)):
+        came = swap(give, dp_bits[level - 1], 0)
+        give, lags = call(
+            functools.partial(halve_body, level),
+            [shape((parts >> level, n_q, LANES), F32)] * 2,
+            (at,),
+            (lags, came),
+        )
+    lags = (lags + swap(give, dp_bits[-1], 0))[0]
     scale = call(scale_body, shape((2, LANES), F32), (at,), (stats, gains))
     outputs = call(out_body, shape(cotan.shape, BF16), (), (hidden, w_out))
 
@@ -521,7 +528,6 @@
         both = call(add_body, half_shape, (), (both, other))
     rest = swap(both, 0, 1)
 
-    lags = call(sum_body, shape((n_q, LANES), F32), (), (lags,))
     for mask in grp_bits[1:]:
         lags = lags + swap(lags, 0, mask)
     more = swap(lags, 0, 1)

time: 81.6 us -> 85.9 us (1.053)
  starting transfers between devices: 30.6 us -> 33.2 us
  Pallas kernels: 18.8 us -> 20.3 us
    ppermute x17 -> x20, starting transfers between devices: 23.2 us -> 29.5 us  [swap(): return lax.ppermute(value, ('dp', 'grp'), pairs)]
    all_to_all x1 -> x0, starting transfers between devices: 4 us -> none  [local_fast(): lags = lax.all_to_all(lags, 'dp', 0, 0, tiled=True)]
    pallas_call x15 -> x16, Pallas kernels: 18.8 us -> 20.3 us  [call(): pl.pallas_call(body, in_specs=more.pop('in_specs', None) or [SMEM] * len(...]
    ppermute x17 -> x20, waiting for transfers between devices: 30.5 us -> 30.2 us  [swap(): return lax.ppermute(value, ('dp', 'grp'), pairs)]
  transfers between devices with their start and end apart: 19 -> 21, of which waited for: 10 -> 10; matrix products, arithmetic and copies ran while one was open for 0% -> 0% of each run, Pallas kernels for 21% -> 22%
where the time goes in v1:
time: 85.9 us; the launch traced here: 85.6 us
  starting transfers between devices  33.2 us (39%)
  waiting for transfers between devices  30.2 us (35%)
  Pallas kernels  20.3 us (24%)
  local copies, waits for them, and re-layouts  0.96 us (1%)
    ppermute x20, waiting for transfers between devices, swap(): return lax.ppermute(value, ('dp', 'grp'), pairs)  30.2 us
    ppermute x20, starting transfers between devices, swap(): return lax.ppermute(value, ('dp', 'grp'), pairs)  29.5 us
    pallas_call x16, Pallas kernels, call(): pl.pallas_call(body, in_specs=more.pop('in_specs', None) or [SMEM] * len(...  20.3 us
    all_to_all x1, starting transfers between devices, local_fast(): received = lax.all_to_all(hidden, 'dp', 0, 0, tiled=True)  3.69 us
  transfers between devices with their start and end apart: 21, of which 10 were waited for; matrix products, arithmetic and copies ran while one was open for 0% of the time, Pallas kernels for 22%

profile of v1, /device:TPU:0, one launch (start us, length us, event | category | flops | bytes accessed | tf_op | source)
XLA Modules:
  0.0 85.6 jit_solution(1057248571945956322)
XLA Ops:
  0.6 3.0 %collective-permute-start.5 = (bf16[192,1024]{1,0:T(8,128)(2,1)}, bf16[192,1024]{1,0:T(8,128)(2,1)}, u32[]{:S(2)}, u32[]{:S(2)}) collective-permute-start(bf16[192,1024]{1,0:T(8,128)(2,1)} %bitcast.9), channel_id=1, source_target_pairs={{0,8},{1,9},{2,10},{3,11},{4,12},{5,13},{6,14},{7,15},{8,0},{9,1},... | collective-permute-start | bytes 1179656 | tf_op jit(solution)/shard_map/ppermute | solution.py:424
  3.7 1.5 %collective-permute-start.6 = (bf16[192,1024]{1,0:T(8,128)(2,1)}, bf16[192,1024]{1,0:T(8,128)(2,1)}, u32[]{:S(2)}, u32[]{:S(2)}) collective-permute-start(bf16[192,1024]{1,0:T(8,128)(2,1)} %bitcast.10), channel_id=1, source_target_pairs={{0,16},{1,17},{2,18},{3,19},{4,20},{5,21},{6,22},{7,23},{8,24},{9,... | collective-permute-start | bytes 1179656 | tf_op jit(solution)/shard_map/ppermute | solution.py:424
  5.2 7.9 %collective-permute-done.5.refs_1_ = bf16[192,1024]{1,0:T(8,128)(2,1)} collective-permute-done((bf16[192,1024]{1,0:T(8,128)(2,1)}, bf16[192,1024]{1,0:T(8,128)(2,1)}, u32[]{:S(2)}, u32[]{:S(2)}) %collective-permute-start.5) | collective-permute-done | bytes 393248 | tf_op jit(solution)/shard_map/ppermute | solution.py:424
  13.1 1.8 %collective-permute-start.7 = (bf16[192,1024]{1,0:T(8,128)(2,1)}, bf16[192,1024]{1,0:T(8,128)(2,1)}, u32[]{:S(2)}, u32[]{:S(2)}) collective-permute-start(bf16[192,1024]{1,0:T(8,128)(2,1)} %collective-permute-done.5.refs_1_), channel_id=1, source_target_pairs={{0,16},{1,17},{2,18},{3,19},{4,20},{5,21},{6,22},{7,23},{8,24},{9,... | collective-permute-start | bytes 1179656 | tf_op jit(solution)/shard_map/ppermute | solution.py:424
  14.9 0.5 collective-permute-start.9
  15.4 8.3 %collective-permute-done.7.refs_3_ = bf16[192,1024]{1,0:T(8,128)(2,1)} collective-permute-done((bf16[192,1024]{1,0:T(8,128)(2,1)}, bf16[192,1024]{1,0:T(8,128)(2,1)}, u32[]{:S(2)}, u32[]{:S(2)}) %collective-permute-start.7) | collective-permute-done | bytes 393248 | tf_op jit(solution)/shard_map/ppermute | solution.py:424
  23.7 3.2 %shard_map.119 = (f32[8,6,64,128]{3,2,1,0:T(8,128)S(1)}, f32[8,6,32,128]{3,2,1,0:T(8,128)S(1)}, f32[2,1152]{1,0:T(2,128)S(1)}, f32[6,32,128]{2,1,0:T(8,128)S(1)}...) custom-call(s32[6]{0:T(128)} %len_hbm.1, s32[6]{0:T(128)} %off_hbm.1, bf16[6,32,2048]{2,1,0:T(8,128)(2,1)} %acts_hbm.1, ...), custom_call_target="tpu_custom_call" | custom-call | flops 25165824 | bytes 925744 | tf_op jit(solution)/shard_map/pallas_call | solution.py:395
  26.9 1.7 %collective-permute-start = (f32[2,1152]{1,0:T(2,128)S(1)}, f32[2,1152]{1,0:T(2,128)S(1)}, u32[]{:S(2)}, u32[]{:S(2)}) collective-permute-start(f32[2,1152]{1,0:T(2,128)S(1)} %get-tuple-element.23), channel_id=1, source_target_pairs={{0,5},{1,4},{2,7},{3,6},{4,1},{5,0},{6,3},{7,2},{8,13},{9,12},{10,... | collective-permute-start | bytes 27656 | tf_op jit(solution)/shard_map/ppermute | solution.py:424
  28.6 1.4 %collective-permute-done = f32[2,1152]{1,0:T(2,128)S(1)} collective-permute-done((f32[2,1152]{1,0:T(2,128)S(1)}, f32[2,1152]{1,0:T(2,128)S(1)}, u32[]{:S(2)}, u32[]{:S(2)}) %collective-permute-start) | collective-permute-done | bytes 9248 | tf_op jit(solution)/shard_map/ppermute | solution.py:424
  30.0 2.7 %collective-permute-start.1 = (f32[2,1152]{1,0:T(2,128)S(1)}, f32[2,1152]{1,0:T(2,128)S(1)}, u32[]{:S(2)}, u32[]{:S(2)}) collective-permute-start(f32[2,1152]{1,0:T(2,128)S(1)} %add.25), channel_id=1, source_target_pairs={{0,6},{1,7},{2,4},{3,5},{4,2},{5,3},{6,0},{7,1},{8,14},{9,15},{10,... | collective-permute-start | bytes 27656 | tf_op jit(solution)/shard_map/ppermute | solution.py:424
  32.7 1.4 %collective-permute-done.1 = f32[2,1152]{1,0:T(2,128)S(1)} collective-permute-done((f32[2,1152]{1,0:T(2,128)S(1)}, f32[2,1152]{1,0:T(2,128)S(1)}, u32[]{:S(2)}, u32[]{:S(2)}) %collective-permute-start.1) | collective-permute-done | bytes 9248 | tf_op jit(solution)/shard_map/ppermute | solution.py:424
  34.1 1.5 %collective-permute-start.2 = (f32[2,1152]{1,0:T(2,128)S(1)}, f32[2,1152]{1,0:T(2,128)S(1)}, u32[]{:S(2)}, u32[]{:S(2)}) collective-permute-start(f32[2,1152]{1,0:T(2,128)S(1)} %add.26), channel_id=1, source_target_pairs={{0,12},{1,13},{2,14},{3,15},{4,8},{5,9},{6,10},{7,11},{8,4},{9,5},... | collective-permute-start | bytes 27656 | tf_op jit(solution)/shard_map/ppermute | solution.py:424
  35.6 1.6 %collective-permute-done.2 = f32[2,1152]{1,0:T(2,128)S(1)} collective-permute-done((f32[2,1152]{1,0:T(2,128)S(1)}, f32[2,1152]{1,0:T(2,128)S(1)}, u32[]{:S(2)}, u32[]{:S(2)}) %collective-permute-start.2) | collective-permute-done | bytes 9248 | tf_op jit(solution)/shard_map/ppermute | solution.py:424
  37.2 1.5 %collective-permute-start.3 = (f32[2,1152]{1,0:T(2,128)S(1)}, f32[2,1152]{1,0:T(2,128)S(1)}, u32[]{:S(2)}, u32[]{:S(2)}) collective-permute-start(f32[2,1152]{1,0:T(2,128)S(1)} %add.27), channel_id=1, source_target_pairs={{0,20},{1,21},{2,22},{3,23},{4,16},{5,17},{6,18},{7,19},{8,28},{9,... | collective-permute-start | bytes 27656 | tf_op jit(solution)/shard_map/ppermute | solution.py:424
  38.7 1.5 %collective-permute-done.3 = f32[2,1152]{1,0:T(2,128)S(1)} collective-permute-done((f32[2,1152]{1,0:T(2,128)S(1)}, f32[2,1152]{1,0:T(2,128)S(1)}, u32[]{:S(2)}, u32[]{:S(2)}) %collective-permute-start.3) | collective-permute-done | bytes 9248 | tf_op jit(solution)/shard_map/ppermute | solution.py:424
  40.3 0.5 collective-permute-start.4
  40.7 0.8 collective-permute-done.4
  41.6 1.2 %shard_map.120.hid_ref = bf16[8,192,128]{2,1,0:T(8,128)(2,1)} custom-call(f32[2,1152]{1,0:T(2,128)S(1)} %add.29.st_ref, f32[2,8,128]{2,1,0:T(8,128)S(1)} %get-tuple-element.24.gb_ref, f32[6,32,128]{2,1,0:T(8,128)S(1)} %get-tuple-element.25.ok_ref, f32[8,6,32,128]{3,2,1,0:T(8,128)S(1)} %get-tuple-element.26.cv_ref), custom_call_target="tpu_custom_call" | custom-call | bytes 902144 | tf_op jit(solution)/shard_map/pallas_call | solution.py:395
  42.7 3.7 %all-to-all-start = ((bf16[8,192,128]{2,1,0:T(8,128)(2,1)}), bf16[8,192,128]{2,1,0:T(8,128)(2,1)S(1)}, u32[]{:S(2)}, u32[]{:S(2)}) async-start(bf16[8,192,128]{2,1,0:T(8,128)(2,1)} %shard_map.120.hid_ref), calls=%async_computation | async-start | bytes 786432 | tf_op jit(solution)/shard_map/all_to_all | solution.py:490
  46.4 0.7 shard_map.129.refs_3_
  47.1 0.7 shard_map.128.refs_2_
  47.8 0.0 copy-start
  47.8 0.0 copy-start.2
  47.8 0.7 shard_map.127.refs_1_
  48.5 0.7 shard_map.126.refs_0_
  49.1 0.2 copy-done
  49.4 0.0 copy-done.2
  49.4 1.0 %shard_map.125.bk_ref = f32[8,192,128]{2,1,0:T(8,128)S(1)} custom-call(bf16[192,1024]{1,0:T(8,128)(2,1)S(1)} %bitcast.12, bf16[1024,1024]{1,0:T(8,128)(2,1)S(1)} %copy-done), custom_call_target="tpu_custom_call" | custom-call | flops 402653184 | bytes 2490368 | tf_op jit(solution)/shard_map/pallas_call | solution.py:395
  50.4 0.1 pad_add_fusion.at_ref
  50.4 3.5 %shard_map.130 = (f32[4,112,128]{2,1,0:T(8,128)}, f32[4,112,128]{2,1,0:T(8,128)S(1)}) custom-call(s32[2]{0:T(128)S(1)} %pad_add_fusion.at_ref, f32[2,1152]{1,0:T(2,128)S(1)} %add.29.st_ref, f32[2,8,128]{2,1,0:T(8,128)S(1)} %get-tuple-element.24.gb_ref, f32[6,32,128]{2,1,0:T(8,128)S(1)} %get-tuple-element.25.ok_ref, ...), custom_call_target="tpu_custom_call" | custom-call | flops 25165824 | bytes 3523584 | tf_op jit(solution)/shard_map/pallas_call | solution.py:395
  54.0 0.7 copy-done.3
  54.7 0.5 collective-permute-start.15
  55.2 2.9 %shard_map.122 = (bf16[4,128,128]{2,1,0:T(8,128)(2,1)S(1)}, bf16[4,128,128]{2,1,0:T(8,128)(2,1)S(1)}) custom-call(s32[2]{0:T(128)S(1)} %pad_add_fusion.at_ref, bf16[8,192,128]{2,1,0:T(8,128)(2,1)S(1)} %all-to-all-done.recv_ref, bf16[192,1024]{1,0:T(8,128)(2,1)S(1)} %bitcast.13, bf16[192,1024]{1,0:T(8,128)(2,1)} %collective-permute-done.5.refs_1_, ...), custom_call_target="tpu_custom_call" | custom-call | flops 402653184 | bytes 3538944 | tf_op jit(solution)/shard_map/pallas_call | solution.py:395
  58.2 1.6 %collective-permute-start.12 = (bf16[4,128,128]{2,1,0:T(8,128)(2,1)S(1)}, bf16[4,128,128]{2,1,0:T(8,128)(2,1)S(1)}, u32[]{:S(2)}, u32[]{:S(2)}) collective-permute-start(bf16[4,128,128]{2,1,0:T(8,128)(2,1)S(1)} %get-tuple-element.28), channel_id=1, source_target_pairs={{0,1},{1,0},{2,3},{3,2},{4,5},{5,4},{6,7},{7,6},{8,9},{9,8},{10,11... | collective-permute-start | bytes 393224 | tf_op jit(solution)/shard_map/ppermute | solution.py:424
  59.8 0.6 shard_map.131
  60.4 1.7 %collective-permute-start.16 = (f32[2,112,128]{2,1,0:T(8,128)S(1)}, f32[2,112,128]{2,1,0:T(8,128)S(1)}, u32[]{:S(2)}, u32[]{:S(2)}) collective-permute-start(f32[2,112,128]{2,1,0:T(8,128)S(1)} %get-tuple-element.34), channel_id=1, source_target_pairs={{0,8},{1,9},{2,10},{3,11},{4,12},{5,13},{6,14},{7,15},{8,0},{9,1},... | collective-permute-start | bytes 344072 | tf_op jit(solution)/shard_map/ppermute | solution.py:424
  62.1 1.6 %collective-permute-done.12.recv_ref = bf16[4,128,128]{2,1,0:T(8,128)(2,1)S(1)} collective-permute-done((bf16[4,128,128]{2,1,0:T(8,128)(2,1)S(1)}, bf16[4,128,128]{2,1,0:T(8,128)(2,1)S(1)}, u32[]{:S(2)}, u32[]{:S(2)}) %collective-permute-start.12) | collective-permute-done | bytes 131104 | tf_op jit(solution)/shard_map/ppermute | solution.py:424
  63.7 2.7 %collective-permute-start.13 = (bf16[4,128,128]{2,1,0:T(8,128)(2,1)S(1)}, bf16[4,128,128]{2,1,0:T(8,128)(2,1)S(1)}, u32[]{:S(2)}, u32[]{:S(2)}) collective-permute-start(bf16[4,128,128]{2,1,0:T(8,128)(2,1)S(1)} %shard_map.123.own_ref), channel_id=1, source_target_pairs={{0,2},{1,3},{2,0},{3,1},{4,6},{5,7},{6,4},{7,5},{8,10},{9,11},{10,... | collective-permute-start | bytes 393224 | tf_op jit(solution)/shard_map/ppermute | solution.py:424
  66.4 0.6 shard_map.132
  66.9 2.1 %collective-permute-start.17 = (f32[1,112,128]{2,1,0:T(8,128)S(1)}, f32[1,112,128]{2,1,0:T(8,128)S(1)}, u32[]{:S(2)}, u32[]{:S(2)}) collective-permute-start(f32[1,112,128]{2,1,0:T(8,128)S(1)} %get-tuple-element.36), channel_id=1, source_target_pairs={{0,16},{1,17},{2,18},{3,19},{4,20},{5,21},{6,22},{7,23},{8,24},{9,... | collective-permute-start | bytes 172040 | tf_op jit(solution)/shard_map/ppermute | solution.py:424
  69.0 3.0 %collective-permute-done.13.recv_ref = bf16[4,128,128]{2,1,0:T(8,128)(2,1)S(1)} collective-permute-done((bf16[4,128,128]{2,1,0:T(8,128)(2,1)S(1)}, bf16[4,128,128]{2,1,0:T(8,128)(2,1)S(1)}, u32[]{:S(2)}, u32[]{:S(2)}) %collective-permute-start.13) | collective-permute-done | bytes 131104 | tf_op jit(solution)/shard_map/ppermute | solution.py:424
  72.1 0.7 collective-permute-start.14
  72.8 3.4 %collective-permute-start.18 = (f32[112,128]{1,0:T(8,128)S(1)}, f32[112,128]{1,0:T(8,128)S(1)}, u32[]{:S(2)}, u32[]{:S(2)}) collective-permute-start(f32[112,128]{1,0:T(8,128)S(1)} %add_bitcast_fusion), channel_id=1, source_target_pairs={{0,2},{1,3},{2,0},{3,1},{4,6},{5,7},{6,4},{7,5},{8,10},{9,11},{10,... | collective-permute-start | bytes 172040 | tf_op jit(solution)/shard_map/ppermute | solution.py:424
  76.3 2.5 %collective-permute-done.18 = f32[112,128]{1,0:T(8,128)S(1)} collective-permute-done((f32[112,128]{1,0:T(8,128)S(1)}, f32[112,128]{1,0:T(8,128)S(1)}, u32[]{:S(2)}, u32[]{:S(2)}) %collective-permute-start.18) | collective-permute-done | bytes 57376 | tf_op jit(solution)/shard_map/ppermute | solution.py:424
  78.8 2.1 %collective-permute-start.19 = (f32[112,128]{1,0:T(8,128)S(1)}, f32[112,128]{1,0:T(8,128)S(1)}, u32[]{:S(2)}, u32[]{:S(2)}) collective-permute-start(f32[112,128]{1,0:T(8,128)S(1)} %add.32.lags_ref), channel_id=1, source_target_pairs={{0,1},{1,0},{2,3},{3,2},{4,5},{5,4},{6,7},{7,6},{8,9},{9,8},{10,11... | collective-permute-start | bytes 172040 | tf_op jit(solution)/shard_map/ppermute | solution.py:424
  80.9 0.6 shard_map.133.sc_ref
  81.5 2.7 %shard_map.121 = bf16[6,32,1024]{2,1,0:T(8,128)(2,1)} custom-call(bf16[8,192,128]{2,1,0:T(8,128)(2,1)} %shard_map.120.hid_ref, bf16[1024,1024]{1,0:T(8,128)(2,1)S(1)} %copy-done.1), custom_call_target="tpu_custom_call" | custom-call | bytes 2490368 | tf_op jit(solution)/shard_map/pallas_call | solution.py:395
  84.2 1.4 %shard_map.134 = (f32[128,1024]{1,0:T(8,128)}, f32[32,128]{1,0:T(8,128)}, f32[8,128]{1,0:T(8,128)}, f32[8,128]{1,0:T(8,128)}) custom-call(s32[2]{0:T(128)S(1)} %pad_add_fusion.at_ref, bf16[4,128,128]{2,1,0:T(8,128)(2,1)S(1)} %shard_map.124.own_ref, bf16[4,128,128]{2,1,0:T(8,128)(2,1)S(1)} %collective-permute-done.14.recv_ref, f32[112,128]{1,0:T(8,128)S(1)} %add.32.lags_ref, ...), custom_call_target="tpu_custom_call" | custom-call | bytes 377856 | tf_op jit(solution)/shard_map/pallas_call | solution.py:395
  (28 shorter events, 0.2 us)
Async XLA Ops:
  0.6 12.5 %collective-permute-start.5 = (bf16[192,1024]{1,0:T(8,128)(2,1)}, bf16[192,1024]{1,0:T(8,128)(2,1)}, u32[]{:S(2)}, u32[]{:S(2)}) collective-permute-start(bf16[192,1024]{1,0:T(8,128)(2,1)} %bitcast.9), channel_id=1, source_target_pairs={{0,8},{1,9},{2,10},{3,11},{4,12},{5,13},{6,14},{7,15},{8,0},{9,1},... | collective-permute-start | bytes 1179656 | tf_op jit(solution)/shard_map/ppermute | solution.py:424
  3.7 11.7 %collective-permute-start.6 = (bf16[192,1024]{1,0:T(8,128)(2,1)}, bf16[192,1024]{1,0:T(8,128)(2,1)}, u32[]{:S(2)}, u32[]{:S(2)}) collective-permute-start(bf16[192,1024]{1,0:T(8,128)(2,1)} %bitcast.10), channel_id=1, source_target_pairs={{0,16},{1,17},{2,18},{3,19},{4,20},{5,21},{6,22},{7,23},{8,24},{9,... | collective-permute-start | bytes 1179656 | tf_op jit(solution)/shard_map/ppermute | solution.py:424
  13.1 10.6 %collective-permute-start.7 = (bf16[192,1024]{1,0:T(8,128)(2,1)}, bf16[192,1024]{1,0:T(8,128)(2,1)}, u32[]{:S(2)}, u32[]{:S(2)}) collective-permute-start(bf16[192,1024]{1,0:T(8,128)(2,1)} %collective-permute-done.5.refs_1_), channel_id=1, source_target_pairs={{0,16},{1,17},{2,18},{3,19},{4,20},{5,21},{6,22},{7,23},{8,24},{9,... | collective-permute-start | bytes 1179656 | tf_op jit(solution)/shard_map/ppermute | solution.py:424
  14.9 40.3 %collective-permute-start.8 = (bf16[192,1024]{1,0:T(8,128)(2,1)}, bf16[192,1024]{1,0:T(8,128)(2,1)}, u32[]{:S(2)}, u32[]{:S(2)}) collective-permute-start(bf16[192,1024]{1,0:T(8,128)(2,1)} %bitcast.11), channel_id=1, source_target_pairs={{0,4},{1,5},{2,6},{3,7},{4,0},{5,1},{6,2},{7,3},{8,12},{9,13},{10,... | collective-permute-start | bytes 1179656 | tf_op jit(solution)/shard_map/ppermute | solution.py:424
  14.9 40.3 %collective-permute-start.9 = (bf16[192,1024]{1,0:T(8,128)(2,1)}, bf16[192,1024]{1,0:T(8,128)(2,1)}, u32[]{:S(2)}, u32[]{:S(2)}) collective-permute-start(bf16[192,1024]{1,0:T(8,128)(2,1)} %collective-permute-done.5.refs_1_), channel_id=1, source_target_pairs={{0,4},{1,5},{2,6},{3,7},{4,0},{5,1},{6,2},{7,3},{8,12},{9,13},{10,... | collective-permute-start | bytes 1179656 | tf_op jit(solution)/shard_map/ppermute | solution.py:424
  15.4 39.8 %collective-permute-start.10 = (bf16[192,1024]{1,0:T(8,128)(2,1)}, bf16[192,1024]{1,0:T(8,128)(2,1)}, u32[]{:S(2)}, u32[]{:S(2)}) collective-permute-start(bf16[192,1024]{1,0:T(8,128)(2,1)} %collective-permute-done.6.refs_2_), channel_id=1, source_target_pairs={{0,4},{1,5},{2,6},{3,7},{4,0},{5,1},{6,2},{7,3},{8,12},{9,13},{10,... | collective-permute-start | bytes 1179656 | tf_op jit(solution)/shard_map/ppermute | solution.py:424
  23.7 31.5 %collective-permute-start.11 = (bf16[192,1024]{1,0:T(8,128)(2,1)}, bf16[192,1024]{1,0:T(8,128)(2,1)}, u32[]{:S(2)}, u32[]{:S(2)}) collective-permute-start(bf16[192,1024]{1,0:T(8,128)(2,1)} %collective-permute-done.7.refs_3_), channel_id=1, source_target_pairs={{0,4},{1,5},{2,6},{3,7},{4,0},{5,1},{6,2},{7,3},{8,12},{9,13},{10,... | collective-permute-start | bytes 1179656 | tf_op jit(solution)/shard_map/ppermute | solution.py:424
  26.9 3.2 %collective-permute-start = (f32[2,1152]{1,0:T(2,128)S(1)}, f32[2,1152]{1,0:T(2,128)S(1)}, u32[]{:S(2)}, u32[]{:S(2)}) collective-permute-start(f32[2,1152]{1,0:T(2,128)S(1)} %get-tuple-element.23), channel_id=1, source_target_pairs={{0,5},{1,4},{2,7},{3,6},{4,1},{5,0},{6,3},{7,2},{8,13},{9,12},{10,... | collective-permute-start | bytes 27656 | tf_op jit(solution)/shard_map/ppermute | solution.py:424
  30.0 4.0 %collective-permute-start.1 = (f32[2,1152]{1,0:T(2,128)S(1)}, f32[2,1152]{1,0:T(2,128)S(1)}, u32[]{:S(2)}, u32[]{:S(2)}) collective-permute-start(f32[2,1152]{1,0:T(2,128)S(1)} %add.25), channel_id=1, source_target_pairs={{0,6},{1,7},{2,4},{3,5},{4,2},{5,3},{6,0},{7,1},{8,14},{9,15},{10,... | collective-permute-start | bytes 27656 | tf_op jit(solution)/shard_map/ppermute | solution.py:424
  34.1 3.1 %collective-permute-start.2 = (f32[2,1152]{1,0:T(2,128)S(1)}, f32[2,1152]{1,0:T(2,128)S(1)}, u32[]{:S(2)}, u32[]{:S(2)}) collective-permute-start(f32[2,1152]{1,0:T(2,128)S(1)} %add.26), channel_id=1, source_target_pairs={{0,12},{1,13},{2,14},{3,15},{4,8},{5,9},{6,10},{7,11},{8,4},{9,5},... | collective-permute-start | bytes 27656 | tf_op jit(solution)/shard_map/ppermute | solution.py:424
  37.2 3.1 %collective-permute-start.3 = (f32[2,1152]{1,0:T(2,128)S(1)}, f32[2,1152]{1,0:T(2,128)S(1)}, u32[]{:S(2)}, u32[]{:S(2)}) collective-permute-start(f32[2,1152]{1,0:T(2,128)S(1)} %add.27), channel_id=1, source_target_pairs={{0,20},{1,21},{2,22},{3,23},{4,16},{5,17},{6,18},{7,19},{8,28},{9,... | collective-permute-start | bytes 27656 | tf_op jit(solution)/shard_map/ppermute | solution.py:424
  40.3 1.3 %collective-permute-start.4 = (f32[2,1152]{1,0:T(2,128)S(1)}, f32[2,1152]{1,0:T(2,128)S(1)}, u32[]{:S(2)}, u32[]{:S(2)}) collective-permute-start(f32[2,1152]{1,0:T(2,128)S(1)} %add.28), channel_id=1, source_target_pairs={{0,4},{1,5},{2,6},{3,7},{4,0},{5,1},{6,2},{7,3},{8,12},{9,13},{10,... | collective-permute-start | bytes 27656 | tf_op jit(solution)/shard_map/ppermute | solution.py:424
  42.7 12.5 %all-to-all-start = ((bf16[8,192,128]{2,1,0:T(8,128)(2,1)}), bf16[8,192,128]{2,1,0:T(8,128)(2,1)S(1)}, u32[]{:S(2)}, u32[]{:S(2)}) async-start(bf16[8,192,128]{2,1,0:T(8,128)(2,1)} %shard_map.120.hid_ref), calls=%async_computation | async-start | bytes 786432 | tf_op jit(solution)/shard_map/all_to_all | solution.py:490
  47.8 1.6 %copy-start = (bf16[1024,1024]{1,0:T(8,128)(2,1)S(1)}, bf16[1024,1024]{1,0:T(8,128)(2,1)}, u32[]{:S(2)}) copy-start(bf16[1024,1024]{1,0:T(8,128)(2,1)} %w_ref.3) | copy-start | bytes 6291460
  47.8 1.6 %copy-start.2 = (bf16[6,32,1024]{2,1,0:T(8,128)(2,1)S(1)}, bf16[6,32,1024]{2,1,0:T(8,128)(2,1)}, u32[]{:S(2)}) copy-start(bf16[6,32,1024]{2,1,0:T(8,128)(2,1)} %param.9) | copy-start | bytes 1179652
  54.0 0.7 copy-start.3
  54.7 5.1 %copy-start.4 = (f32[4,112,128]{2,1,0:T(8,128)S(1)}, f32[4,112,128]{2,1,0:T(8,128)}, u32[]{:S(2)}) copy-start(f32[4,112,128]{2,1,0:T(8,128)} %copy-done.3) | copy-start | bytes 688132
  54.7 26.8 %copy-start.1 = (bf16[1024,1024]{1,0:T(8,128)(2,1)S(1)}, bf16[1024,1024]{1,0:T(8,128)(2,1)}, u32[]{:S(2)}) copy-start(bf16[1024,1024]{1,0:T(8,128)(2,1)} %w_ref.3) | copy-start | bytes 6291460
  54.7 5.1 %collective-permute-start.15 = (f32[4,112,128]{2,1,0:T(8,128)}, f32[4,112,128]{2,1,0:T(8,128)S(1)}, u32[]{:S(2)}, u32[]{:S(2)}) collective-permute-start(f32[4,112,128]{2,1,0:T(8,128)} %get-tuple-element.32), channel_id=1, source_target_pairs={{0,4},{1,5},{2,6},{3,7},{4,0},{5,1},{6,2},{7,3},{8,12},{9,13},{10,... | collective-permute-start | bytes 688136 | tf_op jit(solution)/shard_map/ppermute | solution.py:424
  58.2 5.5 %collective-permute-start.12 = (bf16[4,128,128]{2,1,0:T(8,128)(2,1)S(1)}, bf16[4,128,128]{2,1,0:T(8,128)(2,1)S(1)}, u32[]{:S(2)}, u32[]{:S(2)}) collective-permute-start(bf16[4,128,128]{2,1,0:T(8,128)(2,1)S(1)} %get-tuple-element.28), channel_id=1, source_target_pairs={{0,1},{1,0},{2,3},{3,2},{4,5},{5,4},{6,7},{7,6},{8,9},{9,8},{10,11... | collective-permute-start | bytes 393224 | tf_op jit(solution)/shard_map/ppermute | solution.py:424
  60.4 6.0 %collective-permute-start.16 = (f32[2,112,128]{2,1,0:T(8,128)S(1)}, f32[2,112,128]{2,1,0:T(8,128)S(1)}, u32[]{:S(2)}, u32[]{:S(2)}) collective-permute-start(f32[2,112,128]{2,1,0:T(8,128)S(1)} %get-tuple-element.34), channel_id=1, source_target_pairs={{0,8},{1,9},{2,10},{3,11},{4,12},{5,13},{6,14},{7,15},{8,0},{9,1},... | collective-permute-start | bytes 344072 | tf_op jit(solution)/shard_map/ppermute | solution.py:424
  63.7 8.3 %collective-permute-start.13 = (bf16[4,128,128]{2,1,0:T(8,128)(2,1)S(1)}, bf16[4,128,128]{2,1,0:T(8,128)(2,1)S(1)}, u32[]{:S(2)}, u32[]{:S(2)}) collective-permute-start(bf16[4,128,128]{2,1,0:T(8,128)(2,1)S(1)} %shard_map.123.own_ref), channel_id=1, source_target_pairs={{0,2},{1,3},{2,0},{3,1},{4,6},{5,7},{6,4},{7,5},{8,10},{9,11},{10,... | collective-permute-start | bytes 393224 | tf_op jit(solution)/shard_map/ppermute | solution.py:424
  66.9 5.9 %collective-permute-start.17 = (f32[1,112,128]{2,1,0:T(8,128)S(1)}, f32[1,112,128]{2,1,0:T(8,128)S(1)}, u32[]{:S(2)}, u32[]{:S(2)}) collective-permute-start(f32[1,112,128]{2,1,0:T(8,128)S(1)} %get-tuple-element.36), channel_id=1, source_target_pairs={{0,16},{1,17},{2,18},{3,19},{4,20},{5,21},{6,22},{7,23},{8,24},{9,... | collective-permute-start | bytes 172040 | tf_op jit(solution)/shard_map/ppermute | solution.py:424
  72.1 12.1 %collective-permute-start.14 = (bf16[4,128,128]{2,1,0:T(8,128)(2,1)S(1)}, bf16[4,128,128]{2,1,0:T(8,128)(2,1)S(1)}, u32[]{:S(2)}, u32[]{:S(2)}) collective-permute-start(bf16[4,128,128]{2,1,0:T(8,128)(2,1)S(1)} %shard_map.124.own_ref), channel_id=1, source_target_pairs={{0,1},{1,0},{2,3},{3,2},{4,5},{5,4},{6,7},{7,6},{8,9},{9,8},{10,11... | collective-permute-start | bytes 393224 | tf_op jit(solution)/shard_map/ppermute | solution.py:424
  72.8 6.0 %collective-permute-start.18 = (f32[112,128]{1,0:T(8,128)S(1)}, f32[112,128]{1,0:T(8,128)S(1)}, u32[]{:S(2)}, u32[]{:S(2)}) collective-permute-start(f32[112,128]{1,0:T(8,128)S(1)} %add_bitcast_fusion), channel_id=1, source_target_pairs={{0,2},{1,3},{2,0},{3,1},{4,6},{5,7},{6,4},{7,5},{8,10},{9,11},{10,... | collective-permute-start | bytes 172040 | tf_op jit(solution)/shard_map/ppermute | solution.py:424
  78.8 5.3 %collective-permute-start.19 = (f32[112,128]{1,0:T(8,128)S(1)}, f32[112,128]{1,0:T(8,128)S(1)}, u32[]{:S(2)}, u32[]{:S(2)}) collective-permute-start(f32[112,128]{1,0:T(8,128)S(1)} %add.32.lags_ref), channel_id=1, source_target_pairs={{0,1},{1,0},{2,3},{3,2},{4,5},{5,4},{6,7},{7,6},{8,9},{9,8},{10,11... | collective-permute-start | bytes 172040 | tf_op jit(solution)/shard_map/ppermute | solution.py:424

commit v2 on v1

--- a/solution.py
+++ b/solution.py
@@ -134,8 +134,8 @@
     small[2].start()
     for slot in range(1, slots):
         fetch(slot).start()
-    small[3].start()
-    small[4].start()
+    for copy in small[3:]:
+        copy.start()
     acc_ref[...] = jnp.zeros_like(acc_ref)
     position = lax.broadcasted_iota(jnp.int32, (frames, LANES), 0)
     reach = lax.broadcasted_iota(jnp.int32, (taps, frames), 1)
@@ -173,8 +173,8 @@
         return carry
 
     lax.fori_loop(0, slots, one, 0)
-    small[3].wait()
-    small[4].wait()
+    for copy in small[3:]:
+        copy.wait()
     for block in range(blocks):
         cols = slice(block * LANES, (block + 1) * LANES)
         st_ref[0:1, cols] = row_sum(acc_ref[0, block])
@@ -228,8 +228,18 @@
     lax.fori_loop(0, many, one, 0)
 
 
-def back_body(cotan_ref, w_ref, out_ref):
-    for block in range(out_ref.shape[0]):
+def back_body(cotan_hbm, w_hbm, out_ref, cotan_ref, w_ref, sems):
+    blocks = out_ref.shape[0]
+    fetch = pltpu.make_async_copy(cotan_hbm, cotan_ref, sems.at[blocks])
+    fetch.start()
+    copies = []
+    for block in range(blocks):
+        rows = pl.ds(block * LANES, LANES)
+        copies.append(pltpu.make_async_copy(w_hbm.at[rows], w_ref.at[rows], sems.at[block]))
+        copies[-1].start()
+    fetch.wait()
+    for block in range(blocks):
+        copies[block].wait()
         rows = w_ref[block * LANES : (block + 1) * LANES, :]
         out_ref[block] = lax.dot_general(
             cotan_ref[...], rows, (((1,), (1,)), ((), ())), preferred_element_type=F32
@@ -261,12 +271,12 @@
     lax.fori_loop(0, blocks, one, 0)
 
 
-def slope_body(at_ref, st_ref, gb_ref, ok_ref, gp_ref, cv_ref, bk_ref, *refs):
+def slope_body(st_ref, gb_ref, ok_ref, gp_ref, cv_ref, bk_ref, *refs):
     aux_refs, (give_ref, keep_ref, sl_ref) = refs[:-3], refs[-3:]
     blocks, slots, frames, _ = cv_ref.shape
     taps = aux_refs[0].shape[2]
     last = 3 * taps
-    bit = at_ref[0] & 1
+    bit = lax.axis_index("dp") & 1
 
     def one(i, aux_ref, odd, q_ref):
         block = 2 * i + odd
@@ -300,8 +310,8 @@
             keep_ref[i, last:, :] = keep_ref[0, last:, :]
 
 
-def halve_body(level, at_ref, own_ref, recv_ref, give_ref, keep_ref):
-    bit = (at_ref[0] >> level) & 1
+def halve_body(level, own_ref, recv_ref, give_ref, keep_ref):
+    bit = (lax.axis_index("dp") >> level) & 1
     for i in range(give_ref.shape[0]):
         for odd, ref in ((1 - bit, give_ref), (bit, keep_ref)):
             ref[i] = own_ref[2 * i + odd] + recv_ref[2 * i + odd]
@@ -322,14 +332,26 @@
         out_ref[slot] = total[slot * frames : (slot + 1) * frames, :].astype(BF16)
 
 
-def rows_body(masks, at_ref, recv_ref, *refs):
+def stage_body(*refs):
+    pieces, out_ref, sems = refs[:-2], refs[-2], refs[-1]
+    copies = [
+        pltpu.make_async_copy(piece, out_ref.at[i], sems.at[i]) for i, piece in enumerate(pieces)
+    ]
+    for copy in copies:
+        copy.start()
+    for copy in copies:
+        copy.wait()
+
+
+def rows_body(masks, recv_ref, staged_ref, *refs):
     pieces, (give_ref, keep_ref, held, sems) = refs[:-4], refs[-4:]
-    me, half = at_ref[0], at_ref[1]
+    me, half = lax.axis_index("dp"), lax.axis_index("grp") & 1
     copies = [
         pltpu.make_async_copy(piece, held.at[i], sems.at[i]) for i, piece in enumerate(pieces)
     ]
     for copy in copies:
         copy.start()
+    early = staged_ref.shape[0]
     many = give_ref.shape[0]
     width = many * LANES
     give = pl.ds(pl.multiple_of((1 - half) * width, width), width)
@@ -337,10 +359,12 @@
     totals = [None, None]
     for i, mask in enumerate(masks):
         left = recv_ref[jnp.bitwise_xor(me, mask)]
-        copies[i].wait()
+        if i >= early:
+            copies[i - early].wait()
         for j, cols in enumerate((give, keep)):
+            right = staged_ref[i, :, cols] if i < early else held[i - early, :, cols]
             term = lax.dot_general(
-                left, held[i, :, cols], (((0,), (0,)), ((), ())), preferred_element_type=F32
+                left, right, (((0,), (0,)), ((), ())), preferred_element_type=F32
             )
             totals[j] = term if totals[j] is None else totals[j] + term
     for total, ref in zip(totals, (give_ref, keep_ref)):
@@ -348,25 +372,29 @@
             ref[block] = total[:, block * LANES : (block + 1) * LANES].astype(BF16)
 
 
+def plus_body(own_ref, recv_ref, out_ref):
+    out_ref[...] = own_ref[...] + recv_ref[...]
+
+
 def add_body(own_ref, recv_ref, out_ref):
     out_ref[...] = (own_ref[...].astype(F32) + recv_ref[...].astype(F32)).astype(BF16)
 
 
-def scale_body(at_ref, st_ref, gb_ref, out_ref):
-    me = at_ref[0]
+def scale_body(st_ref, gb_ref, out_ref):
+    me = lax.axis_index("dp")
     count, _, inv = scale_of(st_ref, me)
     out_ref[0:1, :] = gb_ref[0, pl.ds(me, 1), :] * inv
     out_ref[1:2, :] = count
 
 
-def last_body(taps, at_ref, own_ref, recv_ref, lags_ref, more_ref, sc_ref, rows_ref, gk_ref, gg_ref, gb_ref):
-    me, half = at_ref[0], at_ref[1]
+def last_body(taps, own_ref, recv_ref, lags_ref, more_ref, sc_ref, rows_ref, gk_ref, gg_ref, gb_ref):
+    me, half = lax.axis_index("dp"), lax.axis_index("grp") & 1
     many = own_ref.shape[0]
     for which, ref in ((half, own_ref), (1 - half, recv_ref)):
         for block in range(many):
             cols = pl.ds(pl.multiple_of((which * many + block) * LANES, LANES), LANES)
             rows_ref[:, cols] = ref[block].astype(F32)
-    value = lags_ref[...] + more_ref[...]
+    value = lags_ref[0] + more_ref[0]
     blocks = gb_ref.shape[0]
     gb_ref[...] = value[3 * taps : 3 * taps + blocks]
     gg_ref[...] = value[3 * taps + blocks : 3 * taps + 2 * blocks]
@@ -412,7 +440,6 @@
     tokens = slots * frames
     n_q = 3 * taps + 2 * blocks
     padded = 2 * (taps // 2) + frames
-    me_dp, me_grp = lax.axis_index("dp"), lax.axis_index("grp")
     shape = jax.ShapeDtypeStruct
 
     def swap(value, dp_mask, grp_mask):
@@ -423,16 +450,21 @@
         ]
         return lax.ppermute(value, ("dp", "grp"), pairs)
 
+    def plus(own, other):
+        return call(plus_body, shape(own.shape, own.dtype), (), (own, other))
+
     dp_bits = [1 << i for i in range(n_dp.bit_length() - 1)]
     grp_bits = [1 << i for i in range(n_grp.bit_length() - 1)]
-    at = jnp.stack([me_dp, me_grp % 2]).astype(jnp.int32)
     gamma2, beta2 = gamma.reshape(blocks, LANES), beta.reshape(blocks, LANES)
 
     flat_cotan = cotan.reshape(tokens, width)
     pieces = [(0, flat_cotan)]
     for bit in dp_bits[1:] + dp_bits[:1]:
         pieces += [(m | bit, swap(v, bit, 0)) for m, v in pieces]
+    late_bits = dp_bits[-1] | dp_bits[-2]
+    pieces.sort(key=lambda piece: piece[0] & late_bits == late_bits)
     masks, values = tuple(m for m, _ in pieces), [v for _, v in pieces]
+    early = sum(m & late_bits != late_bits for m in masks)
 
     gated, conv_out, stats, valid, inside, gains = call(
         conv_body,
@@ -445,7 +477,7 @@
             shape((2, blocks, LANES), F32),
         ],
         (),
-        [in_hbm(value) for value in (lengths, offsets, acts, kernel, gamma2, beta2)],
+        [in_hbm(v) for v in (lengths, offsets, acts, kernel, gamma2, beta2)],
         flops=4 * taps * tokens * width,
         scratch=[
             pltpu.VMEM((2, blocks, 8, LANES), F32),
@@ -461,14 +493,20 @@
 
     hops = [(1, m) for m in grp_bits] + [(m | 1, 0) for m in dp_bits[1:]] + [(1, 0)]
     for dp_mask, grp_mask in hops:
-        stats = stats + swap(stats, dp_mask, grp_mask)
+        stats = plus(stats, swap(stats, dp_mask, grp_mask))
 
     back = call(
         back_body,
         shape((blocks, tokens, LANES), F32),
         (),
-        (flat_cotan, w_out),
+        (in_hbm(flat_cotan), in_hbm(w_out)),
         flops=2 * tokens * width * width,
+        scratch=[
+            pltpu.VMEM(flat_cotan.shape, BF16),
+            pltpu.VMEM(w_out.shape, BF16),
+            pltpu.SemaphoreType.DMA((blocks + 1,)),
+        ],
+        in_specs=[HBM] * 2,
     )
     parts = blocks // 2
     each = 2
@@ -491,7 +529,7 @@
     give, lags = call(
         slope_body,
         [shape((parts, n_q, LANES), F32)] * 2,
-        (at,),
+        (),
         (stats, gains, valid, gated, conv_out, back, *aux),
         flops=4 * taps * tokens * width,
         scratch=[pltpu.VMEM((slots, frames, LANES), F32)],
@@ -501,25 +539,33 @@
         give, lags = call(
             functools.partial(halve_body, level),
             [shape((parts >> level, n_q, LANES), F32)] * 2,
-            (at,),
+            (),
             (lags, came),
         )
-    lags = (lags + swap(give, dp_bits[-1], 0))[0]
-    scale = call(scale_body, shape((2, LANES), F32), (at,), (stats, gains))
+    lags = plus(lags, swap(give, dp_bits[-1], 0))
+    scale = call(scale_body, shape((2, LANES), F32), (), (stats, gains))
     outputs = call(out_body, shape(cotan.shape, BF16), (), (hidden, w_out))
 
     half_shape = shape((blocks // 2, LANES, LANES), BF16)
+    staged = call(
+        stage_body,
+        shape((early, tokens, width), BF16),
+        (),
+        values[:early],
+        scratch=[pltpu.SemaphoreType.DMA((early,))],
+        in_specs=[ANY] * early,
+    )
     given, kept = call(
         functools.partial(rows_body, masks),
         [half_shape] * 2,
-        (at,),
-        (received, *values),
+        (),
+        (received, staged, *values[early:]),
         flops=2 * n_dp * tokens * LANES * width,
         scratch=[
-            pltpu.VMEM((n_dp, tokens, width), BF16),
-            pltpu.SemaphoreType.DMA((n_dp,)),
+            pltpu.VMEM((n_dp - early, tokens, width), BF16),
+            pltpu.SemaphoreType.DMA((n_dp - early,)),
         ],
-        in_specs=[SMEM, VMEM] + [ANY] * n_dp,
+        in_specs=[VMEM, VMEM] + [ANY] * (n_dp - early),
     )
     taken = swap(given, 0, 1)
     both = call(add_body, half_shape, (), (kept, taken))
@@ -528,9 +574,9 @@
         both = call(add_body, half_shape, (), (both, other))
     rest = swap(both, 0, 1)
 
-    for mask in grp_bits[1:]:
-        lags = lags + swap(lags, 0, mask)
-    more = swap(lags, 0, 1)
+    for mask in grp_bits[:-1]:
+        lags = plus(lags, swap(lags, 0, mask))
+    more = swap(lags, 0, grp_bits[-1])
     weight_rows, grad_kernel, gamma_sum, beta_sum = call(
         functools.partial(last_body, taps),
         [
@@ -539,7 +585,7 @@
             shape((blocks, LANES), F32),
             shape((blocks, LANES), F32),
         ],
-        (at,),
+        (),
         (both, rest, lags, more, scale),
     )
     return (outputs, weight_rows, grad_kernel, gamma_sum.reshape(width), beta_sum.reshape(width))

time: 85.9 us -> 87.6 us (1.020)
  Pallas kernels: 20.3 us -> 22.3 us
  starting transfers between devices: 33.2 us -> 32.2 us
  waiting for transfers between devices: 30.2 us -> 31.2 us
    pallas_call x16 -> x24, Pallas kernels: 20.3 us -> 22.3 us  [call(): pl.pallas_call(body, in_specs=more.pop('in_specs', None) or [SMEM] * len(...]
    ppermute x20, waiting for transfers between devices: 30.2 us -> 31.2 us  [swap(): return lax.ppermute(value, ('dp', 'grp'), pairs)]
    ppermute x20, starting transfers between devices: 29.5 us -> 28.5 us  [swap(): return lax.ppermute(value, ('dp', 'grp'), pairs)]
  transfers between devices with their start and end apart: 21 -> 21, of which waited for: 10 -> 10; matrix products, arithmetic and copies ran while one was open for 0% -> 0% of each run, Pallas kernels for 22% -> 25%
where the time goes in v2:
time: 87.6 us; the launch traced here: 87.2 us
  starting transfers between devices  32.2 us (37%)
  waiting for transfers between devices  31.2 us (36%)
  Pallas kernels  22.3 us (25%)
    ppermute x20, waiting for transfers between devices, swap(): return lax.ppermute(value, ('dp', 'grp'), pairs)  31.2 us
    ppermute x20, starting transfers between devices, swap(): return lax.ppermute(value, ('dp', 'grp'), pairs)  28.5 us
    pallas_call x24, Pallas kernels, call(): pl.pallas_call(body, in_specs=more.pop('in_specs', None) or [SMEM] * len(...  22.3 us
    all_to_all x1, starting transfers between devices, local_fast(): received = lax.all_to_all(hidden, 'dp', 0, 0, tiled=True)  3.69 us
  transfers between devices with their start and end apart: 21, of which 10 were waited for; matrix products, arithmetic and copies ran while one was open for 0% of the time, Pallas kernels for 25%

profile of v2, /device:TPU:0, one launch (start us, length us, event | category | flops | bytes accessed | tf_op | source)
XLA Modules:
  0.0 87.2 jit_solution(12319309347227177911)
XLA Ops:
  0.6 3.0 %collective-permute-start.5 = (bf16[192,1024]{1,0:T(8,128)(2,1)}, bf16[192,1024]{1,0:T(8,128)(2,1)}, u32[]{:S(2)}, u32[]{:S(2)}) collective-permute-start(bf16[192,1024]{1,0:T(8,128)(2,1)} %bitcast.5), channel_id=1, source_target_pairs={{0,8},{1,9},{2,10},{3,11},{4,12},{5,13},{6,14},{7,15},{8,0},{9,1},... | collective-permute-start | bytes 1179656 | tf_op jit(solution)/shard_map/ppermute | solution.py:451
  3.7 1.5 %collective-permute-start.6 = (bf16[192,1024]{1,0:T(8,128)(2,1)}, bf16[192,1024]{1,0:T(8,128)(2,1)}, u32[]{:S(2)}, u32[]{:S(2)}) collective-permute-start(bf16[192,1024]{1,0:T(8,128)(2,1)} %bitcast.6), channel_id=1, source_target_pairs={{0,16},{1,17},{2,18},{3,19},{4,20},{5,21},{6,22},{7,23},{8,24},{9,... | collective-permute-start | bytes 1179656 | tf_op jit(solution)/shard_map/ppermute | solution.py:451
  5.2 7.9 %collective-permute-done.5.refs_1_ = bf16[192,1024]{1,0:T(8,128)(2,1)} collective-permute-done((bf16[192,1024]{1,0:T(8,128)(2,1)}, bf16[192,1024]{1,0:T(8,128)(2,1)}, u32[]{:S(2)}, u32[]{:S(2)}) %collective-permute-start.5) | collective-permute-done | bytes 393248 | tf_op jit(solution)/shard_map/ppermute | solution.py:451
  13.1 1.8 %collective-permute-start.10 = (bf16[192,1024]{1,0:T(8,128)(2,1)}, bf16[192,1024]{1,0:T(8,128)(2,1)S(1)}, u32[]{:S(2)}, u32[]{:S(2)}) collective-permute-start(bf16[192,1024]{1,0:T(8,128)(2,1)} %collective-permute-done.5.refs_1_), channel_id=1, source_target_pairs={{0,16},{1,17},{2,18},{3,19},{4,20},{5,21},{6,22},{7,23},{8,24},{9,... | collective-permute-start | bytes 1179656 | tf_op jit(solution)/shard_map/ppermute | solution.py:451
  14.9 0.0 collective-permute-start.7
  14.9 0.5 collective-permute-start.8
  15.4 0.0 collective-permute-start.9
  15.4 8.2 %collective-permute-done.10.refs_0_ = bf16[192,1024]{1,0:T(8,128)(2,1)S(1)} collective-permute-done((bf16[192,1024]{1,0:T(8,128)(2,1)}, bf16[192,1024]{1,0:T(8,128)(2,1)S(1)}, u32[]{:S(2)}, u32[]{:S(2)}) %collective-permute-start.10) | collective-permute-done | bytes 393248 | tf_op jit(solution)/shard_map/ppermute | solution.py:451
  23.6 3.2 %shard_map.119 = (f32[8,6,64,128]{3,2,1,0:T(8,128)S(1)}, f32[8,6,32,128]{3,2,1,0:T(8,128)S(1)}, f32[2,1152]{1,0:T(2,128)S(1)}, f32[6,32,128]{2,1,0:T(8,128)S(1)}...) custom-call(s32[6]{0:T(128)} %len_hbm.1, s32[6]{0:T(128)} %off_hbm.1, bf16[6,32,2048]{2,1,0:T(8,128)(2,1)} %acts_hbm.1, ...), custom_call_target="tpu_custom_call" | custom-call | flops 25165824 | bytes 925744 | tf_op jit(solution)/shard_map/pallas_call | solution.py:423
  26.8 1.7 %collective-permute-start = (f32[2,1152]{1,0:T(2,128)S(1)}, f32[2,1152]{1,0:T(2,128)S(1)}, u32[]{:S(2)}, u32[]{:S(2)}) collective-permute-start(f32[2,1152]{1,0:T(2,128)S(1)} %get-tuple-element.23.own_ref), channel_id=1, source_target_pairs={{0,5},{1,4},{2,7},{3,6},{4,1},{5,0},{6,3},{7,2},{8,13},{9,12},{10,... | collective-permute-start | bytes 27656 | tf_op jit(solution)/shard_map/ppermute | solution.py:451
  28.5 1.4 %collective-permute-done.recv_ref = f32[2,1152]{1,0:T(2,128)S(1)} collective-permute-done((f32[2,1152]{1,0:T(2,128)S(1)}, f32[2,1152]{1,0:T(2,128)S(1)}, u32[]{:S(2)}, u32[]{:S(2)}) %collective-permute-start) | collective-permute-done | bytes 9248 | tf_op jit(solution)/shard_map/ppermute | solution.py:451
  29.9 2.7 %collective-permute-start.1 = (f32[2,1152]{1,0:T(2,128)S(1)}, f32[2,1152]{1,0:T(2,128)S(1)}, u32[]{:S(2)}, u32[]{:S(2)}) collective-permute-start(f32[2,1152]{1,0:T(2,128)S(1)} %shard_map.120.own_ref), channel_id=1, source_target_pairs={{0,6},{1,7},{2,4},{3,5},{4,2},{5,3},{6,0},{7,1},{8,14},{9,15},{10,... | collective-permute-start | bytes 27656 | tf_op jit(solution)/shard_map/ppermute | solution.py:451
  32.6 1.4 %collective-permute-done.1.recv_ref = f32[2,1152]{1,0:T(2,128)S(1)} collective-permute-done((f32[2,1152]{1,0:T(2,128)S(1)}, f32[2,1152]{1,0:T(2,128)S(1)}, u32[]{:S(2)}, u32[]{:S(2)}) %collective-permute-start.1) | collective-permute-done | bytes 9248 | tf_op jit(solution)/shard_map/ppermute | solution.py:451
  34.0 1.5 %collective-permute-start.2 = (f32[2,1152]{1,0:T(2,128)S(1)}, f32[2,1152]{1,0:T(2,128)S(1)}, u32[]{:S(2)}, u32[]{:S(2)}) collective-permute-start(f32[2,1152]{1,0:T(2,128)S(1)} %shard_map.121.own_ref), channel_id=1, source_target_pairs={{0,12},{1,13},{2,14},{3,15},{4,8},{5,9},{6,10},{7,11},{8,4},{9,5},... | collective-permute-start | bytes 27656 | tf_op jit(solution)/shard_map/ppermute | solution.py:451
  35.5 1.6 %collective-permute-done.2.recv_ref = f32[2,1152]{1,0:T(2,128)S(1)} collective-permute-done((f32[2,1152]{1,0:T(2,128)S(1)}, f32[2,1152]{1,0:T(2,128)S(1)}, u32[]{:S(2)}, u32[]{:S(2)}) %collective-permute-start.2) | collective-permute-done | bytes 9248 | tf_op jit(solution)/shard_map/ppermute | solution.py:451
  37.1 1.5 %collective-permute-start.3 = (f32[2,1152]{1,0:T(2,128)S(1)}, f32[2,1152]{1,0:T(2,128)S(1)}, u32[]{:S(2)}, u32[]{:S(2)}) collective-permute-start(f32[2,1152]{1,0:T(2,128)S(1)} %shard_map.122.own_ref), channel_id=1, source_target_pairs={{0,20},{1,21},{2,22},{3,23},{4,16},{5,17},{6,18},{7,19},{8,28},{9,... | collective-permute-start | bytes 27656 | tf_op jit(solution)/shard_map/ppermute | solution.py:451
  38.6 1.5 %collective-permute-done.3.recv_ref = f32[2,1152]{1,0:T(2,128)S(1)} collective-permute-done((f32[2,1152]{1,0:T(2,128)S(1)}, f32[2,1152]{1,0:T(2,128)S(1)}, u32[]{:S(2)}, u32[]{:S(2)}) %collective-permute-start.3) | collective-permute-done | bytes 9248 | tf_op jit(solution)/shard_map/ppermute | solution.py:451
  40.2 0.5 collective-permute-start.4
  40.6 0.8 collective-permute-done.4.recv_ref
  41.4 1.2 %shard_map.125.hid_ref = bf16[8,192,128]{2,1,0:T(8,128)(2,1)} custom-call(f32[2,1152]{1,0:T(2,128)S(1)} %shard_map.124.st_ref, f32[2,8,128]{2,1,0:T(8,128)S(1)} %get-tuple-element.24.gb_ref, f32[6,32,128]{2,1,0:T(8,128)S(1)} %get-tuple-element.25.ok_ref, f32[8,6,32,128]{3,2,1,0:T(8,128)S(1)} %get-tuple-element.26.cv_ref), custom_call_target="tpu_custom_call" | custom-call | bytes 902144 | tf_op jit(solution)/shard_map/pallas_call | solution.py:423
  42.6 3.7 %all-to-all-start = ((bf16[8,192,128]{2,1,0:T(8,128)(2,1)}), bf16[8,192,128]{2,1,0:T(8,128)(2,1)S(1)}, u32[]{:S(2)}, u32[]{:S(2)}) async-start(bf16[8,192,128]{2,1,0:T(8,128)(2,1)} %shard_map.125.hid_ref), calls=%async_computation | async-start | bytes 786432 | tf_op jit(solution)/shard_map/all_to_all | solution.py:528
  46.3 0.7 shard_map.132.refs_0_
  47.0 0.7 shard_map.133.refs_1_
  47.6 0.7 shard_map.134.refs_2_
  48.3 0.7 shard_map.135.refs_3_
  49.0 4.0 %shard_map.131.bk_ref = f32[8,192,128]{2,1,0:T(8,128)S(1)} custom-call(bf16[192,1024]{1,0:T(8,128)(2,1)} %bitcast.8, bf16[1024,1024]{1,0:T(8,128)(2,1)} %w_hbm.1), custom_call_target="tpu_custom_call" | custom-call | flops 402653184 | bytes 2490368 | tf_op jit(solution)/shard_map/pallas_call | solution.py:423
  53.0 0.0 copy-start.1
  53.0 3.0 %shard_map.136 = (f32[4,112,128]{2,1,0:T(8,128)}, f32[4,112,128]{2,1,0:T(8,128)S(1)}) custom-call(f32[2,1152]{1,0:T(2,128)S(1)} %shard_map.124.st_ref, f32[2,8,128]{2,1,0:T(8,128)S(1)} %get-tuple-element.24.gb_ref, f32[6,32,128]{2,1,0:T(8,128)S(1)} %get-tuple-element.25.ok_ref, f32[8,6,64,128]{3,2,1,0:T(8,128)S(1)} %get-tuple-element.29.gp_ref, ...), custom_call_target="tpu_custom_call" | custom-call | flops 25165824 | bytes 3523584 | tf_op jit(solution)/shard_map/pallas_call | solution.py:423
  56.0 0.7 copy-done.2
  56.7 0.5 collective-permute-start.15
  57.2 0.0 collective-permute-done.7.refs_3_
  57.2 0.0 collective-permute-done.8.refs_4_
  57.2 1.7 %shard_map.127.staged_ref = bf16[6,192,1024]{2,1,0:T(8,128)(2,1)S(1)} custom-call(bf16[192,1024]{1,0:T(8,128)(2,1)S(1)} %bitcast.9, bf16[192,1024]{1,0:T(8,128)(2,1)} %collective-permute-done.5.refs_1_, bf16[192,1024]{1,0:T(8,128)(2,1)} %collective-permute-done.6.refs_2_, bf16[192,1024]{1,0:T(8,128)(2,1)} %collective-permute-done.7.refs_3_, ...), custom_call_target="tpu_custom_call" | custom-call | bytes 2359296 | tf_op jit(solution)/shard_map/pallas_call | solution.py:423
  59.0 0.0 copy-start
  59.0 2.0 %shard_map.128 = (bf16[4,128,128]{2,1,0:T(8,128)(2,1)S(1)}, bf16[4,128,128]{2,1,0:T(8,128)(2,1)S(1)}) custom-call(bf16[8,192,128]{2,1,0:T(8,128)(2,1)S(1)} %all-to-all-done.recv_ref, bf16[6,192,1024]{2,1,0:T(8,128)(2,1)S(1)} %shard_map.127.staged_ref, bf16[192,1024]{1,0:T(8,128)(2,1)S(1)} %collective-permute-done.10.refs_0_, ...), custom_call_target="tpu_custom_call" | custom-call | flops 402653184 | bytes 3538944 | tf_op jit(solution)/shard_map/pallas_call | solution.py:423
  61.0 1.6 %collective-permute-start.12 = (bf16[4,128,128]{2,1,0:T(8,128)(2,1)S(1)}, bf16[4,128,128]{2,1,0:T(8,128)(2,1)S(1)}, u32[]{:S(2)}, u32[]{:S(2)}) collective-permute-start(bf16[4,128,128]{2,1,0:T(8,128)(2,1)S(1)} %get-tuple-element.28), channel_id=1, source_target_pairs={{0,1},{1,0},{2,3},{3,2},{4,5},{5,4},{6,7},{7,6},{8,9},{9,8},{10,11... | collective-permute-start | bytes 393224 | tf_op jit(solution)/shard_map/ppermute | solution.py:451
  62.6 1.0 %shard_map.137 = (f32[2,112,128]{2,1,0:T(8,128)S(1)}, f32[2,112,128]{2,1,0:T(8,128)S(1)}) custom-call(f32[4,112,128]{2,1,0:T(8,128)S(1)} %copy-done.3, f32[4,112,128]{2,1,0:T(8,128)} %collective-permute-done.15.recv_ref), custom_call_target="tpu_custom_call" | custom-call | bytes 458752 | tf_op jit(solution)/shard_map/pallas_call | solution.py:423
  63.6 1.7 %collective-permute-start.16 = (f32[2,112,128]{2,1,0:T(8,128)S(1)}, f32[2,112,128]{2,1,0:T(8,128)S(1)}, u32[]{:S(2)}, u32[]{:S(2)}) collective-permute-start(f32[2,112,128]{2,1,0:T(8,128)S(1)} %get-tuple-element.34), channel_id=1, source_target_pairs={{0,8},{1,9},{2,10},{3,11},{4,12},{5,13},{6,14},{7,15},{8,0},{9,1},... | collective-permute-start | bytes 344072 | tf_op jit(solution)/shard_map/ppermute | solution.py:451
  65.3 1.2 %collective-permute-done.12.recv_ref = bf16[4,128,128]{2,1,0:T(8,128)(2,1)S(1)} collective-permute-done((bf16[4,128,128]{2,1,0:T(8,128)(2,1)S(1)}, bf16[4,128,128]{2,1,0:T(8,128)(2,1)S(1)}, u32[]{:S(2)}, u32[]{:S(2)}) %collective-permute-start.12) | collective-permute-done | bytes 131104 | tf_op jit(solution)/shard_map/ppermute | solution.py:451
  66.5 2.7 %collective-permute-start.13 = (bf16[4,128,128]{2,1,0:T(8,128)(2,1)S(1)}, bf16[4,128,128]{2,1,0:T(8,128)(2,1)S(1)}, u32[]{:S(2)}, u32[]{:S(2)}) collective-permute-start(bf16[4,128,128]{2,1,0:T(8,128)(2,1)S(1)} %shard_map.129.own_ref), channel_id=1, source_target_pairs={{0,2},{1,3},{2,0},{3,1},{4,6},{5,7},{6,4},{7,5},{8,10},{9,11},{10,... | collective-permute-start | bytes 393224 | tf_op jit(solution)/shard_map/ppermute | solution.py:451
  69.2 2.1 %collective-permute-start.17 = (f32[1,112,128]{2,1,0:T(8,128)S(1)}, f32[1,112,128]{2,1,0:T(8,128)S(1)}, u32[]{:S(2)}, u32[]{:S(2)}) collective-permute-start(f32[1,112,128]{2,1,0:T(8,128)S(1)} %get-tuple-element.36), channel_id=1, source_target_pairs={{0,16},{1,17},{2,18},{3,19},{4,20},{5,21},{6,22},{7,23},{8,24},{9,... | collective-permute-start | bytes 172040 | tf_op jit(solution)/shard_map/ppermute | solution.py:451
  71.2 3.6 %collective-permute-done.13.recv_ref = bf16[4,128,128]{2,1,0:T(8,128)(2,1)S(1)} collective-permute-done((bf16[4,128,128]{2,1,0:T(8,128)(2,1)S(1)}, bf16[4,128,128]{2,1,0:T(8,128)(2,1)S(1)}, u32[]{:S(2)}, u32[]{:S(2)}) %collective-permute-start.13) | collective-permute-done | bytes 131104 | tf_op jit(solution)/shard_map/ppermute | solution.py:451
  74.8 0.7 collective-permute-start.14
  75.6 1.4 %collective-permute-start.18 = (f32[1,112,128]{2,1,0:T(8,128)S(1)}, f32[1,112,128]{2,1,0:T(8,128)S(1)}, u32[]{:S(2)}, u32[]{:S(2)}) collective-permute-start(f32[1,112,128]{2,1,0:T(8,128)S(1)} %shard_map.139.own_ref), channel_id=1, source_target_pairs={{0,1},{1,0},{2,3},{3,2},{4,5},{5,4},{6,7},{7,6},{8,9},{9,8},{10,11... | collective-permute-start | bytes 172040 | tf_op jit(solution)/shard_map/ppermute | solution.py:451
  77.0 3.5 %collective-permute-done.18.recv_ref = f32[1,112,128]{2,1,0:T(8,128)S(1)} collective-permute-done((f32[1,112,128]{2,1,0:T(8,128)S(1)}, f32[1,112,128]{2,1,0:T(8,128)S(1)}, u32[]{:S(2)}, u32[]{:S(2)}) %collective-permute-start.18) | collective-permute-done | bytes 57376 | tf_op jit(solution)/shard_map/ppermute | solution.py:451
  80.5 3.1 %collective-permute-start.19 = (f32[1,112,128]{2,1,0:T(8,128)S(1)}, f32[1,112,128]{2,1,0:T(8,128)S(1)}, u32[]{:S(2)}, u32[]{:S(2)}) collective-permute-start(f32[1,112,128]{2,1,0:T(8,128)S(1)} %shard_map.140.lags_ref), channel_id=1, source_target_pairs={{0,2},{1,3},{2,0},{3,1},{4,6},{5,7},{6,4},{7,5},{8,10},{9,11},{10,... | collective-permute-start | bytes 172040 | tf_op jit(solution)/shard_map/ppermute | solution.py:451
  83.6 2.7 %shard_map.126 = bf16[6,32,1024]{2,1,0:T(8,128)(2,1)} custom-call(bf16[8,192,128]{2,1,0:T(8,128)(2,1)} %shard_map.125.hid_ref, bf16[1024,1024]{1,0:T(8,128)(2,1)S(1)} %copy-done), custom_call_target="tpu_custom_call" | custom-call | bytes 2490368 | tf_op jit(solution)/shard_map/pallas_call | solution.py:423
  86.4 0.9 shard_map.142
  (26 shorter events, 0.2 us)
Async XLA Ops:
  0.6 12.5 %collective-permute-start.5 = (bf16[192,1024]{1,0:T(8,128)(2,1)}, bf16[192,1024]{1,0:T(8,128)(2,1)}, u32[]{:S(2)}, u32[]{:S(2)}) collective-permute-start(bf16[192,1024]{1,0:T(8,128)(2,1)} %bitcast.5), channel_id=1, source_target_pairs={{0,8},{1,9},{2,10},{3,11},{4,12},{5,13},{6,14},{7,15},{8,0},{9,1},... | collective-permute-start | bytes 1179656 | tf_op jit(solution)/shard_map/ppermute | solution.py:451
  3.7 11.7 %collective-permute-start.6 = (bf16[192,1024]{1,0:T(8,128)(2,1)}, bf16[192,1024]{1,0:T(8,128)(2,1)}, u32[]{:S(2)}, u32[]{:S(2)}) collective-permute-start(bf16[192,1024]{1,0:T(8,128)(2,1)} %bitcast.6), channel_id=1, source_target_pairs={{0,16},{1,17},{2,18},{3,19},{4,20},{5,21},{6,22},{7,23},{8,24},{9,... | collective-permute-start | bytes 1179656 | tf_op jit(solution)/shard_map/ppermute | solution.py:451
  13.1 10.5 %collective-permute-start.10 = (bf16[192,1024]{1,0:T(8,128)(2,1)}, bf16[192,1024]{1,0:T(8,128)(2,1)S(1)}, u32[]{:S(2)}, u32[]{:S(2)}) collective-permute-start(bf16[192,1024]{1,0:T(8,128)(2,1)} %collective-permute-done.5.refs_1_), channel_id=1, source_target_pairs={{0,16},{1,17},{2,18},{3,19},{4,20},{5,21},{6,22},{7,23},{8,24},{9,... | collective-permute-start | bytes 1179656 | tf_op jit(solution)/shard_map/ppermute | solution.py:451
  14.9 42.3 %collective-permute-start.7 = (bf16[192,1024]{1,0:T(8,128)(2,1)}, bf16[192,1024]{1,0:T(8,128)(2,1)}, u32[]{:S(2)}, u32[]{:S(2)}) collective-permute-start(bf16[192,1024]{1,0:T(8,128)(2,1)} %bitcast.7), channel_id=1, source_target_pairs={{0,4},{1,5},{2,6},{3,7},{4,0},{5,1},{6,2},{7,3},{8,12},{9,13},{10,... | collective-permute-start | bytes 1179656 | tf_op jit(solution)/shard_map/ppermute | solution.py:451
  14.9 42.3 %collective-permute-start.8 = (bf16[192,1024]{1,0:T(8,128)(2,1)}, bf16[192,1024]{1,0:T(8,128)(2,1)}, u32[]{:S(2)}, u32[]{:S(2)}) collective-permute-start(bf16[192,1024]{1,0:T(8,128)(2,1)} %collective-permute-done.5.refs_1_), channel_id=1, source_target_pairs={{0,4},{1,5},{2,6},{3,7},{4,0},{5,1},{6,2},{7,3},{8,12},{9,13},{10,... | collective-permute-start | bytes 1179656 | tf_op jit(solution)/shard_map/ppermute | solution.py:451
  15.4 41.8 %collective-permute-start.9 = (bf16[192,1024]{1,0:T(8,128)(2,1)}, bf16[192,1024]{1,0:T(8,128)(2,1)}, u32[]{:S(2)}, u32[]{:S(2)}) collective-permute-start(bf16[192,1024]{1,0:T(8,128)(2,1)} %collective-permute-done.6.refs_2_), channel_id=1, source_target_pairs={{0,4},{1,5},{2,6},{3,7},{4,0},{5,1},{6,2},{7,3},{8,12},{9,13},{10,... | collective-permute-start | bytes 1179656 | tf_op jit(solution)/shard_map/ppermute | solution.py:451
  23.6 35.4 %collective-permute-start.11 = (bf16[192,1024]{1,0:T(8,128)(2,1)S(1)}, bf16[192,1024]{1,0:T(8,128)(2,1)}, u32[]{:S(2)}, u32[]{:S(2)}) collective-permute-start(bf16[192,1024]{1,0:T(8,128)(2,1)S(1)} %collective-permute-done.10.refs_0_), channel_id=1, source_target_pairs={{0,4},{1,5},{2,6},{3,7},{4,0},{5,1},{6,2},{7,3},{8,12},{9,13},{10,... | collective-permute-start | bytes 1179656 | tf_op jit(solution)/shard_map/ppermute | solution.py:451
  26.8 3.2 %collective-permute-start = (f32[2,1152]{1,0:T(2,128)S(1)}, f32[2,1152]{1,0:T(2,128)S(1)}, u32[]{:S(2)}, u32[]{:S(2)}) collective-permute-start(f32[2,1152]{1,0:T(2,128)S(1)} %get-tuple-element.23.own_ref), channel_id=1, source_target_pairs={{0,5},{1,4},{2,7},{3,6},{4,1},{5,0},{6,3},{7,2},{8,13},{9,12},{10,... | collective-permute-start | bytes 27656 | tf_op jit(solution)/shard_map/ppermute | solution.py:451
  29.9 4.0 %collective-permute-start.1 = (f32[2,1152]{1,0:T(2,128)S(1)}, f32[2,1152]{1,0:T(2,128)S(1)}, u32[]{:S(2)}, u32[]{:S(2)}) collective-permute-start(f32[2,1152]{1,0:T(2,128)S(1)} %shard_map.120.own_ref), channel_id=1, source_target_pairs={{0,6},{1,7},{2,4},{3,5},{4,2},{5,3},{6,0},{7,1},{8,14},{9,15},{10,... | collective-permute-start | bytes 27656 | tf_op jit(solution)/shard_map/ppermute | solution.py:451
  34.0 3.1 %collective-permute-start.2 = (f32[2,1152]{1,0:T(2,128)S(1)}, f32[2,1152]{1,0:T(2,128)S(1)}, u32[]{:S(2)}, u32[]{:S(2)}) collective-permute-start(f32[2,1152]{1,0:T(2,128)S(1)} %shard_map.121.own_ref), channel_id=1, source_target_pairs={{0,12},{1,13},{2,14},{3,15},{4,8},{5,9},{6,10},{7,11},{8,4},{9,5},... | collective-permute-start | bytes 27656 | tf_op jit(solution)/shard_map/ppermute | solution.py:451
  37.1 3.1 %collective-permute-start.3 = (f32[2,1152]{1,0:T(2,128)S(1)}, f32[2,1152]{1,0:T(2,128)S(1)}, u32[]{:S(2)}, u32[]{:S(2)}) collective-permute-start(f32[2,1152]{1,0:T(2,128)S(1)} %shard_map.122.own_ref), channel_id=1, source_target_pairs={{0,20},{1,21},{2,22},{3,23},{4,16},{5,17},{6,18},{7,19},{8,28},{9,... | collective-permute-start | bytes 27656 | tf_op jit(solution)/shard_map/ppermute | solution.py:451
  40.2 1.3 %collective-permute-start.4 = (f32[2,1152]{1,0:T(2,128)S(1)}, f32[2,1152]{1,0:T(2,128)S(1)}, u32[]{:S(2)}, u32[]{:S(2)}) collective-permute-start(f32[2,1152]{1,0:T(2,128)S(1)} %shard_map.123.own_ref), channel_id=1, source_target_pairs={{0,4},{1,5},{2,6},{3,7},{4,0},{5,1},{6,2},{7,3},{8,12},{9,13},{10,... | collective-permute-start | bytes 27656 | tf_op jit(solution)/shard_map/ppermute | solution.py:451
  42.6 16.3 %all-to-all-start = ((bf16[8,192,128]{2,1,0:T(8,128)(2,1)}), bf16[8,192,128]{2,1,0:T(8,128)(2,1)S(1)}, u32[]{:S(2)}, u32[]{:S(2)}) async-start(bf16[8,192,128]{2,1,0:T(8,128)(2,1)} %shard_map.125.hid_ref), calls=%async_computation | async-start | bytes 786432 | tf_op jit(solution)/shard_map/all_to_all | solution.py:528
  53.0 4.3 %copy-start.1 = (bf16[6,32,1024]{2,1,0:T(8,128)(2,1)S(1)}, bf16[6,32,1024]{2,1,0:T(8,128)(2,1)}, u32[]{:S(2)}) copy-start(bf16[6,32,1024]{2,1,0:T(8,128)(2,1)} %param.9) | copy-start | bytes 1179652
  56.0 0.7 copy-start.2
  56.7 5.9 %collective-permute-start.15 = (f32[4,112,128]{2,1,0:T(8,128)}, f32[4,112,128]{2,1,0:T(8,128)}, u32[]{:S(2)}, u32[]{:S(2)}) collective-permute-start(f32[4,112,128]{2,1,0:T(8,128)} %get-tuple-element.32), channel_id=1, source_target_pairs={{0,4},{1,5},{2,6},{3,7},{4,0},{5,1},{6,2},{7,3},{8,12},{9,13},{10,... | collective-permute-start | bytes 688136 | tf_op jit(solution)/shard_map/ppermute | solution.py:451
  59.0 3.7 %copy-start.3 = (f32[4,112,128]{2,1,0:T(8,128)S(1)}, f32[4,112,128]{2,1,0:T(8,128)}, u32[]{:S(2)}) copy-start(f32[4,112,128]{2,1,0:T(8,128)} %copy-done.2) | copy-start | bytes 688132
  59.0 24.7 %copy-start = (bf16[1024,1024]{1,0:T(8,128)(2,1)S(1)}, bf16[1024,1024]{1,0:T(8,128)(2,1)}, u32[]{:S(2)}) copy-start(bf16[1024,1024]{1,0:T(8,128)(2,1)} %w_hbm.1) | copy-start | bytes 6291460
  61.0 5.5 %collective-permute-start.12 = (bf16[4,128,128]{2,1,0:T(8,128)(2,1)S(1)}, bf16[4,128,128]{2,1,0:T(8,128)(2,1)S(1)}, u32[]{:S(2)}, u32[]{:S(2)}) collective-permute-start(bf16[4,128,128]{2,1,0:T(8,128)(2,1)S(1)} %get-tuple-element.28), channel_id=1, source_target_pairs={{0,1},{1,0},{2,3},{3,2},{4,5},{5,4},{6,7},{7,6},{8,9},{9,8},{10,11... | collective-permute-start | bytes 393224 | tf_op jit(solution)/shard_map/ppermute | solution.py:451
  63.6 5.6 %collective-permute-start.16 = (f32[2,112,128]{2,1,0:T(8,128)S(1)}, f32[2,112,128]{2,1,0:T(8,128)S(1)}, u32[]{:S(2)}, u32[]{:S(2)}) collective-permute-start(f32[2,112,128]{2,1,0:T(8,128)S(1)} %get-tuple-element.34), channel_id=1, source_target_pairs={{0,8},{1,9},{2,10},{3,11},{4,12},{5,13},{6,14},{7,15},{8,0},{9,1},... | collective-permute-start | bytes 344072 | tf_op jit(solution)/shard_map/ppermute | solution.py:451
  66.5 8.3 %collective-permute-start.13 = (bf16[4,128,128]{2,1,0:T(8,128)(2,1)S(1)}, bf16[4,128,128]{2,1,0:T(8,128)(2,1)S(1)}, u32[]{:S(2)}, u32[]{:S(2)}) collective-permute-start(bf16[4,128,128]{2,1,0:T(8,128)(2,1)S(1)} %shard_map.129.own_ref), channel_id=1, source_target_pairs={{0,2},{1,3},{2,0},{3,1},{4,6},{5,7},{6,4},{7,5},{8,10},{9,11},{10,... | collective-permute-start | bytes 393224 | tf_op jit(solution)/shard_map/ppermute | solution.py:451
  69.2 6.4 %collective-permute-start.17 = (f32[1,112,128]{2,1,0:T(8,128)S(1)}, f32[1,112,128]{2,1,0:T(8,128)S(1)}, u32[]{:S(2)}, u32[]{:S(2)}) collective-permute-start(f32[1,112,128]{2,1,0:T(8,128)S(1)} %get-tuple-element.36), channel_id=1, source_target_pairs={{0,16},{1,17},{2,18},{3,19},{4,20},{5,21},{6,22},{7,23},{8,24},{9,... | collective-permute-start | bytes 172040 | tf_op jit(solution)/shard_map/ppermute | solution.py:451
  74.8 11.5 %collective-permute-start.14 = (bf16[4,128,128]{2,1,0:T(8,128)(2,1)S(1)}, bf16[4,128,128]{2,1,0:T(8,128)(2,1)S(1)}, u32[]{:S(2)}, u32[]{:S(2)}) collective-permute-start(bf16[4,128,128]{2,1,0:T(8,128)(2,1)S(1)} %shard_map.130.own_ref), channel_id=1, source_target_pairs={{0,1},{1,0},{2,3},{3,2},{4,5},{5,4},{6,7},{7,6},{8,9},{9,8},{10,11... | collective-permute-start | bytes 393224 | tf_op jit(solution)/shard_map/ppermute | solution.py:451
  75.6 4.9 %collective-permute-start.18 = (f32[1,112,128]{2,1,0:T(8,128)S(1)}, f32[1,112,128]{2,1,0:T(8,128)S(1)}, u32[]{:S(2)}, u32[]{:S(2)}) collective-permute-start(f32[1,112,128]{2,1,0:T(8,128)S(1)} %shard_map.139.own_ref), channel_id=1, source_target_pairs={{0,1},{1,0},{2,3},{3,2},{4,5},{5,4},{6,7},{7,6},{8,9},{9,8},{10,11... | collective-permute-start | bytes 172040 | tf_op jit(solution)/shard_map/ppermute | solution.py:451
  80.5 5.8 %collective-permute-start.19 = (f32[1,112,128]{2,1,0:T(8,128)S(1)}, f32[1,112,128]{2,1,0:T(8,128)S(1)}, u32[]{:S(2)}, u32[]{:S(2)}) collective-permute-start(f32[1,112,128]{2,1,0:T(8,128)S(1)} %shard_map.140.lags_ref), channel_id=1, source_target_pairs={{0,2},{1,3},{2,0},{3,1},{4,6},{5,7},{6,4},{7,5},{8,10},{9,11},{10,... | collective-permute-start | bytes 172040 | tf_op jit(solution)/shard_map/ppermute | solution.py:451

commit v3 on v2

--- a/solution.py
+++ b/solution.py
@@ -228,14 +228,14 @@
     lax.fori_loop(0, many, one, 0)
 
 
-def back_body(cotan_hbm, w_hbm, out_ref, cotan_ref, w_ref, sems):
+def back_body(start, cotan_hbm, w_hbm, out_ref, cotan_ref, w_ref, sems):
     blocks = out_ref.shape[0]
     fetch = pltpu.make_async_copy(cotan_hbm, cotan_ref, sems.at[blocks])
     fetch.start()
     copies = []
     for block in range(blocks):
-        rows = pl.ds(block * LANES, LANES)
-        copies.append(pltpu.make_async_copy(w_hbm.at[rows], w_ref.at[rows], sems.at[block]))
+        rows, source = pl.ds(block * LANES, LANES), pl.ds((start + block) * LANES, LANES)
+        copies.append(pltpu.make_async_copy(w_hbm.at[source], w_ref.at[rows], sems.at[block]))
         copies[-1].start()
     fetch.wait()
     for block in range(blocks):
@@ -271,7 +271,7 @@
     lax.fori_loop(0, blocks, one, 0)
 
 
-def slope_body(st_ref, gb_ref, ok_ref, gp_ref, cv_ref, bk_ref, *refs):
+def slope_body(st_ref, gb_ref, ok_ref, gp_ref, cv_ref, low_ref, high_ref, *refs):
     aux_refs, (give_ref, keep_ref, sl_ref) = refs[:-3], refs[-3:]
     blocks, slots, frames, _ = cv_ref.shape
     taps = aux_refs[0].shape[2]
@@ -280,6 +280,7 @@
 
     def one(i, aux_ref, odd, q_ref):
         block = 2 * i + odd
+        bk_ref, at = (low_ref, block) if 4 * i < blocks else (high_ref, block - blocks // 2)
         _, mean, inv = scale_of(st_ref, block)
         gain, shift = gb_ref[0, pl.ds(block, 1), :], gb_ref[1, pl.ds(block, 1), :]
         first = second = jnp.zeros((8, LANES), F32)
@@ -287,7 +288,7 @@
             normed = (cv_ref[block, slot] - mean) * inv
             shifted = gain * normed + shift
             sig = jax.nn.sigmoid(shifted)
-            back = bk_ref[block, slot * frames : (slot + 1) * frames, :]
+            back = bk_ref[at, slot * frames : (slot + 1) * frames, :]
             slope = back * sig * (1.0 + shifted * (1.0 - sig)) * ok_ref[slot]
             sl_ref[slot] = slope
             first, second = first + fold(slope), second + fold(slope * normed)
@@ -343,14 +344,17 @@
         copy.wait()
 
 
-def rows_body(masks, recv_ref, staged_ref, *refs):
-    pieces, (give_ref, keep_ref, held, sems) = refs[:-4], refs[-4:]
+def rows_body(masks, recv_hbm, staged_ref, *refs):
+    pieces, (give_ref, keep_ref, recv_ref, held, sems) = refs[:-5], refs[-5:]
     me, half = lax.axis_index("dp"), lax.axis_index("grp") & 1
     copies = [
         pltpu.make_async_copy(piece, held.at[i], sems.at[i]) for i, piece in enumerate(pieces)
     ]
+    fetch = pltpu.make_async_copy(recv_hbm, recv_ref, sems.at[len(pieces)])
+    fetch.start()
     for copy in copies:
         copy.start()
+    fetch.wait()
     early = staged_ref.shape[0]
     many = give_ref.shape[0]
     width = many * LANES
@@ -491,23 +495,26 @@
         in_specs=[HBM] * 6,
     )
 
-    hops = [(1, m) for m in grp_bits] + [(m | 1, 0) for m in dp_bits[1:]] + [(1, 0)]
+    hops = [(1, m) for m in grp_bits] + [(m | 1, 0) for m in dp_bits[:0:-1]] + [(1, 0)]
     for dp_mask, grp_mask in hops:
         stats = plus(stats, swap(stats, dp_mask, grp_mask))
 
-    back = call(
-        back_body,
-        shape((blocks, tokens, LANES), F32),
-        (),
-        (in_hbm(flat_cotan), in_hbm(w_out)),
-        flops=2 * tokens * width * width,
-        scratch=[
-            pltpu.VMEM(flat_cotan.shape, BF16),
-            pltpu.VMEM(w_out.shape, BF16),
-            pltpu.SemaphoreType.DMA((blocks + 1,)),
-        ],
-        in_specs=[HBM] * 2,
-    )
+    back = [
+        call(
+            functools.partial(back_body, i * (blocks // 2)),
+            shape((blocks // 2, tokens, LANES), F32),
+            (),
+            (in_hbm(flat_cotan), in_hbm(w_out)),
+            flops=tokens * width * width,
+            scratch=[
+                pltpu.VMEM(flat_cotan.shape, BF16),
+                pltpu.VMEM((width // 2, width), BF16),
+                pltpu.SemaphoreType.DMA((blocks // 2 + 1,)),
+            ],
+            in_specs=[HBM] * 2,
+        )
+        for i in range(2)
+    ]
     parts = blocks // 2
     each = 2
     aux = [
@@ -530,7 +537,7 @@
         slope_body,
         [shape((parts, n_q, LANES), F32)] * 2,
         (),
-        (stats, gains, valid, gated, conv_out, back, *aux),
+        (stats, gains, valid, gated, conv_out, *back, *aux),
         flops=4 * taps * tokens * width,
         scratch=[pltpu.VMEM((slots, frames, LANES), F32)],
     )
@@ -562,10 +569,11 @@
         (received, staged, *values[early:]),
         flops=2 * n_dp * tokens * LANES * width,
         scratch=[
+            pltpu.VMEM(received.shape, BF16),
             pltpu.VMEM((n_dp - early, tokens, width), BF16),
-            pltpu.SemaphoreType.DMA((n_dp - early,)),
+            pltpu.SemaphoreType.DMA((n_dp - early + 1,)),
         ],
-        in_specs=[VMEM, VMEM] + [ANY] * (n_dp - early),
+        in_specs=[ANY, VMEM] + [ANY] * (n_dp - early),
     )
     taken = swap(given, 0, 1)
     both = call(add_body, half_shape, (), (kept, taken))

time: 87.6 us -> 91.5 us (1.045)
  local copies, waits for them, and re-layouts: 0.71 us -> 3.91 us
    unnamed x8 -> x12, local copies, waits for them, and re-layouts: 0.71 us -> 3.91 us
    ppermute x20, waiting for transfers between devices: 31.2 us -> 32.1 us  [swap(): return lax.ppermute(value, ('dp', 'grp'), pairs)]
    pallas_call x24 -> x25, Pallas kernels: 22.3 us -> 22.1 us  [call(): pl.pallas_call(body, in_specs=more.pop('in_specs', None) or [SMEM] * len(...]
  transfers between devices with their start and end apart: 21 -> 21, of which waited for: 10 -> 10; matrix products, arithmetic and copies ran while one was open for 0% -> 0% of each run, Pallas kernels for 25% -> 23%
where the time goes in v3:
time: 91.5 us; the launch traced here: 91.2 us
  starting transfers between devices  32.2 us (35%)
  waiting for transfers between devices  32.1 us (35%)
  Pallas kernels  22.1 us (24%)
  local copies, waits for them, and re-layouts  3.91 us (4%)
    ppermute x20, waiting for transfers between devices, swap(): return lax.ppermute(value, ('dp', 'grp'), pairs)  32.1 us
    ppermute x20, starting transfers between devices, swap(): return lax.ppermute(value, ('dp', 'grp'), pairs)  28.5 us
    pallas_call x25, Pallas kernels, call(): pl.pallas_call(body, in_specs=more.pop('in_specs', None) or [SMEM] * len(...  22.1 us
    unnamed x12, local copies, waits for them, and re-layouts  3.91 us
    all_to_all x1, starting transfers between devices, local_fast(): received = lax.all_to_all(hidden, 'dp', 0, 0, tiled=True)  3.69 us
  transfers between devices with their start and end apart: 21, of which 10 were waited for; matrix products, arithmetic and copies ran while one was open for 0% of the time, Pallas kernels for 23%

profile of v3, /device:TPU:0, one launch (start us, length us, event | category | flops | bytes accessed | tf_op | source)
XLA Modules:
  0.0 91.2 jit_solution(1954221672986221515)
XLA Ops:
  0.6 3.0 %collective-permute-start.5 = (bf16[192,1024]{1,0:T(8,128)(2,1)}, bf16[192,1024]{1,0:T(8,128)(2,1)}, u32[]{:S(2)}, u32[]{:S(2)}) collective-permute-start(bf16[192,1024]{1,0:T(8,128)(2,1)} %bitcast.5), channel_id=1, source_target_pairs={{0,8},{1,9},{2,10},{3,11},{4,12},{5,13},{6,14},{7,15},{8,0},{9,1},... | collective-permute-start | bytes 1179656 | tf_op jit(solution)/shard_map/ppermute | solution.py:455
  3.7 1.5 %collective-permute-start.6 = (bf16[192,1024]{1,0:T(8,128)(2,1)}, bf16[192,1024]{1,0:T(8,128)(2,1)}, u32[]{:S(2)}, u32[]{:S(2)}) collective-permute-start(bf16[192,1024]{1,0:T(8,128)(2,1)} %bitcast.6), channel_id=1, source_target_pairs={{0,16},{1,17},{2,18},{3,19},{4,20},{5,21},{6,22},{7,23},{8,24},{9,... | collective-permute-start | bytes 1179656 | tf_op jit(solution)/shard_map/ppermute | solution.py:455
  5.2 7.9 %collective-permute-done.5.refs_1_ = bf16[192,1024]{1,0:T(8,128)(2,1)} collective-permute-done((bf16[192,1024]{1,0:T(8,128)(2,1)}, bf16[192,1024]{1,0:T(8,128)(2,1)}, u32[]{:S(2)}, u32[]{:S(2)}) %collective-permute-start.5) | collective-permute-done | bytes 393248 | tf_op jit(solution)/shard_map/ppermute | solution.py:455
  13.1 1.8 %collective-permute-start.10 = (bf16[192,1024]{1,0:T(8,128)(2,1)}, bf16[192,1024]{1,0:T(8,128)(2,1)S(1)}, u32[]{:S(2)}, u32[]{:S(2)}) collective-permute-start(bf16[192,1024]{1,0:T(8,128)(2,1)} %collective-permute-done.5.refs_1_), channel_id=1, source_target_pairs={{0,16},{1,17},{2,18},{3,19},{4,20},{5,21},{6,22},{7,23},{8,24},{9,... | collective-permute-start | bytes 1179656 | tf_op jit(solution)/shard_map/ppermute | solution.py:455
  14.9 0.0 collective-permute-start.7
  14.9 0.5 collective-permute-start.8
  15.4 0.0 collective-permute-start.9
  15.4 8.2 %collective-permute-done.10.refs_0_ = bf16[192,1024]{1,0:T(8,128)(2,1)S(1)} collective-permute-done((bf16[192,1024]{1,0:T(8,128)(2,1)}, bf16[192,1024]{1,0:T(8,128)(2,1)S(1)}, u32[]{:S(2)}, u32[]{:S(2)}) %collective-permute-start.10) | collective-permute-done | bytes 393248 | tf_op jit(solution)/shard_map/ppermute | solution.py:455
  23.6 3.2 %shard_map.119 = (f32[8,6,64,128]{3,2,1,0:T(8,128)S(1)}, f32[8,6,32,128]{3,2,1,0:T(8,128)S(1)}, f32[2,1152]{1,0:T(2,128)S(1)}, f32[6,32,128]{2,1,0:T(8,128)S(1)}...) custom-call(s32[6]{0:T(128)} %len_hbm.1, s32[6]{0:T(128)} %off_hbm.1, bf16[6,32,2048]{2,1,0:T(8,128)(2,1)} %acts_hbm.1, ...), custom_call_target="tpu_custom_call" | custom-call | flops 25165824 | bytes 925744 | tf_op jit(solution)/shard_map/pallas_call | solution.py:427
  26.8 1.7 %collective-permute-start = (f32[2,1152]{1,0:T(2,128)S(1)}, f32[2,1152]{1,0:T(2,128)S(1)}, u32[]{:S(2)}, u32[]{:S(2)}) collective-permute-start(f32[2,1152]{1,0:T(2,128)S(1)} %get-tuple-element.23.own_ref), channel_id=1, source_target_pairs={{0,5},{1,4},{2,7},{3,6},{4,1},{5,0},{6,3},{7,2},{8,13},{9,12},{10,... | collective-permute-start | bytes 27656 | tf_op jit(solution)/shard_map/ppermute | solution.py:455
  28.5 1.4 %collective-permute-done.recv_ref = f32[2,1152]{1,0:T(2,128)S(1)} collective-permute-done((f32[2,1152]{1,0:T(2,128)S(1)}, f32[2,1152]{1,0:T(2,128)S(1)}, u32[]{:S(2)}, u32[]{:S(2)}) %collective-permute-start) | collective-permute-done | bytes 9248 | tf_op jit(solution)/shard_map/ppermute | solution.py:455
  29.9 2.7 %collective-permute-start.1 = (f32[2,1152]{1,0:T(2,128)S(1)}, f32[2,1152]{1,0:T(2,128)S(1)}, u32[]{:S(2)}, u32[]{:S(2)}) collective-permute-start(f32[2,1152]{1,0:T(2,128)S(1)} %shard_map.120.own_ref), channel_id=1, source_target_pairs={{0,6},{1,7},{2,4},{3,5},{4,2},{5,3},{6,0},{7,1},{8,14},{9,15},{10,... | collective-permute-start | bytes 27656 | tf_op jit(solution)/shard_map/ppermute | solution.py:455
  32.6 1.4 %collective-permute-done.1.recv_ref = f32[2,1152]{1,0:T(2,128)S(1)} collective-permute-done((f32[2,1152]{1,0:T(2,128)S(1)}, f32[2,1152]{1,0:T(2,128)S(1)}, u32[]{:S(2)}, u32[]{:S(2)}) %collective-permute-start.1) | collective-permute-done | bytes 9248 | tf_op jit(solution)/shard_map/ppermute | solution.py:455
  34.0 1.5 %collective-permute-start.2 = (f32[2,1152]{1,0:T(2,128)S(1)}, f32[2,1152]{1,0:T(2,128)S(1)}, u32[]{:S(2)}, u32[]{:S(2)}) collective-permute-start(f32[2,1152]{1,0:T(2,128)S(1)} %shard_map.121.own_ref), channel_id=1, source_target_pairs={{0,20},{1,21},{2,22},{3,23},{4,16},{5,17},{6,18},{7,19},{8,28},{9,... | collective-permute-start | bytes 27656 | tf_op jit(solution)/shard_map/ppermute | solution.py:455
  35.5 1.5 %collective-permute-done.2.recv_ref = f32[2,1152]{1,0:T(2,128)S(1)} collective-permute-done((f32[2,1152]{1,0:T(2,128)S(1)}, f32[2,1152]{1,0:T(2,128)S(1)}, u32[]{:S(2)}, u32[]{:S(2)}) %collective-permute-start.2) | collective-permute-done | bytes 9248 | tf_op jit(solution)/shard_map/ppermute | solution.py:455
  37.1 1.5 %collective-permute-start.3 = (f32[2,1152]{1,0:T(2,128)S(1)}, f32[2,1152]{1,0:T(2,128)S(1)}, u32[]{:S(2)}, u32[]{:S(2)}) collective-permute-start(f32[2,1152]{1,0:T(2,128)S(1)} %shard_map.122.own_ref), channel_id=1, source_target_pairs={{0,12},{1,13},{2,14},{3,15},{4,8},{5,9},{6,10},{7,11},{8,4},{9,5},... | collective-permute-start | bytes 27656 | tf_op jit(solution)/shard_map/ppermute | solution.py:455
  38.6 1.6 %collective-permute-done.3.recv_ref = f32[2,1152]{1,0:T(2,128)S(1)} collective-permute-done((f32[2,1152]{1,0:T(2,128)S(1)}, f32[2,1152]{1,0:T(2,128)S(1)}, u32[]{:S(2)}, u32[]{:S(2)}) %collective-permute-start.3) | collective-permute-done | bytes 9248 | tf_op jit(solution)/shard_map/ppermute | solution.py:455
  40.2 0.5 collective-permute-start.4
  40.6 0.8 collective-permute-done.4.recv_ref
  41.4 1.2 %shard_map.125.hid_ref = bf16[8,192,128]{2,1,0:T(8,128)(2,1)} custom-call(f32[2,1152]{1,0:T(2,128)S(1)} %shard_map.124.st_ref, f32[2,8,128]{2,1,0:T(8,128)S(1)} %get-tuple-element.24.gb_ref, f32[6,32,128]{2,1,0:T(8,128)S(1)} %get-tuple-element.25.ok_ref, f32[8,6,32,128]{3,2,1,0:T(8,128)S(1)} %get-tuple-element.26.cv_ref), custom_call_target="tpu_custom_call" | custom-call | bytes 902144 | tf_op jit(solution)/shard_map/pallas_call | solution.py:427
  42.6 3.7 %all-to-all-start = ((bf16[8,192,128]{2,1,0:T(8,128)(2,1)}), bf16[8,192,128]{2,1,0:T(8,128)(2,1)S(1)}, u32[]{:S(2)}, u32[]{:S(2)}) async-start(bf16[8,192,128]{2,1,0:T(8,128)(2,1)} %shard_map.125.hid_ref), calls=%async_computation | async-start | bytes 786432 | tf_op jit(solution)/shard_map/all_to_all | solution.py:535
  46.3 0.7 shard_map.133.refs_0_
  47.0 0.7 shard_map.134.refs_1_
  47.6 0.7 shard_map.135.refs_2_
  48.3 0.7 shard_map.136.refs_3_
  49.0 2.5 %shard_map.131.low_ref = f32[4,192,128]{2,1,0:T(8,128)S(1)} custom-call(bf16[192,1024]{1,0:T(8,128)(2,1)} %bitcast.8, bf16[1024,1024]{1,0:T(8,128)(2,1)} %w_hbm.3), custom_call_target="tpu_custom_call" | custom-call | flops 201326592 | bytes 2490368 | tf_op jit(solution)/shard_map/pallas_call | solution.py:427
  51.5 2.5 %shard_map.132.high_ref = f32[4,192,128]{2,1,0:T(8,128)S(1)} custom-call(bf16[192,1024]{1,0:T(8,128)(2,1)} %bitcast.9, bf16[1024,1024]{1,0:T(8,128)(2,1)} %w_hbm.3), custom_call_target="tpu_custom_call" | custom-call | flops 201326592 | bytes 2490368 | tf_op jit(solution)/shard_map/pallas_call | solution.py:427
  54.0 0.0 copy-start.3
  54.1 3.0 %shard_map.137 = (f32[4,112,128]{2,1,0:T(8,128)}, f32[4,112,128]{2,1,0:T(8,128)S(1)}) custom-call(f32[2,1152]{1,0:T(2,128)S(1)} %shard_map.124.st_ref, f32[2,8,128]{2,1,0:T(8,128)S(1)} %get-tuple-element.24.gb_ref, f32[6,32,128]{2,1,0:T(8,128)S(1)} %get-tuple-element.25.ok_ref, f32[8,6,64,128]{3,2,1,0:T(8,128)S(1)} %get-tuple-element.29.gp_ref, ...), custom_call_target="tpu_custom_call" | custom-call | flops 25165824 | bytes 3523584 | tf_op jit(solution)/shard_map/pallas_call | solution.py:427
  57.1 0.7 copy-done.4
  57.8 0.5 collective-permute-start.15
  58.3 0.0 collective-permute-done.9.refs_5_
  58.3 1.7 %shard_map.127.staged_ref = bf16[6,192,1024]{2,1,0:T(8,128)(2,1)S(1)} custom-call(bf16[192,1024]{1,0:T(8,128)(2,1)S(1)} %bitcast.10, bf16[192,1024]{1,0:T(8,128)(2,1)} %collective-permute-done.5.refs_1_, bf16[192,1024]{1,0:T(8,128)(2,1)} %collective-permute-done.6.refs_2_, bf16[192,1024]{1,0:T(8,128)(2,1)} %collective-permute-done.7.refs_3_, ...), custom_call_target="tpu_custom_call" | custom-call | bytes 2359296 | tf_op jit(solution)/shard_map/pallas_call | solution.py:427
  60.0 1.4 %copy-done.1 = bf16[6,192,1024]{2,1,0:T(8,128)(2,1)} copy-done((bf16[6,192,1024]{2,1,0:T(8,128)(2,1)}, bf16[6,192,1024]{2,1,0:T(8,128)(2,1)S(1)}, u32[]{:S(2)}) %copy-start.1) | copy-done | bytes 2359320
  61.5 1.8 %copy-done.2 = bf16[6,192,1024]{2,1,0:T(8,128)(2,1)S(1)} copy-done((bf16[6,192,1024]{2,1,0:T(8,128)(2,1)S(1)}, bf16[6,192,1024]{2,1,0:T(8,128)(2,1)}, u32[]{:S(2)}) %copy-start.2) | copy-done | bytes 2359320
  63.3 1.6 %shard_map.128 = (bf16[4,128,128]{2,1,0:T(8,128)(2,1)S(1)}, bf16[4,128,128]{2,1,0:T(8,128)(2,1)S(1)}) custom-call(bf16[8,192,128]{2,1,0:T(8,128)(2,1)S(1)} %all-to-all-done.recv_hbm, bf16[6,192,1024]{2,1,0:T(8,128)(2,1)S(1)} %copy-done.2, bf16[192,1024]{1,0:T(8,128)(2,1)S(1)} %collective-permute-done.10.refs_0_, ...), custom_call_target="tpu_custom_call" | custom-call | flops 402653184 | bytes 3538944 | tf_op jit(solution)/shard_map/pallas_call | solution.py:427
  64.9 1.6 %collective-permute-start.12 = (bf16[4,128,128]{2,1,0:T(8,128)(2,1)S(1)}, bf16[4,128,128]{2,1,0:T(8,128)(2,1)S(1)}, u32[]{:S(2)}, u32[]{:S(2)}) collective-permute-start(bf16[4,128,128]{2,1,0:T(8,128)(2,1)S(1)} %get-tuple-element.28), channel_id=1, source_target_pairs={{0,1},{1,0},{2,3},{3,2},{4,5},{5,4},{6,7},{7,6},{8,9},{9,8},{10,11... | collective-permute-start | bytes 393224 | tf_op jit(solution)/shard_map/ppermute | solution.py:455
  66.6 1.7 %collective-permute-start.16 = (f32[2,112,128]{2,1,0:T(8,128)S(1)}, f32[2,112,128]{2,1,0:T(8,128)S(1)}, u32[]{:S(2)}, u32[]{:S(2)}) collective-permute-start(f32[2,112,128]{2,1,0:T(8,128)S(1)} %get-tuple-element.34), channel_id=1, source_target_pairs={{0,8},{1,9},{2,10},{3,11},{4,12},{5,13},{6,14},{7,15},{8,0},{9,1},... | collective-permute-start | bytes 344072 | tf_op jit(solution)/shard_map/ppermute | solution.py:455
  68.3 2.1 %collective-permute-done.12.recv_ref = bf16[4,128,128]{2,1,0:T(8,128)(2,1)S(1)} collective-permute-done((bf16[4,128,128]{2,1,0:T(8,128)(2,1)S(1)}, bf16[4,128,128]{2,1,0:T(8,128)(2,1)S(1)}, u32[]{:S(2)}, u32[]{:S(2)}) %collective-permute-start.12) | collective-permute-done | bytes 131104 | tf_op jit(solution)/shard_map/ppermute | solution.py:455
  70.4 2.7 %collective-permute-start.13 = (bf16[4,128,128]{2,1,0:T(8,128)(2,1)S(1)}, bf16[4,128,128]{2,1,0:T(8,128)(2,1)S(1)}, u32[]{:S(2)}, u32[]{:S(2)}) collective-permute-start(bf16[4,128,128]{2,1,0:T(8,128)(2,1)S(1)} %shard_map.129.own_ref), channel_id=1, source_target_pairs={{0,2},{1,3},{2,0},{3,1},{4,6},{5,7},{6,4},{7,5},{8,10},{9,11},{10,... | collective-permute-start | bytes 393224 | tf_op jit(solution)/shard_map/ppermute | solution.py:455
  73.1 2.1 %collective-permute-start.17 = (f32[1,112,128]{2,1,0:T(8,128)S(1)}, f32[1,112,128]{2,1,0:T(8,128)S(1)}, u32[]{:S(2)}, u32[]{:S(2)}) collective-permute-start(f32[1,112,128]{2,1,0:T(8,128)S(1)} %get-tuple-element.36), channel_id=1, source_target_pairs={{0,16},{1,17},{2,18},{3,19},{4,20},{5,21},{6,22},{7,23},{8,24},{9,... | collective-permute-start | bytes 172040 | tf_op jit(solution)/shard_map/ppermute | solution.py:455
  75.2 3.6 %collective-permute-done.13.recv_ref = bf16[4,128,128]{2,1,0:T(8,128)(2,1)S(1)} collective-permute-done((bf16[4,128,128]{2,1,0:T(8,128)(2,1)S(1)}, bf16[4,128,128]{2,1,0:T(8,128)(2,1)S(1)}, u32[]{:S(2)}, u32[]{:S(2)}) %collective-permute-start.13) | collective-permute-done | bytes 131104 | tf_op jit(solution)/shard_map/ppermute | solution.py:455
  78.8 0.7 collective-permute-start.14
  79.5 1.4 %collective-permute-start.18 = (f32[1,112,128]{2,1,0:T(8,128)S(1)}, f32[1,112,128]{2,1,0:T(8,128)S(1)}, u32[]{:S(2)}, u32[]{:S(2)}) collective-permute-start(f32[1,112,128]{2,1,0:T(8,128)S(1)} %shard_map.140.own_ref), channel_id=1, source_target_pairs={{0,1},{1,0},{2,3},{3,2},{4,5},{5,4},{6,7},{7,6},{8,9},{9,8},{10,11... | collective-permute-start | bytes 172040 | tf_op jit(solution)/shard_map/ppermute | solution.py:455
  81.0 3.5 %collective-permute-done.18.recv_ref = f32[1,112,128]{2,1,0:T(8,128)S(1)} collective-permute-done((f32[1,112,128]{2,1,0:T(8,128)S(1)}, f32[1,112,128]{2,1,0:T(8,128)S(1)}, u32[]{:S(2)}, u32[]{:S(2)}) %collective-permute-start.18) | collective-permute-done | bytes 57376 | tf_op jit(solution)/shard_map/ppermute | solution.py:455
  84.5 3.1 %collective-permute-start.19 = (f32[1,112,128]{2,1,0:T(8,128)S(1)}, f32[1,112,128]{2,1,0:T(8,128)S(1)}, u32[]{:S(2)}, u32[]{:S(2)}) collective-permute-start(f32[1,112,128]{2,1,0:T(8,128)S(1)} %shard_map.141.lags_ref), channel_id=1, source_target_pairs={{0,2},{1,3},{2,0},{3,1},{4,6},{5,7},{6,4},{7,5},{8,10},{9,11},{10,... | collective-permute-start | bytes 172040 | tf_op jit(solution)/shard_map/ppermute | solution.py:455
  87.6 2.7 %shard_map.126 = bf16[6,32,1024]{2,1,0:T(8,128)(2,1)} custom-call(bf16[8,192,128]{2,1,0:T(8,128)(2,1)} %shard_map.125.hid_ref, bf16[1024,1024]{1,0:T(8,128)(2,1)S(1)} %copy-done), custom_call_target="tpu_custom_call" | custom-call | bytes 2490368 | tf_op jit(solution)/shard_map/pallas_call | solution.py:427
  90.3 0.9 shard_map.143
  (31 shorter events, 0.2 us)
Async XLA Ops:
  0.6 12.5 %collective-permute-start.5 = (bf16[192,1024]{1,0:T(8,128)(2,1)}, bf16[192,1024]{1,0:T(8,128)(2,1)}, u32[]{:S(2)}, u32[]{:S(2)}) collective-permute-start(bf16[192,1024]{1,0:T(8,128)(2,1)} %bitcast.5), channel_id=1, source_target_pairs={{0,8},{1,9},{2,10},{3,11},{4,12},{5,13},{6,14},{7,15},{8,0},{9,1},... | collective-permute-start | bytes 1179656 | tf_op jit(solution)/shard_map/ppermute | solution.py:455
  3.7 11.7 %collective-permute-start.6 = (bf16[192,1024]{1,0:T(8,128)(2,1)}, bf16[192,1024]{1,0:T(8,128)(2,1)}, u32[]{:S(2)}, u32[]{:S(2)}) collective-permute-start(bf16[192,1024]{1,0:T(8,128)(2,1)} %bitcast.6), channel_id=1, source_target_pairs={{0,16},{1,17},{2,18},{3,19},{4,20},{5,21},{6,22},{7,23},{8,24},{9,... | collective-permute-start | bytes 1179656 | tf_op jit(solution)/shard_map/ppermute | solution.py:455
  13.1 10.5 %collective-permute-start.10 = (bf16[192,1024]{1,0:T(8,128)(2,1)}, bf16[192,1024]{1,0:T(8,128)(2,1)S(1)}, u32[]{:S(2)}, u32[]{:S(2)}) collective-permute-start(bf16[192,1024]{1,0:T(8,128)(2,1)} %collective-permute-done.5.refs_1_), channel_id=1, source_target_pairs={{0,16},{1,17},{2,18},{3,19},{4,20},{5,21},{6,22},{7,23},{8,24},{9,... | collective-permute-start | bytes 1179656 | tf_op jit(solution)/shard_map/ppermute | solution.py:455
  14.9 43.4 %collective-permute-start.7 = (bf16[192,1024]{1,0:T(8,128)(2,1)}, bf16[192,1024]{1,0:T(8,128)(2,1)}, u32[]{:S(2)}, u32[]{:S(2)}) collective-permute-start(bf16[192,1024]{1,0:T(8,128)(2,1)} %bitcast.7), channel_id=1, source_target_pairs={{0,4},{1,5},{2,6},{3,7},{4,0},{5,1},{6,2},{7,3},{8,12},{9,13},{10,... | collective-permute-start | bytes 1179656 | tf_op jit(solution)/shard_map/ppermute | solution.py:455
  14.9 43.4 %collective-permute-start.8 = (bf16[192,1024]{1,0:T(8,128)(2,1)}, bf16[192,1024]{1,0:T(8,128)(2,1)}, u32[]{:S(2)}, u32[]{:S(2)}) collective-permute-start(bf16[192,1024]{1,0:T(8,128)(2,1)} %collective-permute-done.5.refs_1_), channel_id=1, source_target_pairs={{0,4},{1,5},{2,6},{3,7},{4,0},{5,1},{6,2},{7,3},{8,12},{9,13},{10,... | collective-permute-start | bytes 1179656 | tf_op jit(solution)/shard_map/ppermute | solution.py:455
  15.4 42.9 %collective-permute-start.9 = (bf16[192,1024]{1,0:T(8,128)(2,1)}, bf16[192,1024]{1,0:T(8,128)(2,1)}, u32[]{:S(2)}, u32[]{:S(2)}) collective-permute-start(bf16[192,1024]{1,0:T(8,128)(2,1)} %collective-permute-done.6.refs_2_), channel_id=1, source_target_pairs={{0,4},{1,5},{2,6},{3,7},{4,0},{5,1},{6,2},{7,3},{8,12},{9,13},{10,... | collective-permute-start | bytes 1179656 | tf_op jit(solution)/shard_map/ppermute | solution.py:455
  23.6 37.9 %collective-permute-start.11 = (bf16[192,1024]{1,0:T(8,128)(2,1)S(1)}, bf16[192,1024]{1,0:T(8,128)(2,1)}, u32[]{:S(2)}, u32[]{:S(2)}) collective-permute-start(bf16[192,1024]{1,0:T(8,128)(2,1)S(1)} %collective-permute-done.10.refs_0_), channel_id=1, source_target_pairs={{0,4},{1,5},{2,6},{3,7},{4,0},{5,1},{6,2},{7,3},{8,12},{9,13},{10,... | collective-permute-start | bytes 1179656 | tf_op jit(solution)/shard_map/ppermute | solution.py:455
  26.8 3.2 %collective-permute-start = (f32[2,1152]{1,0:T(2,128)S(1)}, f32[2,1152]{1,0:T(2,128)S(1)}, u32[]{:S(2)}, u32[]{:S(2)}) collective-permute-start(f32[2,1152]{1,0:T(2,128)S(1)} %get-tuple-element.23.own_ref), channel_id=1, source_target_pairs={{0,5},{1,4},{2,7},{3,6},{4,1},{5,0},{6,3},{7,2},{8,13},{9,12},{10,... | collective-permute-start | bytes 27656 | tf_op jit(solution)/shard_map/ppermute | solution.py:455
  29.9 4.0 %collective-permute-start.1 = (f32[2,1152]{1,0:T(2,128)S(1)}, f32[2,1152]{1,0:T(2,128)S(1)}, u32[]{:S(2)}, u32[]{:S(2)}) collective-permute-start(f32[2,1152]{1,0:T(2,128)S(1)} %shard_map.120.own_ref), channel_id=1, source_target_pairs={{0,6},{1,7},{2,4},{3,5},{4,2},{5,3},{6,0},{7,1},{8,14},{9,15},{10,... | collective-permute-start | bytes 27656 | tf_op jit(solution)/shard_map/ppermute | solution.py:455
  34.0 3.1 %collective-permute-start.2 = (f32[2,1152]{1,0:T(2,128)S(1)}, f32[2,1152]{1,0:T(2,128)S(1)}, u32[]{:S(2)}, u32[]{:S(2)}) collective-permute-start(f32[2,1152]{1,0:T(2,128)S(1)} %shard_map.121.own_ref), channel_id=1, source_target_pairs={{0,20},{1,21},{2,22},{3,23},{4,16},{5,17},{6,18},{7,19},{8,28},{9,... | collective-permute-start | bytes 27656 | tf_op jit(solution)/shard_map/ppermute | solution.py:455
  37.1 3.1 %collective-permute-start.3 = (f32[2,1152]{1,0:T(2,128)S(1)}, f32[2,1152]{1,0:T(2,128)S(1)}, u32[]{:S(2)}, u32[]{:S(2)}) collective-permute-start(f32[2,1152]{1,0:T(2,128)S(1)} %shard_map.122.own_ref), channel_id=1, source_target_pairs={{0,12},{1,13},{2,14},{3,15},{4,8},{5,9},{6,10},{7,11},{8,4},{9,5},... | collective-permute-start | bytes 27656 | tf_op jit(solution)/shard_map/ppermute | solution.py:455
  40.2 1.3 %collective-permute-start.4 = (f32[2,1152]{1,0:T(2,128)S(1)}, f32[2,1152]{1,0:T(2,128)S(1)}, u32[]{:S(2)}, u32[]{:S(2)}) collective-permute-start(f32[2,1152]{1,0:T(2,128)S(1)} %shard_map.123.own_ref), channel_id=1, source_target_pairs={{0,4},{1,5},{2,6},{3,7},{4,0},{5,1},{6,2},{7,3},{8,12},{9,13},{10,... | collective-permute-start | bytes 27656 | tf_op jit(solution)/shard_map/ppermute | solution.py:455
  42.6 18.8 %all-to-all-start = ((bf16[8,192,128]{2,1,0:T(8,128)(2,1)}), bf16[8,192,128]{2,1,0:T(8,128)(2,1)S(1)}, u32[]{:S(2)}, u32[]{:S(2)}) async-start(bf16[8,192,128]{2,1,0:T(8,128)(2,1)} %shard_map.125.hid_ref), calls=%async_computation | async-start | bytes 786432 | tf_op jit(solution)/shard_map/all_to_all | solution.py:535
  54.0 4.2 %copy-start.3 = (bf16[6,32,1024]{2,1,0:T(8,128)(2,1)S(1)}, bf16[6,32,1024]{2,1,0:T(8,128)(2,1)}, u32[]{:S(2)}) copy-start(bf16[6,32,1024]{2,1,0:T(8,128)(2,1)} %param.9) | copy-start | bytes 1179652
  57.1 0.7 copy-start.4
  57.8 8.8 %collective-permute-start.15 = (f32[4,112,128]{2,1,0:T(8,128)}, f32[4,112,128]{2,1,0:T(8,128)S(1)}, u32[]{:S(2)}, u32[]{:S(2)}) collective-permute-start(f32[4,112,128]{2,1,0:T(8,128)} %get-tuple-element.32), channel_id=1, source_target_pairs={{0,4},{1,5},{2,6},{3,7},{4,0},{5,1},{6,2},{7,3},{8,12},{9,13},{10,... | collective-permute-start | bytes 688136 | tf_op jit(solution)/shard_map/ppermute | solution.py:455
  58.3 8.3 %copy-start.5 = (f32[4,112,128]{2,1,0:T(8,128)S(1)}, f32[4,112,128]{2,1,0:T(8,128)}, u32[]{:S(2)}) copy-start(f32[4,112,128]{2,1,0:T(8,128)} %copy-done.4) | copy-start | bytes 688132
  60.0 1.4 %copy-start.1 = (bf16[6,192,1024]{2,1,0:T(8,128)(2,1)}, bf16[6,192,1024]{2,1,0:T(8,128)(2,1)S(1)}, u32[]{:S(2)}) copy-start(bf16[6,192,1024]{2,1,0:T(8,128)(2,1)S(1)} %shard_map.127.staged_ref) | copy-start | bytes 7077892
  61.4 26.1 %copy-start = (bf16[1024,1024]{1,0:T(8,128)(2,1)S(1)}, bf16[1024,1024]{1,0:T(8,128)(2,1)}, u32[]{:S(2)}) copy-start(bf16[1024,1024]{1,0:T(8,128)(2,1)} %w_hbm.3) | copy-start | bytes 6291460
  61.4 1.8 %copy-start.2 = (bf16[6,192,1024]{2,1,0:T(8,128)(2,1)S(1)}, bf16[6,192,1024]{2,1,0:T(8,128)(2,1)}, u32[]{:S(2)}) copy-start(bf16[6,192,1024]{2,1,0:T(8,128)(2,1)} %copy-done.1) | copy-start | bytes 7077892
  64.9 5.5 %collective-permute-start.12 = (bf16[4,128,128]{2,1,0:T(8,128)(2,1)S(1)}, bf16[4,128,128]{2,1,0:T(8,128)(2,1)S(1)}, u32[]{:S(2)}, u32[]{:S(2)}) collective-permute-start(bf16[4,128,128]{2,1,0:T(8,128)(2,1)S(1)} %get-tuple-element.28), channel_id=1, source_target_pairs={{0,1},{1,0},{2,3},{3,2},{4,5},{5,4},{6,7},{7,6},{8,9},{9,8},{10,11... | collective-permute-start | bytes 393224 | tf_op jit(solution)/shard_map/ppermute | solution.py:455
  66.6 6.5 %collective-permute-start.16 = (f32[2,112,128]{2,1,0:T(8,128)S(1)}, f32[2,112,128]{2,1,0:T(8,128)S(1)}, u32[]{:S(2)}, u32[]{:S(2)}) collective-permute-start(f32[2,112,128]{2,1,0:T(8,128)S(1)} %get-tuple-element.34), channel_id=1, source_target_pairs={{0,8},{1,9},{2,10},{3,11},{4,12},{5,13},{6,14},{7,15},{8,0},{9,1},... | collective-permute-start | bytes 344072 | tf_op jit(solution)/shard_map/ppermute | solution.py:455
  70.4 8.3 %collective-permute-start.13 = (bf16[4,128,128]{2,1,0:T(8,128)(2,1)S(1)}, bf16[4,128,128]{2,1,0:T(8,128)(2,1)S(1)}, u32[]{:S(2)}, u32[]{:S(2)}) collective-permute-start(bf16[4,128,128]{2,1,0:T(8,128)(2,1)S(1)} %shard_map.129.own_ref), channel_id=1, source_target_pairs={{0,2},{1,3},{2,0},{3,1},{4,6},{5,7},{6,4},{7,5},{8,10},{9,11},{10,... | collective-permute-start | bytes 393224 | tf_op jit(solution)/shard_map/ppermute | solution.py:455
  73.1 6.4 %collective-permute-start.17 = (f32[1,112,128]{2,1,0:T(8,128)S(1)}, f32[1,112,128]{2,1,0:T(8,128)S(1)}, u32[]{:S(2)}, u32[]{:S(2)}) collective-permute-start(f32[1,112,128]{2,1,0:T(8,128)S(1)} %get-tuple-element.36), channel_id=1, source_target_pairs={{0,16},{1,17},{2,18},{3,19},{4,20},{5,21},{6,22},{7,23},{8,24},{9,... | collective-permute-start | bytes 172040 | tf_op jit(solution)/shard_map/ppermute | solution.py:455
  78.8 11.5 %collective-permute-start.14 = (bf16[4,128,128]{2,1,0:T(8,128)(2,1)S(1)}, bf16[4,128,128]{2,1,0:T(8,128)(2,1)S(1)}, u32[]{:S(2)}, u32[]{:S(2)}) collective-permute-start(bf16[4,128,128]{2,1,0:T(8,128)(2,1)S(1)} %shard_map.130.own_ref), channel_id=1, source_target_pairs={{0,1},{1,0},{2,3},{3,2},{4,5},{5,4},{6,7},{7,6},{8,9},{9,8},{10,11... | collective-permute-start | bytes 393224 | tf_op jit(solution)/shard_map/ppermute | solution.py:455
  79.5 4.9 %collective-permute-start.18 = (f32[1,112,128]{2,1,0:T(8,128)S(1)}, f32[1,112,128]{2,1,0:T(8,128)S(1)}, u32[]{:S(2)}, u32[]{:S(2)}) collective-permute-start(f32[1,112,128]{2,1,0:T(8,128)S(1)} %shard_map.140.own_ref), channel_id=1, source_target_pairs={{0,1},{1,0},{2,3},{3,2},{4,5},{5,4},{6,7},{7,6},{8,9},{9,8},{10,11... | collective-permute-start | bytes 172040 | tf_op jit(solution)/shard_map/ppermute | solution.py:455
  84.5 5.8 %collective-permute-start.19 = (f32[1,112,128]{2,1,0:T(8,128)S(1)}, f32[1,112,128]{2,1,0:T(8,128)S(1)}, u32[]{:S(2)}, u32[]{:S(2)}) collective-permute-start(f32[1,112,128]{2,1,0:T(8,128)S(1)} %shard_map.141.lags_ref), channel_id=1, source_target_pairs={{0,2},{1,3},{2,0},{3,1},{4,6},{5,7},{6,4},{7,5},{8,10},{9,11},{10,... | collective-permute-start | bytes 172040 | tf_op jit(solution)/shard_map/ppermute | solution.py:455

commit v4 on v3

--- a/solution.py
+++ b/solution.py
@@ -106,65 +106,92 @@
     return jnp.sum(value, axis=0, keepdims=True)
 
 
-def conv_body(len_hbm, off_hbm, acts_hbm, k_hbm, g_hbm, b_hbm, gp_ref, cv_ref, st_ref, ok_ref, in_ref, gb_ref,
-              acc_ref, len_ref, off_ref, acts_ref, k_ref, sems, slot_sems):
+def conv_body(len_hbm, off_hbm, acts_hbm, k_hbm, g_hbm, b_hbm, w_hbm, c_hbm,
+              gp_ref, cv_ref, st_ref, ok_ref, in_ref, gb_ref, bk_hbm,
+              acc_ref, len_ref, off_ref, acts_ref, k_ref, w_ref, c_ref, bk_ref,
+              sems, slot_sems, w_sems, bk_sems):
     slots, frames, wide = acts_ref.shape
-    blocks, _, rows, _ = gp_ref.shape
+    blocks = gp_ref.shape[0]
     taps = k_ref.shape[0]
     lead = taps // 2
+    pitch = frames + lead
+    pairs = (
+        (len_hbm, len_ref),
+        (off_hbm, off_ref),
+        (k_hbm, k_ref),
+        (c_hbm, c_ref),
+        (g_hbm, gb_ref.at[0]),
+        (b_hbm, gb_ref.at[1]),
+    )
     small = [
-        pltpu.make_async_copy(source, target, sems.at[i])
-        for i, (source, target) in enumerate(
-            (
-                (len_hbm, len_ref),
-                (off_hbm, off_ref),
-                (k_hbm, k_ref),
-                (g_hbm, gb_ref.at[0]),
-                (b_hbm, gb_ref.at[1]),
-            )
-        )
+        pltpu.make_async_copy(source, target, sems.at[i]) for i, (source, target) in enumerate(pairs)
     ]
 
     def fetch(slot):
         return pltpu.make_async_copy(acts_hbm.at[slot], acts_ref.at[slot], slot_sems.at[slot])
+
+    def fetch_rows(block):
+        rows = pl.ds(pl.multiple_of(block * LANES, LANES), LANES)
+        return pltpu.make_async_copy(w_hbm.at[rows], w_ref.at[rows], w_sems.at[block])
+
+    def put_back(block):
+        return pltpu.make_async_copy(bk_ref.at[block], bk_hbm.at[block], bk_sems.at[block])
 
     small[0].start()
     small[1].start()
     fetch(0).start()
     small[2].start()
-    for slot in range(1, slots):
-        fetch(slot).start()
-    for copy in small[3:]:
-        copy.start()
+    small[3].start()
+    for at in range(max(blocks, slots)):
+        if at < blocks:
+            fetch_rows(at).start()
+        if 0 < at + 1 < slots:
+            fetch(at + 1).start()
+    small[4].start()
+    small[5].start()
     acc_ref[...] = jnp.zeros_like(acc_ref)
+    for block in range(blocks):
+        for slot in range(slots + 1):
+            gp_ref[block, slot * pitch : slot * pitch + lead, :] = jnp.zeros((lead, LANES), F32)
     position = lax.broadcasted_iota(jnp.int32, (frames, LANES), 0)
     reach = lax.broadcasted_iota(jnp.int32, (taps, frames), 1)
     reach = reach - lax.broadcasted_iota(jnp.int32, (taps, frames), 0) + (lead - 1)
-    for copy in small[:3]:
+    for copy in small[:4]:
         copy.wait()
 
-    def one(slot, carry):
+    def back(block):
+        rows = pl.ds(pl.multiple_of(block * LANES, LANES), LANES)
+        bk_ref[block] = lax.dot_general(
+            c_ref[...], w_ref[rows, :], (((1,), (1,)), ((), ())), preferred_element_type=F32
+        )
+        put_back(block).start()
+
+    inside = min(slots, blocks)
+
+    def one(slot, carry, also=False):
         low = off_ref[slot]
         high = low + len_ref[slot]
+        fetch(slot).wait()
+        if also:
+            fetch_rows(slot).wait()
+            back(slot)
         valid = ((position >= low) & (position < high)).astype(F32)
         ok_ref[slot] = valid
         in_ref[slot] = (
             (reach >= low) & (reach < high) & (reach >= 0) & (reach < frames)
-        ).astype(F32)
-        fetch(slot).wait()
+        ).astype(F32).astype(BF16)
+        first = pl.multiple_of(slot * pitch, 8)
         for block in range(blocks):
             cols = slice(block * LANES, (block + 1) * LANES)
             gate = slice(wide // 2 + block * LANES, wide // 2 + (block + 1) * LANES)
             left, right = acts_ref[slot, :, cols].astype(F32), acts_ref[slot, :, gate].astype(F32)
-            gp_ref[block, slot, 0:lead, :] = jnp.zeros((lead, LANES), F32)
-            gp_ref[block, slot, lead : lead + frames, :] = left * jax.nn.sigmoid(right) * valid
-            tail = jnp.zeros((rows - lead - frames, LANES), F32)
-            gp_ref[block, slot, lead + frames : rows, :] = tail
+            rows = pl.ds(pl.multiple_of(first + lead, 8), frames)
+            gp_ref[block, rows, :] = left * jax.nn.sigmoid(right) * valid
         for block in range(blocks):
             cols = slice(block * LANES, (block + 1) * LANES)
-            total = gp_ref[block, slot, 1 : 1 + frames, :] * k_ref[0:1, cols]
+            total = gp_ref[block, pl.ds(first + 1, frames), :] * k_ref[0:1, cols]
             for tap in range(1, taps):
-                lag = gp_ref[block, slot, 1 + tap : 1 + tap + frames, :]
+                lag = gp_ref[block, pl.ds(first + 1 + tap, frames), :]
                 total = total + lag * k_ref[tap : tap + 1, cols]
             cv_ref[block, slot] = total
             masked = total * valid
@@ -172,9 +199,15 @@
             acc_ref[1, block] += fold(masked * total)
         return carry
 
-    lax.fori_loop(0, slots, one, 0)
-    for copy in small[3:]:
-        copy.wait()
+    lax.fori_loop(0, inside, functools.partial(one, also=True), 0)
+    lax.fori_loop(inside, slots, one, 0)
+    for block in range(inside, blocks):
+        fetch_rows(block).wait()
+        back(block)
+    small[4].wait()
+    small[5].wait()
+    for block in range(blocks):
+        put_back(block).wait()
     for block in range(blocks):
         cols = slice(block * LANES, (block + 1) * LANES)
         st_ref[0:1, cols] = row_sum(acc_ref[0, block])
@@ -185,16 +218,16 @@
     st_ref[:, blocks * LANES :] = jnp.full((2, LANES), count.astype(F32), F32)
 
 
-def lag_sums(gp_ref, block, weights, taps, group, put):
+def lag_sums(gp_ref, block, weights, slots, taps, group, put):
     frames = weights(0).shape[0]
-    slots = gp_ref.shape[1]
+    pitch = frames + taps // 2
     for low in range(0, taps, group):
         sums = [None] * group
         for slot in range(slots):
             weight = weights(slot)
             for j in range(group):
-                at = 1 + low + j
-                term = fold(weight * gp_ref[block, slot, at : at + frames, :])
+                at = slot * pitch + 1 + low + j
+                term = fold(weight * gp_ref[block, at : at + frames, :])
                 sums[j] = term if sums[j] is None else sums[j] + term
         for j in range(group):
             put(low + j, row_sum(sums[j]))
@@ -213,11 +246,12 @@
         def put(k, row):
             out_ref[i, 0, k : k + 1, :] = row
 
-        lag_sums(gp_ref, block, lambda slot: wt_ref[slot], taps, 16, put)
+        lag_sums(gp_ref, block, lambda slot: wt_ref[slot], slots, taps, 16, put)
         total = jnp.zeros((taps, LANES), F32)
         for slot in range(slots):
-            inside = in_ref[slot].astype(BF16)
-            rest = gp_ref[block, slot, lead : lead + frames, :]
+            inside = in_ref[slot]
+            first = slot * (frames + lead) + lead
+            rest = gp_ref[block, first : first + frames, :]
             for _ in range(3):
                 part = rest.astype(BF16)
                 rest = rest - part.astype(F32)
@@ -226,24 +260,6 @@
         return carry
 
     lax.fori_loop(0, many, one, 0)
-
-
-def back_body(start, cotan_hbm, w_hbm, out_ref, cotan_ref, w_ref, sems):
-    blocks = out_ref.shape[0]
-    fetch = pltpu.make_async_copy(cotan_hbm, cotan_ref, sems.at[blocks])
-    fetch.start()
-    copies = []
-    for block in range(blocks):
-        rows, source = pl.ds(block * LANES, LANES), pl.ds((start + block) * LANES, LANES)
-        copies.append(pltpu.make_async_copy(w_hbm.at[source], w_ref.at[rows], sems.at[block]))
-        copies[-1].start()
-    fetch.wait()
-    for block in range(blocks):
-        copies[block].wait()
-        rows = w_ref[block * LANES : (block + 1) * LANES, :]
-        out_ref[block] = lax.dot_general(
-            cotan_ref[...], rows, (((1,), (1,)), ((), ())), preferred_element_type=F32
-        )
 
 
 def scale_of(st_ref, block):
@@ -271,8 +287,10 @@
     lax.fori_loop(0, blocks, one, 0)
 
 
-def slope_body(st_ref, gb_ref, ok_ref, gp_ref, cv_ref, low_ref, high_ref, *refs):
-    aux_refs, (give_ref, keep_ref, sl_ref) = refs[:-3], refs[-3:]
+def slope_body(bk_hbm, st_ref, gb_ref, ok_ref, gp_ref, cv_ref, *refs):
+    aux_refs, (give_ref, keep_ref, sl_ref, bk_ref, sem) = refs[:-5], refs[-5:]
+    fetch = pltpu.make_async_copy(bk_hbm, bk_ref, sem)
+    fetch.start()
     blocks, slots, frames, _ = cv_ref.shape
     taps = aux_refs[0].shape[2]
     last = 3 * taps
@@ -280,7 +298,6 @@
 
     def one(i, aux_ref, odd, q_ref):
         block = 2 * i + odd
-        bk_ref, at = (low_ref, block) if 4 * i < blocks else (high_ref, block - blocks // 2)
         _, mean, inv = scale_of(st_ref, block)
         gain, shift = gb_ref[0, pl.ds(block, 1), :], gb_ref[1, pl.ds(block, 1), :]
         first = second = jnp.zeros((8, LANES), F32)
@@ -288,7 +305,7 @@
             normed = (cv_ref[block, slot] - mean) * inv
             shifted = gain * normed + shift
             sig = jax.nn.sigmoid(shifted)
-            back = bk_ref[at, slot * frames : (slot + 1) * frames, :]
+            back = bk_ref[block, slot * frames : (slot + 1) * frames, :]
             slope = back * sig * (1.0 + shifted * (1.0 - sig)) * ok_ref[slot]
             sl_ref[slot] = slope
             first, second = first + fold(slope), second + fold(slope * normed)
@@ -296,12 +313,13 @@
         def put(k, row):
             q_ref[i, k : k + 1, :] = row
 
-        lag_sums(gp_ref, block, lambda slot: sl_ref[slot], taps, 16, put)
+        lag_sums(gp_ref, block, lambda slot: sl_ref[slot], slots, taps, 16, put)
         q_ref[i, taps : 2 * taps, :] = aux_ref[odd, 1]
         q_ref[i, 2 * taps : last, :] = inv * (aux_ref[odd, 0] - mean * aux_ref[odd, 1])
         keep_ref[0, pl.ds(last + block, 1), :] = row_sum(first)
         keep_ref[0, pl.ds(last + blocks + block, 1), :] = row_sum(second)
 
+    fetch.wait()
     for i, aux_ref in enumerate(aux_refs):
         one(i, aux_ref, 1 - bit, give_ref)
         one(i, aux_ref, bit, keep_ref)
@@ -318,16 +336,26 @@
             ref[i] = own_ref[2 * i + odd] + recv_ref[2 * i + odd]
 
 
-def out_body(hid_ref, w_ref, out_ref):
+def out_body(hid_hbm, w_hbm, out_ref, hid_ref, w_ref, sems):
     blocks = hid_ref.shape[0]
     slots, frames, _ = out_ref.shape
+    copies = []
+    for block in range(blocks):
+        rows = pl.ds(block * LANES, LANES)
+        copies.append(
+            (
+                pltpu.make_async_copy(hid_hbm.at[block], hid_ref.at[block], sems.at[0, block]),
+                pltpu.make_async_copy(w_hbm.at[rows], w_ref.at[rows], sems.at[1, block]),
+            )
+        )
+        copies[-1][0].start()
+        copies[-1][1].start()
     total = None
     for block in range(blocks):
-        term = jnp.dot(
-            hid_ref[block],
-            w_ref[block * LANES : (block + 1) * LANES, :],
-            preferred_element_type=F32,
-        )
+        copies[block][0].wait()
+        copies[block][1].wait()
+        rows = w_ref[block * LANES : (block + 1) * LANES, :]
+        term = jnp.dot(hid_ref[block], rows, preferred_element_type=F32)
         total = term if total is None else total + term
     for slot in range(slots):
         out_ref[slot] = total[slot * frames : (slot + 1) * frames, :].astype(BF16)
@@ -421,13 +449,16 @@
     return pltpu.with_memory_space_constraint(value, pltpu.HBM)
 
 
-def call(body, shapes, scalars, args, flops=0, scratch=(), mib=8, **more):
+def call(body, shapes, scalars, args, flops=0, scratch=(), mib=8, here=False, **more):
     many = isinstance(shapes, list)
+    if here:
+        colour = lambda leaf: pltpu.VMEM(leaf.shape, leaf.dtype)
+        shapes = [colour(leaf) for leaf in shapes] if many else colour(shapes)
     moved = sum(a.size * a.dtype.itemsize for a in args)
     return pl.pallas_call(
         body,
         in_specs=more.pop("in_specs", None) or [SMEM] * len(scalars) + [VMEM] * len(args),
-        out_specs=[VMEM] * len(shapes) if many else VMEM,
+        out_specs=more.pop("out_specs", None) or ([VMEM] * len(shapes) if many else VMEM),
         out_shape=shapes,
         scratch_shapes=scratch,
         compiler_params=pltpu.CompilerParams(vmem_limit_bytes=mib << 20),
@@ -443,7 +474,7 @@
     blocks = width // LANES
     tokens = slots * frames
     n_q = 3 * taps + 2 * blocks
-    padded = 2 * (taps // 2) + frames
+    padded = slots * (frames + taps // 2) + taps // 2
     shape = jax.ShapeDtypeStruct
 
     def swap(value, dp_mask, grp_mask):
@@ -468,20 +499,21 @@
     late_bits = dp_bits[-1] | dp_bits[-2]
     pieces.sort(key=lambda piece: piece[0] & late_bits == late_bits)
     masks, values = tuple(m for m, _ in pieces), [v for _, v in pieces]
-    early = sum(m & late_bits != late_bits for m in masks)
-
-    gated, conv_out, stats, valid, inside, gains = call(
+    early = n_dp * 5 // 8
+
+    gated, conv_out, stats, valid, inside, gains, back = call(
         conv_body,
         [
-            shape((blocks, slots, padded, LANES), F32),
+            shape((blocks, padded, LANES), F32),
             shape((blocks, slots, frames, LANES), F32),
             shape((2, width + LANES), F32),
             shape((slots, frames, LANES), F32),
-            shape((slots, taps, frames), F32),
+            shape((slots, taps, frames), BF16),
             shape((2, blocks, LANES), F32),
+            pltpu.HBM((blocks, tokens, LANES), F32),
         ],
         (),
-        [in_hbm(v) for v in (lengths, offsets, acts, kernel, gamma2, beta2)],
+        [in_hbm(v) for v in (lengths, offsets, acts, kernel, gamma2, beta2, w_out, flat_cotan)],
         flops=4 * taps * tokens * width,
         scratch=[
             pltpu.VMEM((2, blocks, 8, LANES), F32),
@@ -489,32 +521,22 @@
             pltpu.SMEM((slots,), jnp.int32),
             pltpu.VMEM(acts.shape, BF16),
             pltpu.VMEM(kernel.shape, F32),
-            pltpu.SemaphoreType.DMA((5,)),
+            pltpu.VMEM(w_out.shape, BF16),
+            pltpu.VMEM(flat_cotan.shape, BF16),
+            pltpu.VMEM((blocks, tokens, LANES), F32),
+            pltpu.SemaphoreType.DMA((6,)),
             pltpu.SemaphoreType.DMA((slots,)),
+            pltpu.SemaphoreType.DMA((blocks,)),
+            pltpu.SemaphoreType.DMA((blocks,)),
         ],
-        in_specs=[HBM] * 6,
+        out_specs=[VMEM] * 6 + [HBM],
+        in_specs=[HBM] * 8,
     )
 
     hops = [(1, m) for m in grp_bits] + [(m | 1, 0) for m in dp_bits[:0:-1]] + [(1, 0)]
     for dp_mask, grp_mask in hops:
         stats = plus(stats, swap(stats, dp_mask, grp_mask))
 
-    back = [
-        call(
-            functools.partial(back_body, i * (blocks // 2)),
-            shape((blocks // 2, tokens, LANES), F32),
-            (),
-            (in_hbm(flat_cotan), in_hbm(w_out)),
-            flops=tokens * width * width,
-            scratch=[
-                pltpu.VMEM(flat_cotan.shape, BF16),
-                pltpu.VMEM((width // 2, width), BF16),
-                pltpu.SemaphoreType.DMA((blocks // 2 + 1,)),
-            ],
-            in_specs=[HBM] * 2,
-        )
-        for i in range(2)
-    ]
     parts = blocks // 2
     each = 2
     aux = [
@@ -524,6 +546,7 @@
             (),
             (valid, inside, gated, conv_out),
             flops=4 * taps * tokens * each * LANES,
+            here=True,
             scratch=[pltpu.VMEM((slots, frames, LANES), F32)],
         )
         for i in range(parts)
@@ -537,9 +560,15 @@
         slope_body,
         [shape((parts, n_q, LANES), F32)] * 2,
         (),
-        (stats, gains, valid, gated, conv_out, *back, *aux),
+        (in_hbm(back), stats, gains, valid, gated, conv_out, *aux),
         flops=4 * taps * tokens * width,
-        scratch=[pltpu.VMEM((slots, frames, LANES), F32)],
+        scratch=[
+            pltpu.VMEM((slots, frames, LANES), F32),
+            pltpu.VMEM(back.shape, F32),
+            pltpu.SemaphoreType.DMA,
+        ],
+        in_specs=[HBM] + [VMEM] * (5 + parts),
+        here=True,
     )
     for level in range(1, len(dp_bits)):
         came = swap(give, dp_bits[level - 1], 0)
@@ -548,10 +577,23 @@
             [shape((parts >> level, n_q, LANES), F32)] * 2,
             (),
             (lags, came),
+            here=True,
         )
     lags = plus(lags, swap(give, dp_bits[-1], 0))
     scale = call(scale_body, shape((2, LANES), F32), (), (stats, gains))
-    outputs = call(out_body, shape(cotan.shape, BF16), (), (hidden, w_out))
+    outputs = call(
+        out_body,
+        shape(cotan.shape, BF16),
+        (),
+        (in_hbm(hidden), in_hbm(w_out)),
+        flops=2 * tokens * width * width,
+        scratch=[
+            pltpu.VMEM(hidden.shape, BF16),
+            pltpu.VMEM(w_out.shape, BF16),
+            pltpu.SemaphoreType.DMA((2, blocks)),
+        ],
+        in_specs=[HBM] * 2,
+    )
 
     half_shape = shape((blocks // 2, LANES, LANES), BF16)
     staged = call(

time: 91.5 us -> 88.6 us (0.968)
  local copies, waits for them, and re-layouts: 3.91 us -> 0.69 us
  Pallas kernels: 22.1 us -> 23.4 us
    unnamed x12 -> x6, local copies, waits for them, and re-layouts: 3.91 us -> 0.69 us
    pallas_call x25 -> x23, Pallas kernels: 22.1 us -> 23.4 us  [call(): pl.pallas_call(body, in_specs=more.pop('in_specs', None) or [SMEM] * len(...]
  transfers between devices with their start and end apart: 21 -> 21, of which waited for: 10 -> 10; matrix products, arithmetic and copies ran while one was open for 0% -> 0% of each run, Pallas kernels for 23% -> 25%
where the time goes in v4:
time: 88.6 us; the launch traced here: 88.3 us
  starting transfers between devices  32.2 us (36%)
  waiting for transfers between devices  31.2 us (35%)
  Pallas kernels  23.4 us (26%)
    ppermute x20, waiting for transfers between devices, swap(): return lax.ppermute(value, ('dp', 'grp'), pairs)  31.2 us
    ppermute x20, starting transfers between devices, swap(): return lax.ppermute(value, ('dp', 'grp'), pairs)  28.5 us
    pallas_call x23, Pallas kernels, call(): pl.pallas_call(body, in_specs=more.pop('in_specs', None) or [SMEM] * len(...  23.4 us
    all_to_all x1, starting transfers between devices, local_fast(): received = lax.all_to_all(hidden, 'dp', 0, 0, tiled=True)  3.69 us
  transfers between devices with their start and end apart: 21, of which 10 were waited for; matrix products, arithmetic and copies ran while one was open for 0% of the time, Pallas kernels for 25%

profile of v4, /device:TPU:0, one launch (start us, length us, event | category | flops | bytes accessed | tf_op | source)
XLA Modules:
  0.0 88.3 jit_solution(14889047290338455460)
XLA Ops:
  0.6 3.0 %collective-permute-start.5 = (bf16[192,1024]{1,0:T(8,128)(2,1)}, bf16[192,1024]{1,0:T(8,128)(2,1)}, u32[]{:S(2)}, u32[]{:S(2)}) collective-permute-start(bf16[192,1024]{1,0:T(8,128)(2,1)} %bitcast.5), channel_id=1, source_target_pairs={{0,8},{1,9},{2,10},{3,11},{4,12},{5,13},{6,14},{7,15},{8,0},{9,1},... | collective-permute-start | bytes 1179656 | tf_op jit(solution)/shard_map/ppermute | solution.py:486
  3.7 1.5 %collective-permute-start.6 = (bf16[192,1024]{1,0:T(8,128)(2,1)}, bf16[192,1024]{1,0:T(8,128)(2,1)}, u32[]{:S(2)}, u32[]{:S(2)}) collective-permute-start(bf16[192,1024]{1,0:T(8,128)(2,1)} %bitcast.6), channel_id=1, source_target_pairs={{0,16},{1,17},{2,18},{3,19},{4,20},{5,21},{6,22},{7,23},{8,24},{9,... | collective-permute-start | bytes 1179656 | tf_op jit(solution)/shard_map/ppermute | solution.py:486
  5.2 7.9 %collective-permute-done.5.refs_1_ = bf16[192,1024]{1,0:T(8,128)(2,1)} collective-permute-done((bf16[192,1024]{1,0:T(8,128)(2,1)}, bf16[192,1024]{1,0:T(8,128)(2,1)}, u32[]{:S(2)}, u32[]{:S(2)}) %collective-permute-start.5) | collective-permute-done | bytes 393248 | tf_op jit(solution)/shard_map/ppermute | solution.py:486
  13.1 1.8 %collective-permute-start.10 = (bf16[192,1024]{1,0:T(8,128)(2,1)}, bf16[192,1024]{1,0:T(8,128)(2,1)S(1)}, u32[]{:S(2)}, u32[]{:S(2)}) collective-permute-start(bf16[192,1024]{1,0:T(8,128)(2,1)} %collective-permute-done.5.refs_1_), channel_id=1, source_target_pairs={{0,16},{1,17},{2,18},{3,19},{4,20},{5,21},{6,22},{7,23},{8,24},{9,... | collective-permute-start | bytes 1179656 | tf_op jit(solution)/shard_map/ppermute | solution.py:486
  14.9 0.0 collective-permute-start.7
  14.9 0.5 collective-permute-start.8
  15.4 0.0 collective-permute-start.9
  15.4 8.2 %collective-permute-done.10.refs_1_ = bf16[192,1024]{1,0:T(8,128)(2,1)S(1)} collective-permute-done((bf16[192,1024]{1,0:T(8,128)(2,1)}, bf16[192,1024]{1,0:T(8,128)(2,1)S(1)}, u32[]{:S(2)}, u32[]{:S(2)}) %collective-permute-start.10) | collective-permute-done | bytes 393248 | tf_op jit(solution)/shard_map/ppermute | solution.py:486
  23.6 6.7 %shard_map.119 = (f32[8,304,128]{2,1,0:T(8,128)S(1)}, f32[8,6,32,128]{3,2,1,0:T(8,128)S(1)}, f32[2,1152]{1,0:T(2,128)S(1)}, f32[6,32,128]{2,1,0:T(8,128)S(1)}, b...) custom-call(s32[6]{0:T(128)} %len_hbm.1, s32[6]{0:T(128)} %off_hbm.1, ...), custom_call_target="tpu_custom_call" | custom-call | flops 25165824 | bytes 3416112 | tf_op jit(solution)/shard_map/pallas_call | solution.py:458
  30.3 1.7 %collective-permute-start = (f32[2,1152]{1,0:T(2,128)S(1)}, f32[2,1152]{1,0:T(2,128)S(1)}, u32[]{:S(2)}, u32[]{:S(2)}) collective-permute-start(f32[2,1152]{1,0:T(2,128)S(1)} %get-tuple-element.24.own_ref), channel_id=1, source_target_pairs={{0,5},{1,4},{2,7},{3,6},{4,1},{5,0},{6,3},{7,2},{8,13},{9,12},{10,... | collective-permute-start | bytes 27656 | tf_op jit(solution)/shard_map/ppermute | solution.py:486
  32.1 1.4 %collective-permute-done.recv_ref = f32[2,1152]{1,0:T(2,128)S(1)} collective-permute-done((f32[2,1152]{1,0:T(2,128)S(1)}, f32[2,1152]{1,0:T(2,128)S(1)}, u32[]{:S(2)}, u32[]{:S(2)}) %collective-permute-start) | collective-permute-done | bytes 9248 | tf_op jit(solution)/shard_map/ppermute | solution.py:486
  33.5 2.7 %collective-permute-start.1 = (f32[2,1152]{1,0:T(2,128)S(1)}, f32[2,1152]{1,0:T(2,128)S(1)}, u32[]{:S(2)}, u32[]{:S(2)}) collective-permute-start(f32[2,1152]{1,0:T(2,128)S(1)} %shard_map.120.own_ref), channel_id=1, source_target_pairs={{0,6},{1,7},{2,4},{3,5},{4,2},{5,3},{6,0},{7,1},{8,14},{9,15},{10,... | collective-permute-start | bytes 27656 | tf_op jit(solution)/shard_map/ppermute | solution.py:486
  36.2 1.4 %collective-permute-done.1.recv_ref = f32[2,1152]{1,0:T(2,128)S(1)} collective-permute-done((f32[2,1152]{1,0:T(2,128)S(1)}, f32[2,1152]{1,0:T(2,128)S(1)}, u32[]{:S(2)}, u32[]{:S(2)}) %collective-permute-start.1) | collective-permute-done | bytes 9248 | tf_op jit(solution)/shard_map/ppermute | solution.py:486
  37.5 1.5 %collective-permute-start.2 = (f32[2,1152]{1,0:T(2,128)S(1)}, f32[2,1152]{1,0:T(2,128)S(1)}, u32[]{:S(2)}, u32[]{:S(2)}) collective-permute-start(f32[2,1152]{1,0:T(2,128)S(1)} %shard_map.121.own_ref), channel_id=1, source_target_pairs={{0,20},{1,21},{2,22},{3,23},{4,16},{5,17},{6,18},{7,19},{8,28},{9,... | collective-permute-start | bytes 27656 | tf_op jit(solution)/shard_map/ppermute | solution.py:486
  39.1 1.5 %collective-permute-done.2.recv_ref = f32[2,1152]{1,0:T(2,128)S(1)} collective-permute-done((f32[2,1152]{1,0:T(2,128)S(1)}, f32[2,1152]{1,0:T(2,128)S(1)}, u32[]{:S(2)}, u32[]{:S(2)}) %collective-permute-start.2) | collective-permute-done | bytes 9248 | tf_op jit(solution)/shard_map/ppermute | solution.py:486
  40.6 1.5 %collective-permute-start.3 = (f32[2,1152]{1,0:T(2,128)S(1)}, f32[2,1152]{1,0:T(2,128)S(1)}, u32[]{:S(2)}, u32[]{:S(2)}) collective-permute-start(f32[2,1152]{1,0:T(2,128)S(1)} %shard_map.122.own_ref), channel_id=1, source_target_pairs={{0,12},{1,13},{2,14},{3,15},{4,8},{5,9},{6,10},{7,11},{8,4},{9,5},... | collective-permute-start | bytes 27656 | tf_op jit(solution)/shard_map/ppermute | solution.py:486
  42.1 1.6 %collective-permute-done.3.recv_ref = f32[2,1152]{1,0:T(2,128)S(1)} collective-permute-done((f32[2,1152]{1,0:T(2,128)S(1)}, f32[2,1152]{1,0:T(2,128)S(1)}, u32[]{:S(2)}, u32[]{:S(2)}) %collective-permute-start.3) | collective-permute-done | bytes 9248 | tf_op jit(solution)/shard_map/ppermute | solution.py:486
  43.7 0.4 collective-permute-start.4
  44.2 0.8 collective-permute-done.4.recv_ref
  45.0 1.2 %shard_map.125.hid_hbm = bf16[8,192,128]{2,1,0:T(8,128)(2,1)} custom-call(f32[2,1152]{1,0:T(2,128)S(1)} %shard_map.124.st_ref, f32[2,8,128]{2,1,0:T(8,128)S(1)} %get-tuple-element.25.gb_ref, f32[6,32,128]{2,1,0:T(8,128)S(1)} %get-tuple-element.26.ok_ref, f32[8,6,32,128]{3,2,1,0:T(8,128)S(1)} %get-tuple-element.27.cv_ref), custom_call_target="tpu_custom_call" | custom-call | bytes 902144 | tf_op jit(solution)/shard_map/pallas_call | solution.py:458
  46.2 3.7 %all-to-all-start = ((bf16[8,192,128]{2,1,0:T(8,128)(2,1)}), bf16[8,192,128]{2,1,0:T(8,128)(2,1)S(1)}, u32[]{:S(2)}, u32[]{:S(2)}) async-start(bf16[8,192,128]{2,1,0:T(8,128)(2,1)} %shard_map.125.hid_hbm), calls=%async_computation | async-start | bytes 786432 | tf_op jit(solution)/shard_map/all_to_all | solution.py:558
  49.9 0.7 shard_map.134.refs_3_
  50.5 0.7 shard_map.133.refs_2_
  51.2 0.7 shard_map.132.refs_1_
  51.9 0.7 shard_map.131.refs_0_
  52.6 0.0 copy-start
  52.6 4.2 %shard_map.135 = (f32[4,112,128]{2,1,0:T(8,128)}, f32[4,112,128]{2,1,0:T(8,128)S(1)}) custom-call(f32[8,192,128]{2,1,0:T(8,128)} %get-tuple-element.30.bk_hbm, f32[2,1152]{1,0:T(2,128)S(1)} %shard_map.124.st_ref, f32[2,8,128]{2,1,0:T(8,128)S(1)} %get-tuple-element.25.gb_ref, f32[6,32,128]{2,1,0:T(8,128)S(1)} %get-tuple-element.26.ok_ref, ...), custom_call_target="tpu_custom_call" | custom-call | flops 25165824 | bytes 3195904 | tf_op jit(solution)/shard_map/pallas_call | solution.py:458
  56.9 0.7 copy-done.1
  57.5 0.5 collective-permute-start.15
  58.1 1.6 %shard_map.127.staged_ref = bf16[5,192,1024]{2,1,0:T(8,128)(2,1)S(1)} custom-call(bf16[192,1024]{1,0:T(8,128)(2,1)S(1)} %bitcast.9, bf16[192,1024]{1,0:T(8,128)(2,1)} %collective-permute-done.5.refs_1_, bf16[192,1024]{1,0:T(8,128)(2,1)} %collective-permute-done.6.refs_2_, bf16[192,1024]{1,0:T(8,128)(2,1)} %collective-permute-done.7.refs_3_, ...), custom_call_target="tpu_custom_call" | custom-call | bytes 1966080 | tf_op jit(solution)/shard_map/pallas_call | solution.py:458
  59.7 0.0 all-to-all-done.recv_hbm
  59.7 0.0 collective-permute-done.9.refs_0_
  59.7 1.8 %shard_map.128 = (bf16[4,128,128]{2,1,0:T(8,128)(2,1)S(1)}, bf16[4,128,128]{2,1,0:T(8,128)(2,1)S(1)}) custom-call(bf16[8,192,128]{2,1,0:T(8,128)(2,1)S(1)} %all-to-all-done.recv_hbm, bf16[5,192,1024]{2,1,0:T(8,128)(2,1)S(1)} %shard_map.127.staged_ref, bf16[192,1024]{1,0:T(8,128)(2,1)S(1)} %collective-permute-done.9.refs_0_, ...), custom_call_target="tpu_custom_call" | custom-call | flops 402653184 | bytes 3538944 | tf_op jit(solution)/shard_map/pallas_call | solution.py:458
  61.6 1.6 %collective-permute-start.12 = (bf16[4,128,128]{2,1,0:T(8,128)(2,1)S(1)}, bf16[4,128,128]{2,1,0:T(8,128)(2,1)S(1)}, u32[]{:S(2)}, u32[]{:S(2)}) collective-permute-start(bf16[4,128,128]{2,1,0:T(8,128)(2,1)S(1)} %get-tuple-element.29), channel_id=1, source_target_pairs={{0,1},{1,0},{2,3},{3,2},{4,5},{5,4},{6,7},{7,6},{8,9},{9,8},{10,11... | collective-permute-start | bytes 393224 | tf_op jit(solution)/shard_map/ppermute | solution.py:486
  63.2 1.0 %shard_map.136 = (f32[2,112,128]{2,1,0:T(8,128)S(1)}, f32[2,112,128]{2,1,0:T(8,128)S(1)}) custom-call(f32[4,112,128]{2,1,0:T(8,128)S(1)} %copy-done.2, f32[4,112,128]{2,1,0:T(8,128)} %collective-permute-done.15.recv_ref), custom_call_target="tpu_custom_call" | custom-call | bytes 458752 | tf_op jit(solution)/shard_map/pallas_call | solution.py:458
  64.2 1.7 %collective-permute-start.16 = (f32[2,112,128]{2,1,0:T(8,128)S(1)}, f32[2,112,128]{2,1,0:T(8,128)S(1)}, u32[]{:S(2)}, u32[]{:S(2)}) collective-permute-start(f32[2,112,128]{2,1,0:T(8,128)S(1)} %get-tuple-element.36), channel_id=1, source_target_pairs={{0,8},{1,9},{2,10},{3,11},{4,12},{5,13},{6,14},{7,15},{8,0},{9,1},... | collective-permute-start | bytes 344072 | tf_op jit(solution)/shard_map/ppermute | solution.py:486
  65.9 1.2 %collective-permute-done.12.recv_ref = bf16[4,128,128]{2,1,0:T(8,128)(2,1)S(1)} collective-permute-done((bf16[4,128,128]{2,1,0:T(8,128)(2,1)S(1)}, bf16[4,128,128]{2,1,0:T(8,128)(2,1)S(1)}, u32[]{:S(2)}, u32[]{:S(2)}) %collective-permute-start.12) | collective-permute-done | bytes 131104 | tf_op jit(solution)/shard_map/ppermute | solution.py:486
  67.1 2.6 %collective-permute-start.13 = (bf16[4,128,128]{2,1,0:T(8,128)(2,1)S(1)}, bf16[4,128,128]{2,1,0:T(8,128)(2,1)S(1)}, u32[]{:S(2)}, u32[]{:S(2)}) collective-permute-start(bf16[4,128,128]{2,1,0:T(8,128)(2,1)S(1)} %shard_map.129.own_ref), channel_id=1, source_target_pairs={{0,2},{1,3},{2,0},{3,1},{4,6},{5,7},{6,4},{7,5},{8,10},{9,11},{10,... | collective-permute-start | bytes 393224 | tf_op jit(solution)/shard_map/ppermute | solution.py:486
  69.7 2.1 %collective-permute-start.17 = (f32[1,112,128]{2,1,0:T(8,128)S(1)}, f32[1,112,128]{2,1,0:T(8,128)S(1)}, u32[]{:S(2)}, u32[]{:S(2)}) collective-permute-start(f32[1,112,128]{2,1,0:T(8,128)S(1)} %get-tuple-element.38), channel_id=1, source_target_pairs={{0,16},{1,17},{2,18},{3,19},{4,20},{5,21},{6,22},{7,23},{8,24},{9,... | collective-permute-start | bytes 172040 | tf_op jit(solution)/shard_map/ppermute | solution.py:486
  71.8 3.6 %collective-permute-done.13.recv_ref = bf16[4,128,128]{2,1,0:T(8,128)(2,1)S(1)} collective-permute-done((bf16[4,128,128]{2,1,0:T(8,128)(2,1)S(1)}, bf16[4,128,128]{2,1,0:T(8,128)(2,1)S(1)}, u32[]{:S(2)}, u32[]{:S(2)}) %collective-permute-start.13) | collective-permute-done | bytes 131104 | tf_op jit(solution)/shard_map/ppermute | solution.py:486
  75.4 0.7 collective-permute-start.14
  76.2 0.0 collective-permute-done.17.recv_ref
  76.2 1.4 %collective-permute-start.18 = (f32[1,112,128]{2,1,0:T(8,128)S(1)}, f32[1,112,128]{2,1,0:T(8,128)S(1)}, u32[]{:S(2)}, u32[]{:S(2)}) collective-permute-start(f32[1,112,128]{2,1,0:T(8,128)S(1)} %shard_map.138.own_ref), channel_id=1, source_target_pairs={{0,1},{1,0},{2,3},{3,2},{4,5},{5,4},{6,7},{7,6},{8,9},{9,8},{10,11... | collective-permute-start | bytes 172040 | tf_op jit(solution)/shard_map/ppermute | solution.py:486
  77.6 3.5 %collective-permute-done.18.recv_ref = f32[1,112,128]{2,1,0:T(8,128)S(1)} collective-permute-done((f32[1,112,128]{2,1,0:T(8,128)S(1)}, f32[1,112,128]{2,1,0:T(8,128)S(1)}, u32[]{:S(2)}, u32[]{:S(2)}) %collective-permute-start.18) | collective-permute-done | bytes 57376 | tf_op jit(solution)/shard_map/ppermute | solution.py:486
  81.1 3.1 %collective-permute-start.19 = (f32[1,112,128]{2,1,0:T(8,128)S(1)}, f32[1,112,128]{2,1,0:T(8,128)S(1)}, u32[]{:S(2)}, u32[]{:S(2)}) collective-permute-start(f32[1,112,128]{2,1,0:T(8,128)S(1)} %shard_map.139.lags_ref), channel_id=1, source_target_pairs={{0,2},{1,3},{2,0},{3,1},{4,6},{5,7},{6,4},{7,5},{8,10},{9,11},{10,... | collective-permute-start | bytes 172040 | tf_op jit(solution)/shard_map/ppermute | solution.py:486
  84.2 3.1 %shard_map.126 = bf16[6,32,1024]{2,1,0:T(8,128)(2,1)} custom-call(bf16[8,192,128]{2,1,0:T(8,128)(2,1)} %shard_map.125.hid_hbm, bf16[1024,1024]{1,0:T(8,128)(2,1)} %w_hbm.3), custom_call_target="tpu_custom_call" | custom-call | flops 402653184 | bytes 2490368 | tf_op jit(solution)/shard_map/pallas_call | solution.py:458
  87.4 0.0 collective-permute-done.19.more_ref
  87.4 0.9 shard_map.141
  (23 shorter events, 0.2 us)
Async XLA Ops:
  0.6 12.5 %collective-permute-start.5 = (bf16[192,1024]{1,0:T(8,128)(2,1)}, bf16[192,1024]{1,0:T(8,128)(2,1)}, u32[]{:S(2)}, u32[]{:S(2)}) collective-permute-start(bf16[192,1024]{1,0:T(8,128)(2,1)} %bitcast.5), channel_id=1, source_target_pairs={{0,8},{1,9},{2,10},{3,11},{4,12},{5,13},{6,14},{7,15},{8,0},{9,1},... | collective-permute-start | bytes 1179656 | tf_op jit(solution)/shard_map/ppermute | solution.py:486
  3.7 11.7 %collective-permute-start.6 = (bf16[192,1024]{1,0:T(8,128)(2,1)}, bf16[192,1024]{1,0:T(8,128)(2,1)}, u32[]{:S(2)}, u32[]{:S(2)}) collective-permute-start(bf16[192,1024]{1,0:T(8,128)(2,1)} %bitcast.6), channel_id=1, source_target_pairs={{0,16},{1,17},{2,18},{3,19},{4,20},{5,21},{6,22},{7,23},{8,24},{9,... | collective-permute-start | bytes 1179656 | tf_op jit(solution)/shard_map/ppermute | solution.py:486
  13.1 10.5 %collective-permute-start.10 = (bf16[192,1024]{1,0:T(8,128)(2,1)}, bf16[192,1024]{1,0:T(8,128)(2,1)S(1)}, u32[]{:S(2)}, u32[]{:S(2)}) collective-permute-start(bf16[192,1024]{1,0:T(8,128)(2,1)} %collective-permute-done.5.refs_1_), channel_id=1, source_target_pairs={{0,16},{1,17},{2,18},{3,19},{4,20},{5,21},{6,22},{7,23},{8,24},{9,... | collective-permute-start | bytes 1179656 | tf_op jit(solution)/shard_map/ppermute | solution.py:486
  14.9 43.2 %collective-permute-start.7 = (bf16[192,1024]{1,0:T(8,128)(2,1)}, bf16[192,1024]{1,0:T(8,128)(2,1)}, u32[]{:S(2)}, u32[]{:S(2)}) collective-permute-start(bf16[192,1024]{1,0:T(8,128)(2,1)} %bitcast.7), channel_id=1, source_target_pairs={{0,4},{1,5},{2,6},{3,7},{4,0},{5,1},{6,2},{7,3},{8,12},{9,13},{10,... | collective-permute-start | bytes 1179656 | tf_op jit(solution)/shard_map/ppermute | solution.py:486
  14.9 43.2 %collective-permute-start.8 = (bf16[192,1024]{1,0:T(8,128)(2,1)}, bf16[192,1024]{1,0:T(8,128)(2,1)}, u32[]{:S(2)}, u32[]{:S(2)}) collective-permute-start(bf16[192,1024]{1,0:T(8,128)(2,1)} %collective-permute-done.5.refs_1_), channel_id=1, source_target_pairs={{0,4},{1,5},{2,6},{3,7},{4,0},{5,1},{6,2},{7,3},{8,12},{9,13},{10,... | collective-permute-start | bytes 1179656 | tf_op jit(solution)/shard_map/ppermute | solution.py:486
  15.4 44.3 %collective-permute-start.9 = (bf16[192,1024]{1,0:T(8,128)(2,1)}, bf16[192,1024]{1,0:T(8,128)(2,1)S(1)}, u32[]{:S(2)}, u32[]{:S(2)}) collective-permute-start(bf16[192,1024]{1,0:T(8,128)(2,1)} %collective-permute-done.6.refs_2_), channel_id=1, source_target_pairs={{0,4},{1,5},{2,6},{3,7},{4,0},{5,1},{6,2},{7,3},{8,12},{9,13},{10,... | collective-permute-start | bytes 1179656 | tf_op jit(solution)/shard_map/ppermute | solution.py:486
  23.6 36.1 %collective-permute-start.11 = (bf16[192,1024]{1,0:T(8,128)(2,1)S(1)}, bf16[192,1024]{1,0:T(8,128)(2,1)}, u32[]{:S(2)}, u32[]{:S(2)}) collective-permute-start(bf16[192,1024]{1,0:T(8,128)(2,1)S(1)} %collective-permute-done.10.refs_1_), channel_id=1, source_target_pairs={{0,4},{1,5},{2,6},{3,7},{4,0},{5,1},{6,2},{7,3},{8,12},{9,13},{10,... | collective-permute-start | bytes 1179656 | tf_op jit(solution)/shard_map/ppermute | solution.py:486
  30.3 3.2 %collective-permute-start = (f32[2,1152]{1,0:T(2,128)S(1)}, f32[2,1152]{1,0:T(2,128)S(1)}, u32[]{:S(2)}, u32[]{:S(2)}) collective-permute-start(f32[2,1152]{1,0:T(2,128)S(1)} %get-tuple-element.24.own_ref), channel_id=1, source_target_pairs={{0,5},{1,4},{2,7},{3,6},{4,1},{5,0},{6,3},{7,2},{8,13},{9,12},{10,... | collective-permute-start | bytes 27656 | tf_op jit(solution)/shard_map/ppermute | solution.py:486
  33.5 4.0 %collective-permute-start.1 = (f32[2,1152]{1,0:T(2,128)S(1)}, f32[2,1152]{1,0:T(2,128)S(1)}, u32[]{:S(2)}, u32[]{:S(2)}) collective-permute-start(f32[2,1152]{1,0:T(2,128)S(1)} %shard_map.120.own_ref), channel_id=1, source_target_pairs={{0,6},{1,7},{2,4},{3,5},{4,2},{5,3},{6,0},{7,1},{8,14},{9,15},{10,... | collective-permute-start | bytes 27656 | tf_op jit(solution)/shard_map/ppermute | solution.py:486
  37.5 3.1 %collective-permute-start.2 = (f32[2,1152]{1,0:T(2,128)S(1)}, f32[2,1152]{1,0:T(2,128)S(1)}, u32[]{:S(2)}, u32[]{:S(2)}) collective-permute-start(f32[2,1152]{1,0:T(2,128)S(1)} %shard_map.121.own_ref), channel_id=1, source_target_pairs={{0,20},{1,21},{2,22},{3,23},{4,16},{5,17},{6,18},{7,19},{8,28},{9,... | collective-permute-start | bytes 27656 | tf_op jit(solution)/shard_map/ppermute | solution.py:486
  40.6 3.1 %collective-permute-start.3 = (f32[2,1152]{1,0:T(2,128)S(1)}, f32[2,1152]{1,0:T(2,128)S(1)}, u32[]{:S(2)}, u32[]{:S(2)}) collective-permute-start(f32[2,1152]{1,0:T(2,128)S(1)} %shard_map.122.own_ref), channel_id=1, source_target_pairs={{0,12},{1,13},{2,14},{3,15},{4,8},{5,9},{6,10},{7,11},{8,4},{9,5},... | collective-permute-start | bytes 27656 | tf_op jit(solution)/shard_map/ppermute | solution.py:486
  43.7 1.3 %collective-permute-start.4 = (f32[2,1152]{1,0:T(2,128)S(1)}, f32[2,1152]{1,0:T(2,128)S(1)}, u32[]{:S(2)}, u32[]{:S(2)}) collective-permute-start(f32[2,1152]{1,0:T(2,128)S(1)} %shard_map.123.own_ref), channel_id=1, source_target_pairs={{0,4},{1,5},{2,6},{3,7},{4,0},{5,1},{6,2},{7,3},{8,12},{9,13},{10,... | collective-permute-start | bytes 27656 | tf_op jit(solution)/shard_map/ppermute | solution.py:486
  46.2 13.5 %all-to-all-start = ((bf16[8,192,128]{2,1,0:T(8,128)(2,1)}), bf16[8,192,128]{2,1,0:T(8,128)(2,1)S(1)}, u32[]{:S(2)}, u32[]{:S(2)}) async-start(bf16[8,192,128]{2,1,0:T(8,128)(2,1)} %shard_map.125.hid_hbm), calls=%async_computation | async-start | bytes 786432 | tf_op jit(solution)/shard_map/all_to_all | solution.py:558
  52.6 5.5 %copy-start = (bf16[6,32,1024]{2,1,0:T(8,128)(2,1)S(1)}, bf16[6,32,1024]{2,1,0:T(8,128)(2,1)}, u32[]{:S(2)}) copy-start(bf16[6,32,1024]{2,1,0:T(8,128)(2,1)} %param.9) | copy-start | bytes 1179652
  56.9 0.7 copy-start.1
  57.5 5.6 %collective-permute-start.15 = (f32[4,112,128]{2,1,0:T(8,128)}, f32[4,112,128]{2,1,0:T(8,128)}, u32[]{:S(2)}, u32[]{:S(2)}) collective-permute-start(f32[4,112,128]{2,1,0:T(8,128)} %get-tuple-element.34), channel_id=1, source_target_pairs={{0,4},{1,5},{2,6},{3,7},{4,0},{5,1},{6,2},{7,3},{8,12},{9,13},{10,... | collective-permute-start | bytes 688136 | tf_op jit(solution)/shard_map/ppermute | solution.py:486
  59.7 3.5 %copy-start.2 = (f32[4,112,128]{2,1,0:T(8,128)S(1)}, f32[4,112,128]{2,1,0:T(8,128)}, u32[]{:S(2)}) copy-start(f32[4,112,128]{2,1,0:T(8,128)} %copy-done.1) | copy-start | bytes 688132
  61.6 5.5 %collective-permute-start.12 = (bf16[4,128,128]{2,1,0:T(8,128)(2,1)S(1)}, bf16[4,128,128]{2,1,0:T(8,128)(2,1)S(1)}, u32[]{:S(2)}, u32[]{:S(2)}) collective-permute-start(bf16[4,128,128]{2,1,0:T(8,128)(2,1)S(1)} %get-tuple-element.29), channel_id=1, source_target_pairs={{0,1},{1,0},{2,3},{3,2},{4,5},{5,4},{6,7},{7,6},{8,9},{9,8},{10,11... | collective-permute-start | bytes 393224 | tf_op jit(solution)/shard_map/ppermute | solution.py:486
  64.2 5.6 %collective-permute-start.16 = (f32[2,112,128]{2,1,0:T(8,128)S(1)}, f32[2,112,128]{2,1,0:T(8,128)S(1)}, u32[]{:S(2)}, u32[]{:S(2)}) collective-permute-start(f32[2,112,128]{2,1,0:T(8,128)S(1)} %get-tuple-element.36), channel_id=1, source_target_pairs={{0,8},{1,9},{2,10},{3,11},{4,12},{5,13},{6,14},{7,15},{8,0},{9,1},... | collective-permute-start | bytes 344072 | tf_op jit(solution)/shard_map/ppermute | solution.py:486
  67.1 8.3 %collective-permute-start.13 = (bf16[4,128,128]{2,1,0:T(8,128)(2,1)S(1)}, bf16[4,128,128]{2,1,0:T(8,128)(2,1)S(1)}, u32[]{:S(2)}, u32[]{:S(2)}) collective-permute-start(bf16[4,128,128]{2,1,0:T(8,128)(2,1)S(1)} %shard_map.129.own_ref), channel_id=1, source_target_pairs={{0,2},{1,3},{2,0},{3,1},{4,6},{5,7},{6,4},{7,5},{8,10},{9,11},{10,... | collective-permute-start | bytes 393224 | tf_op jit(solution)/shard_map/ppermute | solution.py:486
  69.7 6.4 %collective-permute-start.17 = (f32[1,112,128]{2,1,0:T(8,128)S(1)}, f32[1,112,128]{2,1,0:T(8,128)S(1)}, u32[]{:S(2)}, u32[]{:S(2)}) collective-permute-start(f32[1,112,128]{2,1,0:T(8,128)S(1)} %get-tuple-element.38), channel_id=1, source_target_pairs={{0,16},{1,17},{2,18},{3,19},{4,20},{5,21},{6,22},{7,23},{8,24},{9,... | collective-permute-start | bytes 172040 | tf_op jit(solution)/shard_map/ppermute | solution.py:486
  75.4 11.9 %collective-permute-start.14 = (bf16[4,128,128]{2,1,0:T(8,128)(2,1)S(1)}, bf16[4,128,128]{2,1,0:T(8,128)(2,1)S(1)}, u32[]{:S(2)}, u32[]{:S(2)}) collective-permute-start(bf16[4,128,128]{2,1,0:T(8,128)(2,1)S(1)} %shard_map.130.own_ref), channel_id=1, source_target_pairs={{0,1},{1,0},{2,3},{3,2},{4,5},{5,4},{6,7},{7,6},{8,9},{9,8},{10,11... | collective-permute-start | bytes 393224 | tf_op jit(solution)/shard_map/ppermute | solution.py:486
  76.2 5.0 %collective-permute-start.18 = (f32[1,112,128]{2,1,0:T(8,128)S(1)}, f32[1,112,128]{2,1,0:T(8,128)S(1)}, u32[]{:S(2)}, u32[]{:S(2)}) collective-permute-start(f32[1,112,128]{2,1,0:T(8,128)S(1)} %shard_map.138.own_ref), channel_id=1, source_target_pairs={{0,1},{1,0},{2,3},{3,2},{4,5},{5,4},{6,7},{7,6},{8,9},{9,8},{10,11... | collective-permute-start | bytes 172040 | tf_op jit(solution)/shard_map/ppermute | solution.py:486
  81.1 6.2 %collective-permute-start.19 = (f32[1,112,128]{2,1,0:T(8,128)S(1)}, f32[1,112,128]{2,1,0:T(8,128)S(1)}, u32[]{:S(2)}, u32[]{:S(2)}) collective-permute-start(f32[1,112,128]{2,1,0:T(8,128)S(1)} %shard_map.139.lags_ref), channel_id=1, source_target_pairs={{0,2},{1,3},{2,0},{3,1},{4,6},{5,7},{6,4},{7,5},{8,10},{9,11},{10,... | collective-permute-start | bytes 172040 | tf_op jit(solution)/shard_map/ppermute | solution.py:486

commit v5 on v2

--- a/solution.py
+++ b/solution.py
@@ -343,14 +343,17 @@
         copy.wait()
 
 
-def rows_body(masks, recv_ref, staged_ref, *refs):
-    pieces, (give_ref, keep_ref, held, sems) = refs[:-4], refs[-4:]
+def rows_body(masks, recv_hbm, staged_ref, *refs):
+    pieces, (give_ref, keep_ref, recv_ref, held, sems) = refs[:-5], refs[-5:]
     me, half = lax.axis_index("dp"), lax.axis_index("grp") & 1
     copies = [
         pltpu.make_async_copy(piece, held.at[i], sems.at[i]) for i, piece in enumerate(pieces)
     ]
+    fetch = pltpu.make_async_copy(recv_hbm, recv_ref, sems.at[len(pieces)])
+    fetch.start()
     for copy in copies:
         copy.start()
+    fetch.wait()
     early = staged_ref.shape[0]
     many = give_ref.shape[0]
     width = many * LANES
@@ -562,10 +565,11 @@
         (received, staged, *values[early:]),
         flops=2 * n_dp * tokens * LANES * width,
         scratch=[
+            pltpu.VMEM(received.shape, BF16),
             pltpu.VMEM((n_dp - early, tokens, width), BF16),
-            pltpu.SemaphoreType.DMA((n_dp - early,)),
+            pltpu.SemaphoreType.DMA((n_dp - early + 1,)),
         ],
-        in_specs=[VMEM, VMEM] + [ANY] * (n_dp - early),
+        in_specs=[ANY, VMEM] + [ANY] * (n_dp - early),
     )
     taken = swap(given, 0, 1)
     both = call(add_body, half_shape, (), (kept, taken))

time: 87.6 us -> 87.5 us (level)
  no operation moved by 1% of the time
where the time goes in v5:
time: 87.5 us; the launch traced here: 87.2 us
  starting transfers between devices  32.2 us (37%)
  waiting for transfers between devices  31.2 us (36%)
  Pallas kernels  22.3 us (25%)
    ppermute x20, waiting for transfers between devices, swap(): return lax.ppermute(value, ('dp', 'grp'), pairs)  31.2 us
    ppermute x20, starting transfers between devices, swap(): return lax.ppermute(value, ('dp', 'grp'), pairs)  28.5 us
    pallas_call x24, Pallas kernels, call(): pl.pallas_call(body, in_specs=more.pop('in_specs', None) or [SMEM] * len(...  22.3 us
    all_to_all x1, starting transfers between devices, local_fast(): received = lax.all_to_all(hidden, 'dp', 0, 0, tiled=True)  3.69 us
  transfers between devices with their start and end apart: 21, of which 10 were waited for; matrix products, arithmetic and copies ran while one was open for 0% of the time, Pallas kernels for 25%

profile of v5, /device:TPU:0, one launch (start us, length us, event | category | flops | bytes accessed | tf_op | source)
XLA Modules:
  0.0 87.2 jit_solution(11572222544200526609)
XLA Ops:
  0.6 3.0 %collective-permute-start.5 = (bf16[192,1024]{1,0:T(8,128)(2,1)}, bf16[192,1024]{1,0:T(8,128)(2,1)}, u32[]{:S(2)}, u32[]{:S(2)}) collective-permute-start(bf16[192,1024]{1,0:T(8,128)(2,1)} %bitcast.5), channel_id=1, source_target_pairs={{0,8},{1,9},{2,10},{3,11},{4,12},{5,13},{6,14},{7,15},{8,0},{9,1},... | collective-permute-start | bytes 1179656 | tf_op jit(solution)/shard_map/ppermute | solution.py:454
  3.7 1.5 %collective-permute-start.6 = (bf16[192,1024]{1,0:T(8,128)(2,1)}, bf16[192,1024]{1,0:T(8,128)(2,1)}, u32[]{:S(2)}, u32[]{:S(2)}) collective-permute-start(bf16[192,1024]{1,0:T(8,128)(2,1)} %bitcast.6), channel_id=1, source_target_pairs={{0,16},{1,17},{2,18},{3,19},{4,20},{5,21},{6,22},{7,23},{8,24},{9,... | collective-permute-start | bytes 1179656 | tf_op jit(solution)/shard_map/ppermute | solution.py:454
  5.2 7.9 %collective-permute-done.5.refs_1_ = bf16[192,1024]{1,0:T(8,128)(2,1)} collective-permute-done((bf16[192,1024]{1,0:T(8,128)(2,1)}, bf16[192,1024]{1,0:T(8,128)(2,1)}, u32[]{:S(2)}, u32[]{:S(2)}) %collective-permute-start.5) | collective-permute-done | bytes 393248 | tf_op jit(solution)/shard_map/ppermute | solution.py:454
  13.1 1.8 %collective-permute-start.10 = (bf16[192,1024]{1,0:T(8,128)(2,1)}, bf16[192,1024]{1,0:T(8,128)(2,1)S(1)}, u32[]{:S(2)}, u32[]{:S(2)}) collective-permute-start(bf16[192,1024]{1,0:T(8,128)(2,1)} %collective-permute-done.5.refs_1_), channel_id=1, source_target_pairs={{0,16},{1,17},{2,18},{3,19},{4,20},{5,21},{6,22},{7,23},{8,24},{9,... | collective-permute-start | bytes 1179656 | tf_op jit(solution)/shard_map/ppermute | solution.py:454
  14.9 0.0 collective-permute-start.7
  14.9 0.5 collective-permute-start.8
  15.4 0.0 collective-permute-start.9
  15.4 8.2 %collective-permute-done.10.refs_0_ = bf16[192,1024]{1,0:T(8,128)(2,1)S(1)} collective-permute-done((bf16[192,1024]{1,0:T(8,128)(2,1)}, bf16[192,1024]{1,0:T(8,128)(2,1)S(1)}, u32[]{:S(2)}, u32[]{:S(2)}) %collective-permute-start.10) | collective-permute-done | bytes 393248 | tf_op jit(solution)/shard_map/ppermute | solution.py:454
  23.6 3.2 %shard_map.119 = (f32[8,6,64,128]{3,2,1,0:T(8,128)S(1)}, f32[8,6,32,128]{3,2,1,0:T(8,128)S(1)}, f32[2,1152]{1,0:T(2,128)S(1)}, f32[6,32,128]{2,1,0:T(8,128)S(1)}...) custom-call(s32[6]{0:T(128)} %len_hbm.1, s32[6]{0:T(128)} %off_hbm.1, bf16[6,32,2048]{2,1,0:T(8,128)(2,1)} %acts_hbm.1, ...), custom_call_target="tpu_custom_call" | custom-call | flops 25165824 | bytes 925744 | tf_op jit(solution)/shard_map/pallas_call | solution.py:426
  26.8 1.7 %collective-permute-start = (f32[2,1152]{1,0:T(2,128)S(1)}, f32[2,1152]{1,0:T(2,128)S(1)}, u32[]{:S(2)}, u32[]{:S(2)}) collective-permute-start(f32[2,1152]{1,0:T(2,128)S(1)} %get-tuple-element.23.own_ref), channel_id=1, source_target_pairs={{0,5},{1,4},{2,7},{3,6},{4,1},{5,0},{6,3},{7,2},{8,13},{9,12},{10,... | collective-permute-start | bytes 27656 | tf_op jit(solution)/shard_map/ppermute | solution.py:454
  28.5 1.4 %collective-permute-done.recv_ref = f32[2,1152]{1,0:T(2,128)S(1)} collective-permute-done((f32[2,1152]{1,0:T(2,128)S(1)}, f32[2,1152]{1,0:T(2,128)S(1)}, u32[]{:S(2)}, u32[]{:S(2)}) %collective-permute-start) | collective-permute-done | bytes 9248 | tf_op jit(solution)/shard_map/ppermute | solution.py:454
  29.9 2.7 %collective-permute-start.1 = (f32[2,1152]{1,0:T(2,128)S(1)}, f32[2,1152]{1,0:T(2,128)S(1)}, u32[]{:S(2)}, u32[]{:S(2)}) collective-permute-start(f32[2,1152]{1,0:T(2,128)S(1)} %shard_map.120.own_ref), channel_id=1, source_target_pairs={{0,6},{1,7},{2,4},{3,5},{4,2},{5,3},{6,0},{7,1},{8,14},{9,15},{10,... | collective-permute-start | bytes 27656 | tf_op jit(solution)/shard_map/ppermute | solution.py:454
  32.6 1.4 %collective-permute-done.1.recv_ref = f32[2,1152]{1,0:T(2,128)S(1)} collective-permute-done((f32[2,1152]{1,0:T(2,128)S(1)}, f32[2,1152]{1,0:T(2,128)S(1)}, u32[]{:S(2)}, u32[]{:S(2)}) %collective-permute-start.1) | collective-permute-done | bytes 9248 | tf_op jit(solution)/shard_map/ppermute | solution.py:454
  34.0 1.5 %collective-permute-start.2 = (f32[2,1152]{1,0:T(2,128)S(1)}, f32[2,1152]{1,0:T(2,128)S(1)}, u32[]{:S(2)}, u32[]{:S(2)}) collective-permute-start(f32[2,1152]{1,0:T(2,128)S(1)} %shard_map.121.own_ref), channel_id=1, source_target_pairs={{0,12},{1,13},{2,14},{3,15},{4,8},{5,9},{6,10},{7,11},{8,4},{9,5},... | collective-permute-start | bytes 27656 | tf_op jit(solution)/shard_map/ppermute | solution.py:454
  35.5 1.6 %collective-permute-done.2.recv_ref = f32[2,1152]{1,0:T(2,128)S(1)} collective-permute-done((f32[2,1152]{1,0:T(2,128)S(1)}, f32[2,1152]{1,0:T(2,128)S(1)}, u32[]{:S(2)}, u32[]{:S(2)}) %collective-permute-start.2) | collective-permute-done | bytes 9248 | tf_op jit(solution)/shard_map/ppermute | solution.py:454
  37.1 1.5 %collective-permute-start.3 = (f32[2,1152]{1,0:T(2,128)S(1)}, f32[2,1152]{1,0:T(2,128)S(1)}, u32[]{:S(2)}, u32[]{:S(2)}) collective-permute-start(f32[2,1152]{1,0:T(2,128)S(1)} %shard_map.122.own_ref), channel_id=1, source_target_pairs={{0,20},{1,21},{2,22},{3,23},{4,16},{5,17},{6,18},{7,19},{8,28},{9,... | collective-permute-start | bytes 27656 | tf_op jit(solution)/shard_map/ppermute | solution.py:454
  38.6 1.5 %collective-permute-done.3.recv_ref = f32[2,1152]{1,0:T(2,128)S(1)} collective-permute-done((f32[2,1152]{1,0:T(2,128)S(1)}, f32[2,1152]{1,0:T(2,128)S(1)}, u32[]{:S(2)}, u32[]{:S(2)}) %collective-permute-start.3) | collective-permute-done | bytes 9248 | tf_op jit(solution)/shard_map/ppermute | solution.py:454
  40.2 0.5 collective-permute-start.4
  40.6 0.8 collective-permute-done.4.recv_ref
  41.4 1.2 %shard_map.125.hid_ref = bf16[8,192,128]{2,1,0:T(8,128)(2,1)} custom-call(f32[2,1152]{1,0:T(2,128)S(1)} %shard_map.124.st_ref, f32[2,8,128]{2,1,0:T(8,128)S(1)} %get-tuple-element.24.gb_ref, f32[6,32,128]{2,1,0:T(8,128)S(1)} %get-tuple-element.25.ok_ref, f32[8,6,32,128]{3,2,1,0:T(8,128)S(1)} %get-tuple-element.26.cv_ref), custom_call_target="tpu_custom_call" | custom-call | bytes 902144 | tf_op jit(solution)/shard_map/pallas_call | solution.py:426
  42.6 3.7 %all-to-all-start = ((bf16[8,192,128]{2,1,0:T(8,128)(2,1)}), bf16[8,192,128]{2,1,0:T(8,128)(2,1)S(1)}, u32[]{:S(2)}, u32[]{:S(2)}) async-start(bf16[8,192,128]{2,1,0:T(8,128)(2,1)} %shard_map.125.hid_ref), calls=%async_computation | async-start | bytes 786432 | tf_op jit(solution)/shard_map/all_to_all | solution.py:531
  46.3 0.7 shard_map.132.refs_0_
  47.0 0.7 shard_map.133.refs_1_
  47.6 0.7 shard_map.134.refs_2_
  48.3 0.7 shard_map.135.refs_3_
  49.0 4.0 %shard_map.131.bk_ref = f32[8,192,128]{2,1,0:T(8,128)S(1)} custom-call(bf16[192,1024]{1,0:T(8,128)(2,1)} %bitcast.8, bf16[1024,1024]{1,0:T(8,128)(2,1)} %w_hbm.1), custom_call_target="tpu_custom_call" | custom-call | flops 402653184 | bytes 2490368 | tf_op jit(solution)/shard_map/pallas_call | solution.py:426
  53.0 0.0 copy-start.1
  53.0 3.0 %shard_map.136 = (f32[4,112,128]{2,1,0:T(8,128)}, f32[4,112,128]{2,1,0:T(8,128)S(1)}) custom-call(f32[2,1152]{1,0:T(2,128)S(1)} %shard_map.124.st_ref, f32[2,8,128]{2,1,0:T(8,128)S(1)} %get-tuple-element.24.gb_ref, f32[6,32,128]{2,1,0:T(8,128)S(1)} %get-tuple-element.25.ok_ref, f32[8,6,64,128]{3,2,1,0:T(8,128)S(1)} %get-tuple-element.29.gp_ref, ...), custom_call_target="tpu_custom_call" | custom-call | flops 25165824 | bytes 3523584 | tf_op jit(solution)/shard_map/pallas_call | solution.py:426
  56.0 0.7 copy-done.2
  56.7 0.5 collective-permute-start.15
  57.2 0.0 collective-permute-done.7.refs_3_
  57.2 0.0 collective-permute-done.8.refs_4_
  57.2 1.7 %shard_map.127.staged_ref = bf16[6,192,1024]{2,1,0:T(8,128)(2,1)S(1)} custom-call(bf16[192,1024]{1,0:T(8,128)(2,1)S(1)} %bitcast.9, bf16[192,1024]{1,0:T(8,128)(2,1)} %collective-permute-done.5.refs_1_, bf16[192,1024]{1,0:T(8,128)(2,1)} %collective-permute-done.6.refs_2_, bf16[192,1024]{1,0:T(8,128)(2,1)} %collective-permute-done.7.refs_3_, ...), custom_call_target="tpu_custom_call" | custom-call | bytes 2359296 | tf_op jit(solution)/shard_map/pallas_call | solution.py:426
  59.0 0.0 copy-start
  59.0 1.9 %shard_map.128 = (bf16[4,128,128]{2,1,0:T(8,128)(2,1)S(1)}, bf16[4,128,128]{2,1,0:T(8,128)(2,1)S(1)}) custom-call(bf16[8,192,128]{2,1,0:T(8,128)(2,1)S(1)} %all-to-all-done.recv_hbm, bf16[6,192,1024]{2,1,0:T(8,128)(2,1)S(1)} %shard_map.127.staged_ref, bf16[192,1024]{1,0:T(8,128)(2,1)S(1)} %collective-permute-done.10.refs_0_, ...), custom_call_target="tpu_custom_call" | custom-call | flops 402653184 | bytes 3538944 | tf_op jit(solution)/shard_map/pallas_call | solution.py:426
  60.9 1.6 %collective-permute-start.12 = (bf16[4,128,128]{2,1,0:T(8,128)(2,1)S(1)}, bf16[4,128,128]{2,1,0:T(8,128)(2,1)S(1)}, u32[]{:S(2)}, u32[]{:S(2)}) collective-permute-start(bf16[4,128,128]{2,1,0:T(8,128)(2,1)S(1)} %get-tuple-element.28), channel_id=1, source_target_pairs={{0,1},{1,0},{2,3},{3,2},{4,5},{5,4},{6,7},{7,6},{8,9},{9,8},{10,11... | collective-permute-start | bytes 393224 | tf_op jit(solution)/shard_map/ppermute | solution.py:454
  62.5 1.0 %shard_map.137 = (f32[2,112,128]{2,1,0:T(8,128)S(1)}, f32[2,112,128]{2,1,0:T(8,128)S(1)}) custom-call(f32[4,112,128]{2,1,0:T(8,128)S(1)} %copy-done.3, f32[4,112,128]{2,1,0:T(8,128)} %collective-permute-done.15.recv_ref), custom_call_target="tpu_custom_call" | custom-call | bytes 458752 | tf_op jit(solution)/shard_map/pallas_call | solution.py:426
  63.5 1.7 %collective-permute-start.16 = (f32[2,112,128]{2,1,0:T(8,128)S(1)}, f32[2,112,128]{2,1,0:T(8,128)S(1)}, u32[]{:S(2)}, u32[]{:S(2)}) collective-permute-start(f32[2,112,128]{2,1,0:T(8,128)S(1)} %get-tuple-element.34), channel_id=1, source_target_pairs={{0,8},{1,9},{2,10},{3,11},{4,12},{5,13},{6,14},{7,15},{8,0},{9,1},... | collective-permute-start | bytes 344072 | tf_op jit(solution)/shard_map/ppermute | solution.py:454
  65.2 1.2 %collective-permute-done.12.recv_ref = bf16[4,128,128]{2,1,0:T(8,128)(2,1)S(1)} collective-permute-done((bf16[4,128,128]{2,1,0:T(8,128)(2,1)S(1)}, bf16[4,128,128]{2,1,0:T(8,128)(2,1)S(1)}, u32[]{:S(2)}, u32[]{:S(2)}) %collective-permute-start.12) | collective-permute-done | bytes 131104 | tf_op jit(solution)/shard_map/ppermute | solution.py:454
  66.4 2.7 %collective-permute-start.13 = (bf16[4,128,128]{2,1,0:T(8,128)(2,1)S(1)}, bf16[4,128,128]{2,1,0:T(8,128)(2,1)S(1)}, u32[]{:S(2)}, u32[]{:S(2)}) collective-permute-start(bf16[4,128,128]{2,1,0:T(8,128)(2,1)S(1)} %shard_map.129.own_ref), channel_id=1, source_target_pairs={{0,2},{1,3},{2,0},{3,1},{4,6},{5,7},{6,4},{7,5},{8,10},{9,11},{10,... | collective-permute-start | bytes 393224 | tf_op jit(solution)/shard_map/ppermute | solution.py:454
  69.1 2.1 %collective-permute-start.17 = (f32[1,112,128]{2,1,0:T(8,128)S(1)}, f32[1,112,128]{2,1,0:T(8,128)S(1)}, u32[]{:S(2)}, u32[]{:S(2)}) collective-permute-start(f32[1,112,128]{2,1,0:T(8,128)S(1)} %get-tuple-element.36), channel_id=1, source_target_pairs={{0,16},{1,17},{2,18},{3,19},{4,20},{5,21},{6,22},{7,23},{8,24},{9,... | collective-permute-start | bytes 172040 | tf_op jit(solution)/shard_map/ppermute | solution.py:454
  71.2 3.6 %collective-permute-done.13.recv_ref = bf16[4,128,128]{2,1,0:T(8,128)(2,1)S(1)} collective-permute-done((bf16[4,128,128]{2,1,0:T(8,128)(2,1)S(1)}, bf16[4,128,128]{2,1,0:T(8,128)(2,1)S(1)}, u32[]{:S(2)}, u32[]{:S(2)}) %collective-permute-start.13) | collective-permute-done | bytes 131104 | tf_op jit(solution)/shard_map/ppermute | solution.py:454
  74.8 0.7 collective-permute-start.14
  75.5 1.4 %collective-permute-start.18 = (f32[1,112,128]{2,1,0:T(8,128)S(1)}, f32[1,112,128]{2,1,0:T(8,128)S(1)}, u32[]{:S(2)}, u32[]{:S(2)}) collective-permute-start(f32[1,112,128]{2,1,0:T(8,128)S(1)} %shard_map.139.own_ref), channel_id=1, source_target_pairs={{0,1},{1,0},{2,3},{3,2},{4,5},{5,4},{6,7},{7,6},{8,9},{9,8},{10,11... | collective-permute-start | bytes 172040 | tf_op jit(solution)/shard_map/ppermute | solution.py:454
  76.9 3.5 %collective-permute-done.18.recv_ref = f32[1,112,128]{2,1,0:T(8,128)S(1)} collective-permute-done((f32[1,112,128]{2,1,0:T(8,128)S(1)}, f32[1,112,128]{2,1,0:T(8,128)S(1)}, u32[]{:S(2)}, u32[]{:S(2)}) %collective-permute-start.18) | collective-permute-done | bytes 57376 | tf_op jit(solution)/shard_map/ppermute | solution.py:454
  80.5 3.1 %collective-permute-start.19 = (f32[1,112,128]{2,1,0:T(8,128)S(1)}, f32[1,112,128]{2,1,0:T(8,128)S(1)}, u32[]{:S(2)}, u32[]{:S(2)}) collective-permute-start(f32[1,112,128]{2,1,0:T(8,128)S(1)} %shard_map.140.lags_ref), channel_id=1, source_target_pairs={{0,2},{1,3},{2,0},{3,1},{4,6},{5,7},{6,4},{7,5},{8,10},{9,11},{10,... | collective-permute-start | bytes 172040 | tf_op jit(solution)/shard_map/ppermute | solution.py:454
  83.6 2.7 %shard_map.126 = bf16[6,32,1024]{2,1,0:T(8,128)(2,1)} custom-call(bf16[8,192,128]{2,1,0:T(8,128)(2,1)} %shard_map.125.hid_ref, bf16[1024,1024]{1,0:T(8,128)(2,1)S(1)} %copy-done), custom_call_target="tpu_custom_call" | custom-call | bytes 2490368 | tf_op jit(solution)/shard_map/pallas_call | solution.py:426
  86.3 0.9 shard_map.142
  (26 shorter events, 0.2 us)
Async XLA Ops:
  0.6 12.5 %collective-permute-start.5 = (bf16[192,1024]{1,0:T(8,128)(2,1)}, bf16[192,1024]{1,0:T(8,128)(2,1)}, u32[]{:S(2)}, u32[]{:S(2)}) collective-permute-start(bf16[192,1024]{1,0:T(8,128)(2,1)} %bitcast.5), channel_id=1, source_target_pairs={{0,8},{1,9},{2,10},{3,11},{4,12},{5,13},{6,14},{7,15},{8,0},{9,1},... | collective-permute-start | bytes 1179656 | tf_op jit(solution)/shard_map/ppermute | solution.py:454
  3.7 11.7 %collective-permute-start.6 = (bf16[192,1024]{1,0:T(8,128)(2,1)}, bf16[192,1024]{1,0:T(8,128)(2,1)}, u32[]{:S(2)}, u32[]{:S(2)}) collective-permute-start(bf16[192,1024]{1,0:T(8,128)(2,1)} %bitcast.6), channel_id=1, source_target_pairs={{0,16},{1,17},{2,18},{3,19},{4,20},{5,21},{6,22},{7,23},{8,24},{9,... | collective-permute-start | bytes 1179656 | tf_op jit(solution)/shard_map/ppermute | solution.py:454
  13.1 10.5 %collective-permute-start.10 = (bf16[192,1024]{1,0:T(8,128)(2,1)}, bf16[192,1024]{1,0:T(8,128)(2,1)S(1)}, u32[]{:S(2)}, u32[]{:S(2)}) collective-permute-start(bf16[192,1024]{1,0:T(8,128)(2,1)} %collective-permute-done.5.refs_1_), channel_id=1, source_target_pairs={{0,16},{1,17},{2,18},{3,19},{4,20},{5,21},{6,22},{7,23},{8,24},{9,... | collective-permute-start | bytes 1179656 | tf_op jit(solution)/shard_map/ppermute | solution.py:454
  14.9 42.3 %collective-permute-start.7 = (bf16[192,1024]{1,0:T(8,128)(2,1)}, bf16[192,1024]{1,0:T(8,128)(2,1)}, u32[]{:S(2)}, u32[]{:S(2)}) collective-permute-start(bf16[192,1024]{1,0:T(8,128)(2,1)} %bitcast.7), channel_id=1, source_target_pairs={{0,4},{1,5},{2,6},{3,7},{4,0},{5,1},{6,2},{7,3},{8,12},{9,13},{10,... | collective-permute-start | bytes 1179656 | tf_op jit(solution)/shard_map/ppermute | solution.py:454
  14.9 42.3 %collective-permute-start.8 = (bf16[192,1024]{1,0:T(8,128)(2,1)}, bf16[192,1024]{1,0:T(8,128)(2,1)}, u32[]{:S(2)}, u32[]{:S(2)}) collective-permute-start(bf16[192,1024]{1,0:T(8,128)(2,1)} %collective-permute-done.5.refs_1_), channel_id=1, source_target_pairs={{0,4},{1,5},{2,6},{3,7},{4,0},{5,1},{6,2},{7,3},{8,12},{9,13},{10,... | collective-permute-start | bytes 1179656 | tf_op jit(solution)/shard_map/ppermute | solution.py:454
  15.4 41.8 %collective-permute-start.9 = (bf16[192,1024]{1,0:T(8,128)(2,1)}, bf16[192,1024]{1,0:T(8,128)(2,1)}, u32[]{:S(2)}, u32[]{:S(2)}) collective-permute-start(bf16[192,1024]{1,0:T(8,128)(2,1)} %collective-permute-done.6.refs_2_), channel_id=1, source_target_pairs={{0,4},{1,5},{2,6},{3,7},{4,0},{5,1},{6,2},{7,3},{8,12},{9,13},{10,... | collective-permute-start | bytes 1179656 | tf_op jit(solution)/shard_map/ppermute | solution.py:454
  23.6 35.4 %collective-permute-start.11 = (bf16[192,1024]{1,0:T(8,128)(2,1)S(1)}, bf16[192,1024]{1,0:T(8,128)(2,1)}, u32[]{:S(2)}, u32[]{:S(2)}) collective-permute-start(bf16[192,1024]{1,0:T(8,128)(2,1)S(1)} %collective-permute-done.10.refs_0_), channel_id=1, source_target_pairs={{0,4},{1,5},{2,6},{3,7},{4,0},{5,1},{6,2},{7,3},{8,12},{9,13},{10,... | collective-permute-start | bytes 1179656 | tf_op jit(solution)/shard_map/ppermute | solution.py:454
  26.8 3.2 %collective-permute-start = (f32[2,1152]{1,0:T(2,128)S(1)}, f32[2,1152]{1,0:T(2,128)S(1)}, u32[]{:S(2)}, u32[]{:S(2)}) collective-permute-start(f32[2,1152]{1,0:T(2,128)S(1)} %get-tuple-element.23.own_ref), channel_id=1, source_target_pairs={{0,5},{1,4},{2,7},{3,6},{4,1},{5,0},{6,3},{7,2},{8,13},{9,12},{10,... | collective-permute-start | bytes 27656 | tf_op jit(solution)/shard_map/ppermute | solution.py:454
  29.9 4.0 %collective-permute-start.1 = (f32[2,1152]{1,0:T(2,128)S(1)}, f32[2,1152]{1,0:T(2,128)S(1)}, u32[]{:S(2)}, u32[]{:S(2)}) collective-permute-start(f32[2,1152]{1,0:T(2,128)S(1)} %shard_map.120.own_ref), channel_id=1, source_target_pairs={{0,6},{1,7},{2,4},{3,5},{4,2},{5,3},{6,0},{7,1},{8,14},{9,15},{10,... | collective-permute-start | bytes 27656 | tf_op jit(solution)/shard_map/ppermute | solution.py:454
  34.0 3.1 %collective-permute-start.2 = (f32[2,1152]{1,0:T(2,128)S(1)}, f32[2,1152]{1,0:T(2,128)S(1)}, u32[]{:S(2)}, u32[]{:S(2)}) collective-permute-start(f32[2,1152]{1,0:T(2,128)S(1)} %shard_map.121.own_ref), channel_id=1, source_target_pairs={{0,12},{1,13},{2,14},{3,15},{4,8},{5,9},{6,10},{7,11},{8,4},{9,5},... | collective-permute-start | bytes 27656 | tf_op jit(solution)/shard_map/ppermute | solution.py:454
  37.1 3.1 %collective-permute-start.3 = (f32[2,1152]{1,0:T(2,128)S(1)}, f32[2,1152]{1,0:T(2,128)S(1)}, u32[]{:S(2)}, u32[]{:S(2)}) collective-permute-start(f32[2,1152]{1,0:T(2,128)S(1)} %shard_map.122.own_ref), channel_id=1, source_target_pairs={{0,20},{1,21},{2,22},{3,23},{4,16},{5,17},{6,18},{7,19},{8,28},{9,... | collective-permute-start | bytes 27656 | tf_op jit(solution)/shard_map/ppermute | solution.py:454
  40.2 1.3 %collective-permute-start.4 = (f32[2,1152]{1,0:T(2,128)S(1)}, f32[2,1152]{1,0:T(2,128)S(1)}, u32[]{:S(2)}, u32[]{:S(2)}) collective-permute-start(f32[2,1152]{1,0:T(2,128)S(1)} %shard_map.123.own_ref), channel_id=1, source_target_pairs={{0,4},{1,5},{2,6},{3,7},{4,0},{5,1},{6,2},{7,3},{8,12},{9,13},{10,... | collective-permute-start | bytes 27656 | tf_op jit(solution)/shard_map/ppermute | solution.py:454
  42.6 16.3 %all-to-all-start = ((bf16[8,192,128]{2,1,0:T(8,128)(2,1)}), bf16[8,192,128]{2,1,0:T(8,128)(2,1)S(1)}, u32[]{:S(2)}, u32[]{:S(2)}) async-start(bf16[8,192,128]{2,1,0:T(8,128)(2,1)} %shard_map.125.hid_ref), calls=%async_computation | async-start | bytes 786432 | tf_op jit(solution)/shard_map/all_to_all | solution.py:531
  53.0 4.3 %copy-start.1 = (bf16[6,32,1024]{2,1,0:T(8,128)(2,1)S(1)}, bf16[6,32,1024]{2,1,0:T(8,128)(2,1)}, u32[]{:S(2)}) copy-start(bf16[6,32,1024]{2,1,0:T(8,128)(2,1)} %param.9) | copy-start | bytes 1179652
  56.0 0.7 copy-start.2
  56.7 5.8 %collective-permute-start.15 = (f32[4,112,128]{2,1,0:T(8,128)}, f32[4,112,128]{2,1,0:T(8,128)}, u32[]{:S(2)}, u32[]{:S(2)}) collective-permute-start(f32[4,112,128]{2,1,0:T(8,128)} %get-tuple-element.32), channel_id=1, source_target_pairs={{0,4},{1,5},{2,6},{3,7},{4,0},{5,1},{6,2},{7,3},{8,12},{9,13},{10,... | collective-permute-start | bytes 688136 | tf_op jit(solution)/shard_map/ppermute | solution.py:454
  59.0 3.6 %copy-start.3 = (f32[4,112,128]{2,1,0:T(8,128)S(1)}, f32[4,112,128]{2,1,0:T(8,128)}, u32[]{:S(2)}) copy-start(f32[4,112,128]{2,1,0:T(8,128)} %copy-done.2) | copy-start | bytes 688132
  59.0 24.6 %copy-start = (bf16[1024,1024]{1,0:T(8,128)(2,1)S(1)}, bf16[1024,1024]{1,0:T(8,128)(2,1)}, u32[]{:S(2)}) copy-start(bf16[1024,1024]{1,0:T(8,128)(2,1)} %w_hbm.1) | copy-start | bytes 6291460
  60.9 5.5 %collective-permute-start.12 = (bf16[4,128,128]{2,1,0:T(8,128)(2,1)S(1)}, bf16[4,128,128]{2,1,0:T(8,128)(2,1)S(1)}, u32[]{:S(2)}, u32[]{:S(2)}) collective-permute-start(bf16[4,128,128]{2,1,0:T(8,128)(2,1)S(1)} %get-tuple-element.28), channel_id=1, source_target_pairs={{0,1},{1,0},{2,3},{3,2},{4,5},{5,4},{6,7},{7,6},{8,9},{9,8},{10,11... | collective-permute-start | bytes 393224 | tf_op jit(solution)/shard_map/ppermute | solution.py:454
  63.5 5.6 %collective-permute-start.16 = (f32[2,112,128]{2,1,0:T(8,128)S(1)}, f32[2,112,128]{2,1,0:T(8,128)S(1)}, u32[]{:S(2)}, u32[]{:S(2)}) collective-permute-start(f32[2,112,128]{2,1,0:T(8,128)S(1)} %get-tuple-element.34), channel_id=1, source_target_pairs={{0,8},{1,9},{2,10},{3,11},{4,12},{5,13},{6,14},{7,15},{8,0},{9,1},... | collective-permute-start | bytes 344072 | tf_op jit(solution)/shard_map/ppermute | solution.py:454
  66.4 8.3 %collective-permute-start.13 = (bf16[4,128,128]{2,1,0:T(8,128)(2,1)S(1)}, bf16[4,128,128]{2,1,0:T(8,128)(2,1)S(1)}, u32[]{:S(2)}, u32[]{:S(2)}) collective-permute-start(bf16[4,128,128]{2,1,0:T(8,128)(2,1)S(1)} %shard_map.129.own_ref), channel_id=1, source_target_pairs={{0,2},{1,3},{2,0},{3,1},{4,6},{5,7},{6,4},{7,5},{8,10},{9,11},{10,... | collective-permute-start | bytes 393224 | tf_op jit(solution)/shard_map/ppermute | solution.py:454
  69.1 6.4 %collective-permute-start.17 = (f32[1,112,128]{2,1,0:T(8,128)S(1)}, f32[1,112,128]{2,1,0:T(8,128)S(1)}, u32[]{:S(2)}, u32[]{:S(2)}) collective-permute-start(f32[1,112,128]{2,1,0:T(8,128)S(1)} %get-tuple-element.36), channel_id=1, source_target_pairs={{0,16},{1,17},{2,18},{3,19},{4,20},{5,21},{6,22},{7,23},{8,24},{9,... | collective-permute-start | bytes 172040 | tf_op jit(solution)/shard_map/ppermute | solution.py:454
  74.8 11.5 %collective-permute-start.14 = (bf16[4,128,128]{2,1,0:T(8,128)(2,1)S(1)}, bf16[4,128,128]{2,1,0:T(8,128)(2,1)S(1)}, u32[]{:S(2)}, u32[]{:S(2)}) collective-permute-start(bf16[4,128,128]{2,1,0:T(8,128)(2,1)S(1)} %shard_map.130.own_ref), channel_id=1, source_target_pairs={{0,1},{1,0},{2,3},{3,2},{4,5},{5,4},{6,7},{7,6},{8,9},{9,8},{10,11... | collective-permute-start | bytes 393224 | tf_op jit(solution)/shard_map/ppermute | solution.py:454
  75.5 5.0 %collective-permute-start.18 = (f32[1,112,128]{2,1,0:T(8,128)S(1)}, f32[1,112,128]{2,1,0:T(8,128)S(1)}, u32[]{:S(2)}, u32[]{:S(2)}) collective-permute-start(f32[1,112,128]{2,1,0:T(8,128)S(1)} %shard_map.139.own_ref), channel_id=1, source_target_pairs={{0,1},{1,0},{2,3},{3,2},{4,5},{5,4},{6,7},{7,6},{8,9},{9,8},{10,11... | collective-permute-start | bytes 172040 | tf_op jit(solution)/shard_map/ppermute | solution.py:454
  80.5 5.8 %collective-permute-start.19 = (f32[1,112,128]{2,1,0:T(8,128)S(1)}, f32[1,112,128]{2,1,0:T(8,128)S(1)}, u32[]{:S(2)}, u32[]{:S(2)}) collective-permute-start(f32[1,112,128]{2,1,0:T(8,128)S(1)} %shard_map.140.lags_ref), channel_id=1, source_target_pairs={{0,2},{1,3},{2,0},{3,1},{4,6},{5,7},{6,4},{7,5},{8,10},{9,11},{10,... | collective-permute-start | bytes 172040 | tf_op jit(solution)/shard_map/ppermute | solution.py:454

commit v6 on v5

--- a/solution.py
+++ b/solution.py
@@ -255,8 +255,11 @@
     return count, mean, inv
 
 
-def hidden_body(st_ref, gb_ref, ok_ref, cv_ref, hid_ref):
+def hidden_body(st_ref, gb_ref, ok_ref, cv_ref, hid_hbm, hid_ref, sems):
     blocks, slots, frames, _ = cv_ref.shape
+
+    def put(block):
+        return pltpu.make_async_copy(hid_ref.at[block], hid_hbm.at[block], sems.at[block])
 
     def one(block, carry):
         _, mean, inv = scale_of(st_ref, block)
@@ -266,13 +269,23 @@
             shifted = gain * ((cv_ref[block, slot] - mean) * inv) + shift
             hidden = shifted * jax.nn.sigmoid(shifted) * valid
             hid_ref[block, slot * frames : (slot + 1) * frames, :] = hidden.astype(BF16)
+        put(block).start()
         return carry
 
     lax.fori_loop(0, blocks, one, 0)
-
-
-def slope_body(st_ref, gb_ref, ok_ref, gp_ref, cv_ref, bk_ref, *refs):
-    aux_refs, (give_ref, keep_ref, sl_ref) = refs[:-3], refs[-3:]
+    for block in range(blocks):
+        put(block).wait()
+
+
+def slope_body(c_hbm, w_hbm, st_ref, gb_ref, ok_ref, gp_ref, cv_ref, low_ref, *refs):
+    aux_refs, (give_ref, keep_ref, sl_ref, high_ref, c_ref, w_ref, sems) = refs[:-7], refs[-7:]
+    many = high_ref.shape[0]
+    copies = [pltpu.make_async_copy(c_hbm, c_ref, sems.at[many])]
+    for block in range(many):
+        rows, source = pl.ds(block * LANES, LANES), pl.ds((many + block) * LANES, LANES)
+        copies.append(pltpu.make_async_copy(w_hbm.at[source], w_ref.at[rows], sems.at[block]))
+    for copy in copies:
+        copy.start()
     blocks, slots, frames, _ = cv_ref.shape
     taps = aux_refs[0].shape[2]
     last = 3 * taps
@@ -280,6 +293,7 @@
 
     def one(i, aux_ref, odd, q_ref):
         block = 2 * i + odd
+        bk_ref, at = (low_ref, block) if 2 * i < many else (high_ref, block - many)
         _, mean, inv = scale_of(st_ref, block)
         gain, shift = gb_ref[0, pl.ds(block, 1), :], gb_ref[1, pl.ds(block, 1), :]
         first = second = jnp.zeros((8, LANES), F32)
@@ -287,7 +301,7 @@
             normed = (cv_ref[block, slot] - mean) * inv
             shifted = gain * normed + shift
             sig = jax.nn.sigmoid(shifted)
-            back = bk_ref[block, slot * frames : (slot + 1) * frames, :]
+            back = bk_ref[at, slot * frames : (slot + 1) * frames, :]
             slope = back * sig * (1.0 + shifted * (1.0 - sig)) * ok_ref[slot]
             sl_ref[slot] = slope
             first, second = first + fold(slope), second + fold(slope * normed)
@@ -302,6 +316,14 @@
         keep_ref[0, pl.ds(last + blocks + block, 1), :] = row_sum(second)
 
     for i, aux_ref in enumerate(aux_refs):
+        if 2 * i == many:
+            for copy in copies:
+                copy.wait()
+            for block in range(many):
+                rows = w_ref[block * LANES : (block + 1) * LANES, :]
+                high_ref[block] = lax.dot_general(
+                    c_ref[...], rows, (((1,), (1,)), ((), ())), preferred_element_type=F32
+                )
         one(i, aux_ref, 1 - bit, give_ref)
         one(i, aux_ref, bit, keep_ref)
     for i in range(len(aux_refs)):
@@ -343,11 +365,16 @@
         copy.wait()
 
 
-def rows_body(masks, recv_hbm, staged_ref, *refs):
-    pieces, (give_ref, keep_ref, recv_ref, held, sems) = refs[:-5], refs[-5:]
+def rows_body(masks, flip, recv_hbm, staged_ref, *refs):
+    pieces, (out_ref, recv_ref, held, sems) = refs[:-4], refs[-4:]
     me, half = lax.axis_index("dp"), lax.axis_index("grp") & 1
+    half = 1 - half if flip else half
+    many = out_ref.shape[0]
+    width = many * LANES
+    cols = pl.ds(pl.multiple_of(half * width, width), width)
     copies = [
-        pltpu.make_async_copy(piece, held.at[i], sems.at[i]) for i, piece in enumerate(pieces)
+        pltpu.make_async_copy(piece.at[:, cols], held.at[i], sems.at[i])
+        for i, piece in enumerate(pieces)
     ]
     fetch = pltpu.make_async_copy(recv_hbm, recv_ref, sems.at[len(pieces)])
     fetch.start()
@@ -355,24 +382,18 @@
         copy.start()
     fetch.wait()
     early = staged_ref.shape[0]
-    many = give_ref.shape[0]
-    width = many * LANES
-    give = pl.ds(pl.multiple_of((1 - half) * width, width), width)
-    keep = pl.ds(pl.multiple_of(half * width, width), width)
-    totals = [None, None]
+    total = None
     for i, mask in enumerate(masks):
         left = recv_ref[jnp.bitwise_xor(me, mask)]
         if i >= early:
             copies[i - early].wait()
-        for j, cols in enumerate((give, keep)):
-            right = staged_ref[i, :, cols] if i < early else held[i - early, :, cols]
-            term = lax.dot_general(
-                left, right, (((0,), (0,)), ((), ())), preferred_element_type=F32
-            )
-            totals[j] = term if totals[j] is None else totals[j] + term
-    for total, ref in zip(totals, (give_ref, keep_ref)):
-        for block in range(many):
-            ref[block] = total[:, block * LANES : (block + 1) * LANES].astype(BF16)
+        right = staged_ref[i, :, cols] if i < early else held[i - early]
+        term = lax.dot_general(
+            left, right, (((0,), (0,)), ((), ())), preferred_element_type=F32
+        )
+        total = term if total is None else total + term
+    for block in range(many):
+        out_ref[block] = total[:, block * LANES : (block + 1) * LANES].astype(BF16)
 
 
 def plus_body(own_ref, recv_ref, out_ref):
@@ -426,7 +447,7 @@
     return pl.pallas_call(
         body,
         in_specs=more.pop("in_specs", None) or [SMEM] * len(scalars) + [VMEM] * len(args),
-        out_specs=[VMEM] * len(shapes) if many else VMEM,
+        out_specs=more.pop("out_specs", None) or ([VMEM] * len(shapes) if many else VMEM),
         out_shape=shapes,
         scratch_shapes=scratch,
         compiler_params=pltpu.CompilerParams(vmem_limit_bytes=mib << 20),
@@ -500,14 +521,14 @@
 
     back = call(
         back_body,
-        shape((blocks, tokens, LANES), F32),
+        shape((blocks // 2, tokens, LANES), F32),
         (),
         (in_hbm(flat_cotan), in_hbm(w_out)),
-        flops=2 * tokens * width * width,
+        flops=tokens * width * width,
         scratch=[
             pltpu.VMEM(flat_cotan.shape, BF16),
-            pltpu.VMEM(w_out.shape, BF16),
-            pltpu.SemaphoreType.DMA((blocks + 1,)),
+            pltpu.VMEM((width // 2, width), BF16),
+            pltpu.SemaphoreType.DMA((blocks // 2 + 1,)),
         ],
         in_specs=[HBM] * 2,
     )
@@ -526,16 +547,31 @@
     ]
 
     hidden = call(
-        hidden_body, shape((blocks, tokens, LANES), BF16), (), (stats, gains, valid, conv_out)
+        hidden_body,
+        pltpu.HBM((blocks, tokens, LANES), BF16),
+        (),
+        (stats, gains, valid, conv_out),
+        scratch=[
+            pltpu.VMEM((blocks, tokens, LANES), BF16),
+            pltpu.SemaphoreType.DMA((blocks,)),
+        ],
+        out_specs=HBM,
     )
     received = lax.all_to_all(hidden, "dp", 0, 0, tiled=True)
     give, lags = call(
         slope_body,
         [shape((parts, n_q, LANES), F32)] * 2,
         (),
-        (stats, gains, valid, gated, conv_out, back, *aux),
-        flops=4 * taps * tokens * width,
-        scratch=[pltpu.VMEM((slots, frames, LANES), F32)],
+        (in_hbm(flat_cotan), in_hbm(w_out), stats, gains, valid, gated, conv_out, back, *aux),
+        flops=4 * taps * tokens * width + tokens * width * width,
+        scratch=[
+            pltpu.VMEM((slots, frames, LANES), F32),
+            pltpu.VMEM((blocks // 2, tokens, LANES), F32),
+            pltpu.VMEM(flat_cotan.shape, BF16),
+            pltpu.VMEM((width // 2, width), BF16),
+            pltpu.SemaphoreType.DMA((blocks // 2 + 1,)),
+        ],
+        in_specs=[HBM] * 2 + [VMEM] * (6 + parts),
     )
     for level in range(1, len(dp_bits)):
         came = swap(give, dp_bits[level - 1], 0)
@@ -558,20 +594,25 @@
         scratch=[pltpu.SemaphoreType.DMA((early,))],
         in_specs=[ANY] * early,
     )
-    given, kept = call(
-        functools.partial(rows_body, masks),
-        [half_shape] * 2,
-        (),
-        (received, staged, *values[early:]),
-        flops=2 * n_dp * tokens * LANES * width,
-        scratch=[
-            pltpu.VMEM(received.shape, BF16),
-            pltpu.VMEM((n_dp - early, tokens, width), BF16),
-            pltpu.SemaphoreType.DMA((n_dp - early + 1,)),
-        ],
-        in_specs=[ANY, VMEM] + [ANY] * (n_dp - early),
-    )
+
+    def rows_of(flip):
+        return call(
+            functools.partial(rows_body, masks, flip),
+            half_shape,
+            (),
+            (received, staged, *values[early:]),
+            flops=n_dp * tokens * LANES * width,
+            scratch=[
+                pltpu.VMEM(received.shape, BF16),
+                pltpu.VMEM((n_dp - early, tokens, width // 2), BF16),
+                pltpu.SemaphoreType.DMA((n_dp - early + 1,)),
+            ],
+            in_specs=[ANY, VMEM] + [ANY] * (n_dp - early),
+        )
+
+    given = rows_of(True)
     taken = swap(given, 0, 1)
+    kept = rows_of(False)
     both = call(add_body, half_shape, (), (kept, taken))
     for mask in grp_bits[1:]:
         other = swap(both, 0, mask)

time: 87.5 us -> 87.8 us (level)
  waiting for transfers between devices: 31.2 us -> 34.7 us
  starting transfers between devices: 32.2 us -> 29.8 us
  Pallas kernels: 22.3 us -> 21.4 us
    ppermute x20, waiting for transfers between devices: 31.2 us -> 34.7 us  [swap(): return lax.ppermute(value, ('dp', 'grp'), pairs)]
    ppermute x20, starting transfers between devices: 28.5 us -> 26.1 us  [swap(): return lax.ppermute(value, ('dp', 'grp'), pairs)]
    pallas_call x24 -> x25, Pallas kernels: 22.3 us -> 21.4 us  [call(): pl.pallas_call(body, in_specs=more.pop('in_specs', None) or [SMEM] * len(...]
  transfers between devices with their start and end apart: 21 -> 21, of which waited for: 10 -> 10; matrix products, arithmetic and copies ran while one was open for 0% -> 0% of each run, Pallas kernels for 25% -> 23%
where the time goes in v6:
time: 87.8 us; the launch traced here: 87.5 us
  waiting for transfers between devices  34.7 us (40%)
  starting transfers between devices  29.8 us (34%)
  Pallas kernels  21.4 us (24%)
    ppermute x20, waiting for transfers between devices, swap(): return lax.ppermute(value, ('dp', 'grp'), pairs)  34.7 us
    ppermute x20, starting transfers between devices, swap(): return lax.ppermute(value, ('dp', 'grp'), pairs)  26.1 us
    pallas_call x25, Pallas kernels, call(): pl.pallas_call(body, in_specs=more.pop('in_specs', None) or [SMEM] * len(...  21.4 us
    all_to_all x1, starting transfers between devices, local_fast(): received = lax.all_to_all(hidden, 'dp', 0, 0, tiled=True)  3.7 us
  transfers between devices with their start and end apart: 21, of which 10 were waited for; matrix products, arithmetic and copies ran while one was open for 0% of the time, Pallas kernels for 23%

profile of v6, /device:TPU:0, one launch (start us, length us, event | category | flops | bytes accessed | tf_op | source)
XLA Modules:
  0.0 87.5 jit_solution(5933815603056416753)
XLA Ops:
  0.6 3.0 %collective-permute-start.5 = (bf16[192,1024]{1,0:T(8,128)(2,1)}, bf16[192,1024]{1,0:T(8,128)(2,1)}, u32[]{:S(2)}, u32[]{:S(2)}) collective-permute-start(bf16[192,1024]{1,0:T(8,128)(2,1)} %bitcast.5), channel_id=1, source_target_pairs={{0,8},{1,9},{2,10},{3,11},{4,12},{5,13},{6,14},{7,15},{8,0},{9,1},... | collective-permute-start | bytes 1179656 | tf_op jit(solution)/shard_map/ppermute | solution.py:475
  3.7 1.5 %collective-permute-start.6 = (bf16[192,1024]{1,0:T(8,128)(2,1)}, bf16[192,1024]{1,0:T(8,128)(2,1)}, u32[]{:S(2)}, u32[]{:S(2)}) collective-permute-start(bf16[192,1024]{1,0:T(8,128)(2,1)} %bitcast.6), channel_id=1, source_target_pairs={{0,16},{1,17},{2,18},{3,19},{4,20},{5,21},{6,22},{7,23},{8,24},{9,... | collective-permute-start | bytes 1179656 | tf_op jit(solution)/shard_map/ppermute | solution.py:475
  5.2 7.9 %collective-permute-done.5.refs_1_ = bf16[192,1024]{1,0:T(8,128)(2,1)} collective-permute-done((bf16[192,1024]{1,0:T(8,128)(2,1)}, bf16[192,1024]{1,0:T(8,128)(2,1)}, u32[]{:S(2)}, u32[]{:S(2)}) %collective-permute-start.5) | collective-permute-done | bytes 393248 | tf_op jit(solution)/shard_map/ppermute | solution.py:475
  13.1 1.8 %collective-permute-start.10 = (bf16[192,1024]{1,0:T(8,128)(2,1)}, bf16[192,1024]{1,0:T(8,128)(2,1)S(1)}, u32[]{:S(2)}, u32[]{:S(2)}) collective-permute-start(bf16[192,1024]{1,0:T(8,128)(2,1)} %collective-permute-done.5.refs_1_), channel_id=1, source_target_pairs={{0,16},{1,17},{2,18},{3,19},{4,20},{5,21},{6,22},{7,23},{8,24},{9,... | collective-permute-start | bytes 1179656 | tf_op jit(solution)/shard_map/ppermute | solution.py:475
  14.9 0.0 collective-permute-start.7
  14.9 0.5 collective-permute-start.8
  15.4 0.0 collective-permute-start.9
  15.4 8.2 %collective-permute-done.10.refs_0_ = bf16[192,1024]{1,0:T(8,128)(2,1)S(1)} collective-permute-done((bf16[192,1024]{1,0:T(8,128)(2,1)}, bf16[192,1024]{1,0:T(8,128)(2,1)S(1)}, u32[]{:S(2)}, u32[]{:S(2)}) %collective-permute-start.10) | collective-permute-done | bytes 393248 | tf_op jit(solution)/shard_map/ppermute | solution.py:475
  23.6 3.2 %shard_map.119 = (f32[8,6,64,128]{3,2,1,0:T(8,128)S(1)}, f32[8,6,32,128]{3,2,1,0:T(8,128)S(1)}, f32[2,1152]{1,0:T(2,128)S(1)}, f32[6,32,128]{2,1,0:T(8,128)S(1)}...) custom-call(s32[6]{0:T(128)} %len_hbm.1, s32[6]{0:T(128)} %off_hbm.1, bf16[6,32,2048]{2,1,0:T(8,128)(2,1)} %acts_hbm.1, ...), custom_call_target="tpu_custom_call" | custom-call | flops 25165824 | bytes 925744 | tf_op jit(solution)/shard_map/pallas_call | solution.py:447
  26.8 1.7 %collective-permute-start = (f32[2,1152]{1,0:T(2,128)S(1)}, f32[2,1152]{1,0:T(2,128)S(1)}, u32[]{:S(2)}, u32[]{:S(2)}) collective-permute-start(f32[2,1152]{1,0:T(2,128)S(1)} %get-tuple-element.21.own_ref), channel_id=1, source_target_pairs={{0,5},{1,4},{2,7},{3,6},{4,1},{5,0},{6,3},{7,2},{8,13},{9,12},{10,... | collective-permute-start | bytes 27656 | tf_op jit(solution)/shard_map/ppermute | solution.py:475
  28.5 1.4 %collective-permute-done.recv_ref = f32[2,1152]{1,0:T(2,128)S(1)} collective-permute-done((f32[2,1152]{1,0:T(2,128)S(1)}, f32[2,1152]{1,0:T(2,128)S(1)}, u32[]{:S(2)}, u32[]{:S(2)}) %collective-permute-start) | collective-permute-done | bytes 9248 | tf_op jit(solution)/shard_map/ppermute | solution.py:475
  29.9 2.7 %collective-permute-start.1 = (f32[2,1152]{1,0:T(2,128)S(1)}, f32[2,1152]{1,0:T(2,128)S(1)}, u32[]{:S(2)}, u32[]{:S(2)}) collective-permute-start(f32[2,1152]{1,0:T(2,128)S(1)} %shard_map.120.own_ref), channel_id=1, source_target_pairs={{0,6},{1,7},{2,4},{3,5},{4,2},{5,3},{6,0},{7,1},{8,14},{9,15},{10,... | collective-permute-start | bytes 27656 | tf_op jit(solution)/shard_map/ppermute | solution.py:475
  32.6 1.4 %collective-permute-done.1.recv_ref = f32[2,1152]{1,0:T(2,128)S(1)} collective-permute-done((f32[2,1152]{1,0:T(2,128)S(1)}, f32[2,1152]{1,0:T(2,128)S(1)}, u32[]{:S(2)}, u32[]{:S(2)}) %collective-permute-start.1) | collective-permute-done | bytes 9248 | tf_op jit(solution)/shard_map/ppermute | solution.py:475
  34.0 1.5 %collective-permute-start.2 = (f32[2,1152]{1,0:T(2,128)S(1)}, f32[2,1152]{1,0:T(2,128)S(1)}, u32[]{:S(2)}, u32[]{:S(2)}) collective-permute-start(f32[2,1152]{1,0:T(2,128)S(1)} %shard_map.121.own_ref), channel_id=1, source_target_pairs={{0,12},{1,13},{2,14},{3,15},{4,8},{5,9},{6,10},{7,11},{8,4},{9,5},... | collective-permute-start | bytes 27656 | tf_op jit(solution)/shard_map/ppermute | solution.py:475
  35.5 1.6 %collective-permute-done.2.recv_ref = f32[2,1152]{1,0:T(2,128)S(1)} collective-permute-done((f32[2,1152]{1,0:T(2,128)S(1)}, f32[2,1152]{1,0:T(2,128)S(1)}, u32[]{:S(2)}, u32[]{:S(2)}) %collective-permute-start.2) | collective-permute-done | bytes 9248 | tf_op jit(solution)/shard_map/ppermute | solution.py:475
  37.1 1.5 %collective-permute-start.3 = (f32[2,1152]{1,0:T(2,128)S(1)}, f32[2,1152]{1,0:T(2,128)S(1)}, u32[]{:S(2)}, u32[]{:S(2)}) collective-permute-start(f32[2,1152]{1,0:T(2,128)S(1)} %shard_map.122.own_ref), channel_id=1, source_target_pairs={{0,20},{1,21},{2,22},{3,23},{4,16},{5,17},{6,18},{7,19},{8,28},{9,... | collective-permute-start | bytes 27656 | tf_op jit(solution)/shard_map/ppermute | solution.py:475
  38.6 1.5 %collective-permute-done.3.recv_ref = f32[2,1152]{1,0:T(2,128)S(1)} collective-permute-done((f32[2,1152]{1,0:T(2,128)S(1)}, f32[2,1152]{1,0:T(2,128)S(1)}, u32[]{:S(2)}, u32[]{:S(2)}) %collective-permute-start.3) | collective-permute-done | bytes 9248 | tf_op jit(solution)/shard_map/ppermute | solution.py:475
  40.2 0.5 collective-permute-start.4
  40.6 0.8 collective-permute-done.4.recv_ref
  41.4 1.1 %shard_map.125.hid_ref = bf16[8,192,128]{2,1,0:T(8,128)(2,1)} custom-call(f32[2,1152]{1,0:T(2,128)S(1)} %shard_map.124.st_ref, f32[2,8,128]{2,1,0:T(8,128)S(1)} %get-tuple-element.22.gb_ref, f32[6,32,128]{2,1,0:T(8,128)S(1)} %get-tuple-element.23.ok_ref, f32[8,6,32,128]{3,2,1,0:T(8,128)S(1)} %get-tuple-element.24.cv_ref), custom_call_target="tpu_custom_call" | custom-call | bytes 902144 | tf_op jit(solution)/shard_map/pallas_call | solution.py:447
  42.6 3.7 %all-to-all-start = ((bf16[8,192,128]{2,1,0:T(8,128)(2,1)}), bf16[8,192,128]{2,1,0:T(8,128)(2,1)S(1)}, u32[]{:S(2)}, u32[]{:S(2)}) async-start(bf16[8,192,128]{2,1,0:T(8,128)(2,1)} %shard_map.125.hid_ref), calls=%async_computation | async-start | bytes 786432 | tf_op jit(solution)/shard_map/all_to_all | solution.py:560
  46.3 0.7 shard_map.136.refs_3_
  46.9 0.7 shard_map.135.refs_2_
  47.6 0.7 shard_map.134.refs_1_
  48.3 0.7 shard_map.133.refs_0_
  49.0 2.5 %shard_map.132.low_ref = f32[4,192,128]{2,1,0:T(8,128)S(1)} custom-call(bf16[192,1024]{1,0:T(8,128)(2,1)} %bitcast.8, bf16[1024,1024]{1,0:T(8,128)(2,1)} %w_hbm.3), custom_call_target="tpu_custom_call" | custom-call | flops 201326592 | bytes 2490368 | tf_op jit(solution)/shard_map/pallas_call | solution.py:447
  51.5 0.0 copy-start.1
  51.5 3.8 %shard_map.137 = (f32[4,112,128]{2,1,0:T(8,128)}, f32[4,112,128]{2,1,0:T(8,128)S(1)}) custom-call(bf16[192,1024]{1,0:T(8,128)(2,1)} %bitcast.9, bf16[1024,1024]{1,0:T(8,128)(2,1)} %w_hbm.3, f32[2,1152]{1,0:T(2,128)S(1)} %shard_map.124.st_ref, f32[2,8,128]{2,1,0:T(8,128)S(1)} %get-tuple-element.22.gb_ref, f32[6,32,128]{2,1,0:T(8,128)S(1)} %get-tuple-element.23.ok_ref, ...), custom_call_target="tpu_custom_call" | custom-call | flops 226492416 | bytes 5620736 | tf_op jit(solution)/shard_map/pallas_call | solution.py:447
  55.3 0.7 copy-done.3
  56.0 0.5 collective-permute-start.15
  56.5 1.7 %shard_map.127.staged_ref = bf16[6,192,1024]{2,1,0:T(8,128)(2,1)S(1)} custom-call(bf16[192,1024]{1,0:T(8,128)(2,1)S(1)} %bitcast.10, bf16[192,1024]{1,0:T(8,128)(2,1)} %collective-permute-done.5.refs_1_, bf16[192,1024]{1,0:T(8,128)(2,1)} %collective-permute-done.6.refs_2_, bf16[192,1024]{1,0:T(8,128)(2,1)} %collective-permute-done.7.refs_3_, ...), custom_call_target="tpu_custom_call" | custom-call | bytes 2359296 | tf_op jit(solution)/shard_map/pallas_call | solution.py:447
  58.2 1.4 %shard_map.129 = bf16[4,128,128]{2,1,0:T(8,128)(2,1)S(1)} custom-call(bf16[8,192,128]{2,1,0:T(8,128)(2,1)S(1)} %all-to-all-done.recv_hbm, bf16[6,192,1024]{2,1,0:T(8,128)(2,1)S(1)} %shard_map.127.staged_ref, bf16[192,1024]{1,0:T(8,128)(2,1)S(1)} %collective-permute-done.10.refs_0_, bf16[192,1024]{1,0:T(8,128)(2,1)} %collective-permute-done.11.refs_1_), custom_call_target="tpu_custom_call" | custom-call | flops 201326592 | bytes 3538944 | tf_op jit(solution)/shard_map/pallas_call | solution.py:447
  59.6 1.6 %collective-permute-start.12 = (bf16[4,128,128]{2,1,0:T(8,128)(2,1)S(1)}, bf16[4,128,128]{2,1,0:T(8,128)(2,1)S(1)}, u32[]{:S(2)}, u32[]{:S(2)}) collective-permute-start(bf16[4,128,128]{2,1,0:T(8,128)(2,1)S(1)} %shard_map.129), channel_id=1, source_target_pairs={{0,1},{1,0},{2,3},{3,2},{4,5},{5,4},{6,7},{7,6},{8,9},{9,8},{10,11... | collective-permute-start | bytes 393224 | tf_op jit(solution)/shard_map/ppermute | solution.py:475
  61.3 1.0 %shard_map.138 = (f32[2,112,128]{2,1,0:T(8,128)S(1)}, f32[2,112,128]{2,1,0:T(8,128)S(1)}) custom-call(f32[4,112,128]{2,1,0:T(8,128)S(1)} %copy-done.4, f32[4,112,128]{2,1,0:T(8,128)} %collective-permute-done.15.recv_ref), custom_call_target="tpu_custom_call" | custom-call | bytes 458752 | tf_op jit(solution)/shard_map/pallas_call | solution.py:447
  62.3 0.0 copy-start
  62.3 0.0 copy-start.2
  62.3 1.7 %collective-permute-start.16 = (f32[2,112,128]{2,1,0:T(8,128)S(1)}, f32[2,112,128]{2,1,0:T(8,128)S(1)}, u32[]{:S(2)}, u32[]{:S(2)}) collective-permute-start(f32[2,112,128]{2,1,0:T(8,128)S(1)} %get-tuple-element.30), channel_id=1, source_target_pairs={{0,8},{1,9},{2,10},{3,11},{4,12},{5,13},{6,14},{7,15},{8,0},{9,1},... | collective-permute-start | bytes 344072 | tf_op jit(solution)/shard_map/ppermute | solution.py:475
  64.0 1.4 %shard_map.128.own_ref = bf16[4,128,128]{2,1,0:T(8,128)(2,1)S(1)} custom-call(bf16[8,192,128]{2,1,0:T(8,128)(2,1)S(1)} %all-to-all-done.recv_hbm, bf16[6,192,1024]{2,1,0:T(8,128)(2,1)S(1)} %shard_map.127.staged_ref, bf16[192,1024]{1,0:T(8,128)(2,1)S(1)} %collective-permute-done.10.refs_0_, bf16[192,1024]{1,0:T(8,128)(2,1)} %collective-permute-done.11.refs_1_), custom_call_target="tpu_custom_call" | custom-call | flops 201326592 | bytes 3538944 | tf_op jit(solution)/shard_map/pallas_call | solution.py:447
  65.4 2.7 %collective-permute-start.13 = (bf16[4,128,128]{2,1,0:T(8,128)(2,1)S(1)}, bf16[4,128,128]{2,1,0:T(8,128)(2,1)S(1)}, u32[]{:S(2)}, u32[]{:S(2)}) collective-permute-start(bf16[4,128,128]{2,1,0:T(8,128)(2,1)S(1)} %shard_map.130.own_ref), channel_id=1, source_target_pairs={{0,2},{1,3},{2,0},{3,1},{4,6},{5,7},{6,4},{7,5},{8,10},{9,11},{10,... | collective-permute-start | bytes 393224 | tf_op jit(solution)/shard_map/ppermute | solution.py:475
  68.1 1.8 %collective-permute-start.17 = (f32[1,112,128]{2,1,0:T(8,128)S(1)}, f32[1,112,128]{2,1,0:T(8,128)S(1)}, u32[]{:S(2)}, u32[]{:S(2)}) collective-permute-start(f32[1,112,128]{2,1,0:T(8,128)S(1)} %get-tuple-element.32), channel_id=1, source_target_pairs={{0,16},{1,17},{2,18},{3,19},{4,20},{5,21},{6,22},{7,23},{8,24},{9,... | collective-permute-start | bytes 172040 | tf_op jit(solution)/shard_map/ppermute | solution.py:475
  69.9 4.5 %collective-permute-done.13.recv_ref = bf16[4,128,128]{2,1,0:T(8,128)(2,1)S(1)} collective-permute-done((bf16[4,128,128]{2,1,0:T(8,128)(2,1)S(1)}, bf16[4,128,128]{2,1,0:T(8,128)(2,1)S(1)}, u32[]{:S(2)}, u32[]{:S(2)}) %collective-permute-start.13) | collective-permute-done | bytes 131104 | tf_op jit(solution)/shard_map/ppermute | solution.py:475
  74.5 0.1 collective-permute-start.14
  74.6 2.1 %collective-permute-start.18 = (f32[1,112,128]{2,1,0:T(8,128)S(1)}, f32[1,112,128]{2,1,0:T(8,128)S(1)}, u32[]{:S(2)}, u32[]{:S(2)}) collective-permute-start(f32[1,112,128]{2,1,0:T(8,128)S(1)} %shard_map.140.own_ref), channel_id=1, source_target_pairs={{0,1},{1,0},{2,3},{3,2},{4,5},{5,4},{6,7},{7,6},{8,9},{9,8},{10,11... | collective-permute-start | bytes 172040 | tf_op jit(solution)/shard_map/ppermute | solution.py:475
  76.6 4.5 %collective-permute-done.18.recv_ref = f32[1,112,128]{2,1,0:T(8,128)S(1)} collective-permute-done((f32[1,112,128]{2,1,0:T(8,128)S(1)}, f32[1,112,128]{2,1,0:T(8,128)S(1)}, u32[]{:S(2)}, u32[]{:S(2)}) %collective-permute-start.18) | collective-permute-done | bytes 57376 | tf_op jit(solution)/shard_map/ppermute | solution.py:475
  81.1 1.0 %collective-permute-start.19 = (f32[1,112,128]{2,1,0:T(8,128)S(1)}, f32[1,112,128]{2,1,0:T(8,128)S(1)}, u32[]{:S(2)}, u32[]{:S(2)}) collective-permute-start(f32[1,112,128]{2,1,0:T(8,128)S(1)} %shard_map.141.lags_ref), channel_id=1, source_target_pairs={{0,2},{1,3},{2,0},{3,1},{4,6},{5,7},{6,4},{7,5},{8,10},{9,11},{10,... | collective-permute-start | bytes 172040 | tf_op jit(solution)/shard_map/ppermute | solution.py:475
  82.1 1.7 %shard_map.126 = bf16[6,32,1024]{2,1,0:T(8,128)(2,1)} custom-call(bf16[8,192,128]{2,1,0:T(8,128)(2,1)S(1)} %copy-done.2, bf16[1024,1024]{1,0:T(8,128)(2,1)S(1)} %copy-done), custom_call_target="tpu_custom_call" | custom-call | bytes 2490368 | tf_op jit(solution)/shard_map/pallas_call | solution.py:447
  83.8 2.8 %collective-permute-done.19.more_ref = f32[1,112,128]{2,1,0:T(8,128)S(1)} collective-permute-done((f32[1,112,128]{2,1,0:T(8,128)S(1)}, f32[1,112,128]{2,1,0:T(8,128)S(1)}, u32[]{:S(2)}, u32[]{:S(2)}) %collective-permute-start.19) | collective-permute-done | bytes 57376 | tf_op jit(solution)/shard_map/ppermute | solution.py:475
  86.6 0.9 shard_map.143
  (29 shorter events, 0.2 us)
Async XLA Ops:
  0.6 12.5 %collective-permute-start.5 = (bf16[192,1024]{1,0:T(8,128)(2,1)}, bf16[192,1024]{1,0:T(8,128)(2,1)}, u32[]{:S(2)}, u32[]{:S(2)}) collective-permute-start(bf16[192,1024]{1,0:T(8,128)(2,1)} %bitcast.5), channel_id=1, source_target_pairs={{0,8},{1,9},{2,10},{3,11},{4,12},{5,13},{6,14},{7,15},{8,0},{9,1},... | collective-permute-start | bytes 1179656 | tf_op jit(solution)/shard_map/ppermute | solution.py:475
  3.7 11.7 %collective-permute-start.6 = (bf16[192,1024]{1,0:T(8,128)(2,1)}, bf16[192,1024]{1,0:T(8,128)(2,1)}, u32[]{:S(2)}, u32[]{:S(2)}) collective-permute-start(bf16[192,1024]{1,0:T(8,128)(2,1)} %bitcast.6), channel_id=1, source_target_pairs={{0,16},{1,17},{2,18},{3,19},{4,20},{5,21},{6,22},{7,23},{8,24},{9,... | collective-permute-start | bytes 1179656 | tf_op jit(solution)/shard_map/ppermute | solution.py:475
  13.1 10.5 %collective-permute-start.10 = (bf16[192,1024]{1,0:T(8,128)(2,1)}, bf16[192,1024]{1,0:T(8,128)(2,1)S(1)}, u32[]{:S(2)}, u32[]{:S(2)}) collective-permute-start(bf16[192,1024]{1,0:T(8,128)(2,1)} %collective-permute-done.5.refs_1_), channel_id=1, source_target_pairs={{0,16},{1,17},{2,18},{3,19},{4,20},{5,21},{6,22},{7,23},{8,24},{9,... | collective-permute-start | bytes 1179656 | tf_op jit(solution)/shard_map/ppermute | solution.py:475
  14.9 41.6 %collective-permute-start.7 = (bf16[192,1024]{1,0:T(8,128)(2,1)}, bf16[192,1024]{1,0:T(8,128)(2,1)}, u32[]{:S(2)}, u32[]{:S(2)}) collective-permute-start(bf16[192,1024]{1,0:T(8,128)(2,1)} %bitcast.7), channel_id=1, source_target_pairs={{0,4},{1,5},{2,6},{3,7},{4,0},{5,1},{6,2},{7,3},{8,12},{9,13},{10,... | collective-permute-start | bytes 1179656 | tf_op jit(solution)/shard_map/ppermute | solution.py:475
  14.9 41.6 %collective-permute-start.8 = (bf16[192,1024]{1,0:T(8,128)(2,1)}, bf16[192,1024]{1,0:T(8,128)(2,1)}, u32[]{:S(2)}, u32[]{:S(2)}) collective-permute-start(bf16[192,1024]{1,0:T(8,128)(2,1)} %collective-permute-done.5.refs_1_), channel_id=1, source_target_pairs={{0,4},{1,5},{2,6},{3,7},{4,0},{5,1},{6,2},{7,3},{8,12},{9,13},{10,... | collective-permute-start | bytes 1179656 | tf_op jit(solution)/shard_map/ppermute | solution.py:475
  15.4 41.1 %collective-permute-start.9 = (bf16[192,1024]{1,0:T(8,128)(2,1)}, bf16[192,1024]{1,0:T(8,128)(2,1)}, u32[]{:S(2)}, u32[]{:S(2)}) collective-permute-start(bf16[192,1024]{1,0:T(8,128)(2,1)} %collective-permute-done.6.refs_2_), channel_id=1, source_target_pairs={{0,4},{1,5},{2,6},{3,7},{4,0},{5,1},{6,2},{7,3},{8,12},{9,13},{10,... | collective-permute-start | bytes 1179656 | tf_op jit(solution)/shard_map/ppermute | solution.py:475
  23.6 34.6 %collective-permute-start.11 = (bf16[192,1024]{1,0:T(8,128)(2,1)S(1)}, bf16[192,1024]{1,0:T(8,128)(2,1)}, u32[]{:S(2)}, u32[]{:S(2)}) collective-permute-start(bf16[192,1024]{1,0:T(8,128)(2,1)S(1)} %collective-permute-done.10.refs_0_), channel_id=1, source_target_pairs={{0,4},{1,5},{2,6},{3,7},{4,0},{5,1},{6,2},{7,3},{8,12},{9,13},{10,... | collective-permute-start | bytes 1179656 | tf_op jit(solution)/shard_map/ppermute | solution.py:475
  26.8 3.2 %collective-permute-start = (f32[2,1152]{1,0:T(2,128)S(1)}, f32[2,1152]{1,0:T(2,128)S(1)}, u32[]{:S(2)}, u32[]{:S(2)}) collective-permute-start(f32[2,1152]{1,0:T(2,128)S(1)} %get-tuple-element.21.own_ref), channel_id=1, source_target_pairs={{0,5},{1,4},{2,7},{3,6},{4,1},{5,0},{6,3},{7,2},{8,13},{9,12},{10,... | collective-permute-start | bytes 27656 | tf_op jit(solution)/shard_map/ppermute | solution.py:475
  29.9 4.0 %collective-permute-start.1 = (f32[2,1152]{1,0:T(2,128)S(1)}, f32[2,1152]{1,0:T(2,128)S(1)}, u32[]{:S(2)}, u32[]{:S(2)}) collective-permute-start(f32[2,1152]{1,0:T(2,128)S(1)} %shard_map.120.own_ref), channel_id=1, source_target_pairs={{0,6},{1,7},{2,4},{3,5},{4,2},{5,3},{6,0},{7,1},{8,14},{9,15},{10,... | collective-permute-start | bytes 27656 | tf_op jit(solution)/shard_map/ppermute | solution.py:475
  34.0 3.1 %collective-permute-start.2 = (f32[2,1152]{1,0:T(2,128)S(1)}, f32[2,1152]{1,0:T(2,128)S(1)}, u32[]{:S(2)}, u32[]{:S(2)}) collective-permute-start(f32[2,1152]{1,0:T(2,128)S(1)} %shard_map.121.own_ref), channel_id=1, source_target_pairs={{0,12},{1,13},{2,14},{3,15},{4,8},{5,9},{6,10},{7,11},{8,4},{9,5},... | collective-permute-start | bytes 27656 | tf_op jit(solution)/shard_map/ppermute | solution.py:475
  37.1 3.1 %collective-permute-start.3 = (f32[2,1152]{1,0:T(2,128)S(1)}, f32[2,1152]{1,0:T(2,128)S(1)}, u32[]{:S(2)}, u32[]{:S(2)}) collective-permute-start(f32[2,1152]{1,0:T(2,128)S(1)} %shard_map.122.own_ref), channel_id=1, source_target_pairs={{0,20},{1,21},{2,22},{3,23},{4,16},{5,17},{6,18},{7,19},{8,28},{9,... | collective-permute-start | bytes 27656 | tf_op jit(solution)/shard_map/ppermute | solution.py:475
  40.2 1.3 %collective-permute-start.4 = (f32[2,1152]{1,0:T(2,128)S(1)}, f32[2,1152]{1,0:T(2,128)S(1)}, u32[]{:S(2)}, u32[]{:S(2)}) collective-permute-start(f32[2,1152]{1,0:T(2,128)S(1)} %shard_map.123.own_ref), channel_id=1, source_target_pairs={{0,4},{1,5},{2,6},{3,7},{4,0},{5,1},{6,2},{7,3},{8,12},{9,13},{10,... | collective-permute-start | bytes 27656 | tf_op jit(solution)/shard_map/ppermute | solution.py:475
  42.6 15.7 %all-to-all-start = ((bf16[8,192,128]{2,1,0:T(8,128)(2,1)}), bf16[8,192,128]{2,1,0:T(8,128)(2,1)S(1)}, u32[]{:S(2)}, u32[]{:S(2)}) async-start(bf16[8,192,128]{2,1,0:T(8,128)(2,1)} %shard_map.125.hid_ref), calls=%async_computation | async-start | bytes 786432 | tf_op jit(solution)/shard_map/all_to_all | solution.py:560
  51.5 5.0 %copy-start.1 = (bf16[6,32,1024]{2,1,0:T(8,128)(2,1)S(1)}, bf16[6,32,1024]{2,1,0:T(8,128)(2,1)}, u32[]{:S(2)}) copy-start(bf16[6,32,1024]{2,1,0:T(8,128)(2,1)} %param.9) | copy-start | bytes 1179652
  55.3 0.7 copy-start.3
  56.0 5.3 %collective-permute-start.15 = (f32[4,112,128]{2,1,0:T(8,128)}, f32[4,112,128]{2,1,0:T(8,128)}, u32[]{:S(2)}, u32[]{:S(2)}) collective-permute-start(f32[4,112,128]{2,1,0:T(8,128)} %get-tuple-element.28), channel_id=1, source_target_pairs={{0,4},{1,5},{2,6},{3,7},{4,0},{5,1},{6,2},{7,3},{8,12},{9,13},{10,... | collective-permute-start | bytes 688136 | tf_op jit(solution)/shard_map/ppermute | solution.py:475
  58.2 3.1 %copy-start.4 = (f32[4,112,128]{2,1,0:T(8,128)S(1)}, f32[4,112,128]{2,1,0:T(8,128)}, u32[]{:S(2)}) copy-start(f32[4,112,128]{2,1,0:T(8,128)} %copy-done.3) | copy-start | bytes 688132
  59.6 5.7 %collective-permute-start.12 = (bf16[4,128,128]{2,1,0:T(8,128)(2,1)S(1)}, bf16[4,128,128]{2,1,0:T(8,128)(2,1)S(1)}, u32[]{:S(2)}, u32[]{:S(2)}) collective-permute-start(bf16[4,128,128]{2,1,0:T(8,128)(2,1)S(1)} %shard_map.129), channel_id=1, source_target_pairs={{0,1},{1,0},{2,3},{3,2},{4,5},{5,4},{6,7},{7,6},{8,9},{9,8},{10,11... | collective-permute-start | bytes 393224 | tf_op jit(solution)/shard_map/ppermute | solution.py:475
  62.3 19.8 %copy-start = (bf16[1024,1024]{1,0:T(8,128)(2,1)S(1)}, bf16[1024,1024]{1,0:T(8,128)(2,1)}, u32[]{:S(2)}) copy-start(bf16[1024,1024]{1,0:T(8,128)(2,1)} %w_hbm.3) | copy-start | bytes 6291460
  62.3 19.8 %copy-start.2 = (bf16[8,192,128]{2,1,0:T(8,128)(2,1)S(1)}, bf16[8,192,128]{2,1,0:T(8,128)(2,1)}, u32[]{:S(2)}) copy-start(bf16[8,192,128]{2,1,0:T(8,128)(2,1)} %shard_map.125.hid_ref) | copy-start | bytes 1179652
  62.3 5.8 %collective-permute-start.16 = (f32[2,112,128]{2,1,0:T(8,128)S(1)}, f32[2,112,128]{2,1,0:T(8,128)S(1)}, u32[]{:S(2)}, u32[]{:S(2)}) collective-permute-start(f32[2,112,128]{2,1,0:T(8,128)S(1)} %get-tuple-element.30), channel_id=1, source_target_pairs={{0,8},{1,9},{2,10},{3,11},{4,12},{5,13},{6,14},{7,15},{8,0},{9,1},... | collective-permute-start | bytes 344072 | tf_op jit(solution)/shard_map/ppermute | solution.py:475
  65.4 9.0 %collective-permute-start.13 = (bf16[4,128,128]{2,1,0:T(8,128)(2,1)S(1)}, bf16[4,128,128]{2,1,0:T(8,128)(2,1)S(1)}, u32[]{:S(2)}, u32[]{:S(2)}) collective-permute-start(bf16[4,128,128]{2,1,0:T(8,128)(2,1)S(1)} %shard_map.130.own_ref), channel_id=1, source_target_pairs={{0,2},{1,3},{2,0},{3,1},{4,6},{5,7},{6,4},{7,5},{8,10},{9,11},{10,... | collective-permute-start | bytes 393224 | tf_op jit(solution)/shard_map/ppermute | solution.py:475
  68.1 6.5 %collective-permute-start.17 = (f32[1,112,128]{2,1,0:T(8,128)S(1)}, f32[1,112,128]{2,1,0:T(8,128)S(1)}, u32[]{:S(2)}, u32[]{:S(2)}) collective-permute-start(f32[1,112,128]{2,1,0:T(8,128)S(1)} %get-tuple-element.32), channel_id=1, source_target_pairs={{0,16},{1,17},{2,18},{3,19},{4,20},{5,21},{6,22},{7,23},{8,24},{9,... | collective-permute-start | bytes 172040 | tf_op jit(solution)/shard_map/ppermute | solution.py:475
  74.5 12.1 %collective-permute-start.14 = (bf16[4,128,128]{2,1,0:T(8,128)(2,1)S(1)}, bf16[4,128,128]{2,1,0:T(8,128)(2,1)S(1)}, u32[]{:S(2)}, u32[]{:S(2)}) collective-permute-start(bf16[4,128,128]{2,1,0:T(8,128)(2,1)S(1)} %shard_map.131.own_ref), channel_id=1, source_target_pairs={{0,1},{1,0},{2,3},{3,2},{4,5},{5,4},{6,7},{7,6},{8,9},{9,8},{10,11... | collective-permute-start | bytes 393224 | tf_op jit(solution)/shard_map/ppermute | solution.py:475
  74.6 6.5 %collective-permute-start.18 = (f32[1,112,128]{2,1,0:T(8,128)S(1)}, f32[1,112,128]{2,1,0:T(8,128)S(1)}, u32[]{:S(2)}, u32[]{:S(2)}) collective-permute-start(f32[1,112,128]{2,1,0:T(8,128)S(1)} %shard_map.140.own_ref), channel_id=1, source_target_pairs={{0,1},{1,0},{2,3},{3,2},{4,5},{5,4},{6,7},{7,6},{8,9},{9,8},{10,11... | collective-permute-start | bytes 172040 | tf_op jit(solution)/shard_map/ppermute | solution.py:475
  81.1 5.5 %collective-permute-start.19 = (f32[1,112,128]{2,1,0:T(8,128)S(1)}, f32[1,112,128]{2,1,0:T(8,128)S(1)}, u32[]{:S(2)}, u32[]{:S(2)}) collective-permute-start(f32[1,112,128]{2,1,0:T(8,128)S(1)} %shard_map.141.lags_ref), channel_id=1, source_target_pairs={{0,2},{1,3},{2,0},{3,1},{4,6},{5,7},{6,4},{7,5},{8,10},{9,11},{10,... | collective-permute-start | bytes 172040 | tf_op jit(solution)/shard_map/ppermute | solution.py:475

commit v7 on v5

--- a/solution.py
+++ b/solution.py
@@ -228,18 +228,8 @@
     lax.fori_loop(0, many, one, 0)
 
 
-def back_body(cotan_hbm, w_hbm, out_ref, cotan_ref, w_ref, sems):
-    blocks = out_ref.shape[0]
-    fetch = pltpu.make_async_copy(cotan_hbm, cotan_ref, sems.at[blocks])
-    fetch.start()
-    copies = []
-    for block in range(blocks):
-        rows = pl.ds(block * LANES, LANES)
-        copies.append(pltpu.make_async_copy(w_hbm.at[rows], w_ref.at[rows], sems.at[block]))
-        copies[-1].start()
-    fetch.wait()
-    for block in range(blocks):
-        copies[block].wait()
+def back_body(cotan_ref, w_ref, out_ref):
+    for block in range(out_ref.shape[0]):
         rows = w_ref[block * LANES : (block + 1) * LANES, :]
         out_ref[block] = lax.dot_general(
             cotan_ref[...], rows, (((1,), (1,)), ((), ())), preferred_element_type=F32
@@ -502,14 +492,8 @@
         back_body,
         shape((blocks, tokens, LANES), F32),
         (),
-        (in_hbm(flat_cotan), in_hbm(w_out)),
+        (flat_cotan, w_out),
         flops=2 * tokens * width * width,
-        scratch=[
-            pltpu.VMEM(flat_cotan.shape, BF16),
-            pltpu.VMEM(w_out.shape, BF16),
-            pltpu.SemaphoreType.DMA((blocks + 1,)),
-        ],
-        in_specs=[HBM] * 2,
     )
     parts = blocks // 2
     each = 2

time: 87.5 us -> 84.8 us (0.969)
  Pallas kernels: 22.3 us -> 19.3 us
    pallas_call x24, Pallas kernels: 22.3 us -> 19.3 us  [call(): pl.pallas_call(body, in_specs=more.pop('in_specs', None) or [SMEM] * len(...]
  transfers between devices with their start and end apart: 21 -> 21, of which waited for: 10 -> 10; matrix products, arithmetic and copies ran while one was open for 0% -> 0% of each run, Pallas kernels for 25% -> 22%
where the time goes in v7:
time: 84.8 us; the launch traced here: 84.4 us
  starting transfers between devices  32.2 us (38%)
  waiting for transfers between devices  31.2 us (37%)
  Pallas kernels  19.3 us (23%)
  local copies, waits for them, and re-layouts  0.97 us (1%)
    ppermute x20, waiting for transfers between devices, swap(): return lax.ppermute(value, ('dp', 'grp'), pairs)  31.2 us
    ppermute x20, starting transfers between devices, swap(): return lax.ppermute(value, ('dp', 'grp'), pairs)  28.5 us
    pallas_call x24, Pallas kernels, call(): pl.pallas_call(body, in_specs=more.pop('in_specs', None) or [SMEM] * len(...  19.3 us
    all_to_all x1, starting transfers between devices, local_fast(): received = lax.all_to_all(hidden, 'dp', 0, 0, tiled=True)  3.69 us
  transfers between devices with their start and end apart: 21, of which 10 were waited for; matrix products, arithmetic and copies ran while one was open for 0% of the time, Pallas kernels for 22%

profile of v7, /device:TPU:0, one launch (start us, length us, event | category | flops | bytes accessed | tf_op | source)
XLA Modules:
  0.0 84.4 jit_solution(9065016050948567175)
XLA Ops:
  0.6 3.0 %collective-permute-start.5 = (bf16[192,1024]{1,0:T(8,128)(2,1)}, bf16[192,1024]{1,0:T(8,128)(2,1)}, u32[]{:S(2)}, u32[]{:S(2)}) collective-permute-start(bf16[192,1024]{1,0:T(8,128)(2,1)} %bitcast.5), channel_id=1, source_target_pairs={{0,8},{1,9},{2,10},{3,11},{4,12},{5,13},{6,14},{7,15},{8,0},{9,1},... | collective-permute-start | bytes 1179656 | tf_op jit(solution)/shard_map/ppermute | solution.py:444
  3.7 1.5 %collective-permute-start.6 = (bf16[192,1024]{1,0:T(8,128)(2,1)}, bf16[192,1024]{1,0:T(8,128)(2,1)}, u32[]{:S(2)}, u32[]{:S(2)}) collective-permute-start(bf16[192,1024]{1,0:T(8,128)(2,1)} %bitcast.6), channel_id=1, source_target_pairs={{0,16},{1,17},{2,18},{3,19},{4,20},{5,21},{6,22},{7,23},{8,24},{9,... | collective-permute-start | bytes 1179656 | tf_op jit(solution)/shard_map/ppermute | solution.py:444
  5.2 7.9 %collective-permute-done.5.refs_1_ = bf16[192,1024]{1,0:T(8,128)(2,1)} collective-permute-done((bf16[192,1024]{1,0:T(8,128)(2,1)}, bf16[192,1024]{1,0:T(8,128)(2,1)}, u32[]{:S(2)}, u32[]{:S(2)}) %collective-permute-start.5) | collective-permute-done | bytes 393248 | tf_op jit(solution)/shard_map/ppermute | solution.py:444
  13.1 1.8 %collective-permute-start.10 = (bf16[192,1024]{1,0:T(8,128)(2,1)}, bf16[192,1024]{1,0:T(8,128)(2,1)S(1)}, u32[]{:S(2)}, u32[]{:S(2)}) collective-permute-start(bf16[192,1024]{1,0:T(8,128)(2,1)} %collective-permute-done.5.refs_1_), channel_id=1, source_target_pairs={{0,16},{1,17},{2,18},{3,19},{4,20},{5,21},{6,22},{7,23},{8,24},{9,... | collective-permute-start | bytes 1179656 | tf_op jit(solution)/shard_map/ppermute | solution.py:444
  14.9 0.5 collective-permute-start.8
  15.4 0.0 collective-permute-start.9
  15.4 8.2 %collective-permute-done.10.refs_0_ = bf16[192,1024]{1,0:T(8,128)(2,1)S(1)} collective-permute-done((bf16[192,1024]{1,0:T(8,128)(2,1)}, bf16[192,1024]{1,0:T(8,128)(2,1)S(1)}, u32[]{:S(2)}, u32[]{:S(2)}) %collective-permute-start.10) | collective-permute-done | bytes 393248 | tf_op jit(solution)/shard_map/ppermute | solution.py:444
  23.6 3.2 %shard_map.119 = (f32[8,6,64,128]{3,2,1,0:T(8,128)S(1)}, f32[8,6,32,128]{3,2,1,0:T(8,128)S(1)}, f32[2,1152]{1,0:T(2,128)S(1)}, f32[6,32,128]{2,1,0:T(8,128)S(1)}...) custom-call(s32[6]{0:T(128)} %len_hbm.1, s32[6]{0:T(128)} %off_hbm.1, bf16[6,32,2048]{2,1,0:T(8,128)(2,1)} %acts_hbm.1, ...), custom_call_target="tpu_custom_call" | custom-call | flops 25165824 | bytes 925744 | tf_op jit(solution)/shard_map/pallas_call | solution.py:416
  26.8 1.7 %collective-permute-start = (f32[2,1152]{1,0:T(2,128)S(1)}, f32[2,1152]{1,0:T(2,128)S(1)}, u32[]{:S(2)}, u32[]{:S(2)}) collective-permute-start(f32[2,1152]{1,0:T(2,128)S(1)} %get-tuple-element.23.own_ref), channel_id=1, source_target_pairs={{0,5},{1,4},{2,7},{3,6},{4,1},{5,0},{6,3},{7,2},{8,13},{9,12},{10,... | collective-permute-start | bytes 27656 | tf_op jit(solution)/shard_map/ppermute | solution.py:444
  28.5 1.4 %collective-permute-done.recv_ref = f32[2,1152]{1,0:T(2,128)S(1)} collective-permute-done((f32[2,1152]{1,0:T(2,128)S(1)}, f32[2,1152]{1,0:T(2,128)S(1)}, u32[]{:S(2)}, u32[]{:S(2)}) %collective-permute-start) | collective-permute-done | bytes 9248 | tf_op jit(solution)/shard_map/ppermute | solution.py:444
  29.9 2.7 %collective-permute-start.1 = (f32[2,1152]{1,0:T(2,128)S(1)}, f32[2,1152]{1,0:T(2,128)S(1)}, u32[]{:S(2)}, u32[]{:S(2)}) collective-permute-start(f32[2,1152]{1,0:T(2,128)S(1)} %shard_map.120.own_ref), channel_id=1, source_target_pairs={{0,6},{1,7},{2,4},{3,5},{4,2},{5,3},{6,0},{7,1},{8,14},{9,15},{10,... | collective-permute-start | bytes 27656 | tf_op jit(solution)/shard_map/ppermute | solution.py:444
  32.6 1.4 %collective-permute-done.1.recv_ref = f32[2,1152]{1,0:T(2,128)S(1)} collective-permute-done((f32[2,1152]{1,0:T(2,128)S(1)}, f32[2,1152]{1,0:T(2,128)S(1)}, u32[]{:S(2)}, u32[]{:S(2)}) %collective-permute-start.1) | collective-permute-done | bytes 9248 | tf_op jit(solution)/shard_map/ppermute | solution.py:444
  34.0 1.5 %collective-permute-start.2 = (f32[2,1152]{1,0:T(2,128)S(1)}, f32[2,1152]{1,0:T(2,128)S(1)}, u32[]{:S(2)}, u32[]{:S(2)}) collective-permute-start(f32[2,1152]{1,0:T(2,128)S(1)} %shard_map.121.own_ref), channel_id=1, source_target_pairs={{0,12},{1,13},{2,14},{3,15},{4,8},{5,9},{6,10},{7,11},{8,4},{9,5},... | collective-permute-start | bytes 27656 | tf_op jit(solution)/shard_map/ppermute | solution.py:444
  35.5 1.6 %collective-permute-done.2.recv_ref = f32[2,1152]{1,0:T(2,128)S(1)} collective-permute-done((f32[2,1152]{1,0:T(2,128)S(1)}, f32[2,1152]{1,0:T(2,128)S(1)}, u32[]{:S(2)}, u32[]{:S(2)}) %collective-permute-start.2) | collective-permute-done | bytes 9248 | tf_op jit(solution)/shard_map/ppermute | solution.py:444
  37.1 1.5 %collective-permute-start.3 = (f32[2,1152]{1,0:T(2,128)S(1)}, f32[2,1152]{1,0:T(2,128)S(1)}, u32[]{:S(2)}, u32[]{:S(2)}) collective-permute-start(f32[2,1152]{1,0:T(2,128)S(1)} %shard_map.122.own_ref), channel_id=1, source_target_pairs={{0,20},{1,21},{2,22},{3,23},{4,16},{5,17},{6,18},{7,19},{8,28},{9,... | collective-permute-start | bytes 27656 | tf_op jit(solution)/shard_map/ppermute | solution.py:444
  38.6 1.5 %collective-permute-done.3.recv_ref = f32[2,1152]{1,0:T(2,128)S(1)} collective-permute-done((f32[2,1152]{1,0:T(2,128)S(1)}, f32[2,1152]{1,0:T(2,128)S(1)}, u32[]{:S(2)}, u32[]{:S(2)}) %collective-permute-start.3) | collective-permute-done | bytes 9248 | tf_op jit(solution)/shard_map/ppermute | solution.py:444
  40.2 0.5 collective-permute-start.4
  40.6 0.8 collective-permute-done.4.recv_ref
  41.4 1.2 %shard_map.125.hid_ref = bf16[8,192,128]{2,1,0:T(8,128)(2,1)} custom-call(f32[2,1152]{1,0:T(2,128)S(1)} %shard_map.124.st_ref, f32[2,8,128]{2,1,0:T(8,128)S(1)} %get-tuple-element.24.gb_ref, f32[6,32,128]{2,1,0:T(8,128)S(1)} %get-tuple-element.25.ok_ref, f32[8,6,32,128]{3,2,1,0:T(8,128)S(1)} %get-tuple-element.26.cv_ref), custom_call_target="tpu_custom_call" | custom-call | bytes 902144 | tf_op jit(solution)/shard_map/pallas_call | solution.py:416
  42.6 3.7 %all-to-all-start = ((bf16[8,192,128]{2,1,0:T(8,128)(2,1)}), bf16[8,192,128]{2,1,0:T(8,128)(2,1)S(1)}, u32[]{:S(2)}, u32[]{:S(2)}) async-start(bf16[8,192,128]{2,1,0:T(8,128)(2,1)} %shard_map.125.hid_ref), calls=%async_computation | async-start | bytes 786432 | tf_op jit(solution)/shard_map/all_to_all | solution.py:515
  46.3 0.7 shard_map.132.refs_0_
  47.0 0.7 shard_map.133.refs_1_
  47.6 0.0 copy-start
  47.7 0.0 copy-start.2
  47.7 0.7 shard_map.134.refs_2_
  48.3 0.7 shard_map.135.refs_3_
  49.0 0.2 copy-done
  49.2 0.0 copy-done.2
  49.3 1.0 %shard_map.131.bk_ref = f32[8,192,128]{2,1,0:T(8,128)S(1)} custom-call(bf16[192,1024]{1,0:T(8,128)(2,1)S(1)} %bitcast.8, bf16[1024,1024]{1,0:T(8,128)(2,1)S(1)} %copy-done), custom_call_target="tpu_custom_call" | custom-call | flops 402653184 | bytes 2490368 | tf_op jit(solution)/shard_map/pallas_call | solution.py:416
  50.2 3.0 %shard_map.136 = (f32[4,112,128]{2,1,0:T(8,128)}, f32[4,112,128]{2,1,0:T(8,128)S(1)}) custom-call(f32[2,1152]{1,0:T(2,128)S(1)} %shard_map.124.st_ref, f32[2,8,128]{2,1,0:T(8,128)S(1)} %get-tuple-element.24.gb_ref, f32[6,32,128]{2,1,0:T(8,128)S(1)} %get-tuple-element.25.ok_ref, f32[8,6,64,128]{3,2,1,0:T(8,128)S(1)} %get-tuple-element.29.gp_ref, ...), custom_call_target="tpu_custom_call" | custom-call | flops 25165824 | bytes 3523584 | tf_op jit(solution)/shard_map/pallas_call | solution.py:416
  53.3 0.7 copy-done.3
  54.0 0.5 collective-permute-start.15
  54.5 1.7 %shard_map.127.staged_ref = bf16[6,192,1024]{2,1,0:T(8,128)(2,1)S(1)} custom-call(bf16[192,1024]{1,0:T(8,128)(2,1)S(1)} %bitcast.9, bf16[192,1024]{1,0:T(8,128)(2,1)} %collective-permute-done.5.refs_1_, bf16[192,1024]{1,0:T(8,128)(2,1)} %collective-permute-done.6.refs_2_, bf16[192,1024]{1,0:T(8,128)(2,1)} %collective-permute-done.7.refs_3_, ...), custom_call_target="tpu_custom_call" | custom-call | bytes 2359296 | tf_op jit(solution)/shard_map/pallas_call | solution.py:416
  56.2 0.0 copy-start.1
  56.2 1.9 %shard_map.128 = (bf16[4,128,128]{2,1,0:T(8,128)(2,1)S(1)}, bf16[4,128,128]{2,1,0:T(8,128)(2,1)S(1)}) custom-call(bf16[8,192,128]{2,1,0:T(8,128)(2,1)S(1)} %all-to-all-done.recv_hbm, bf16[6,192,1024]{2,1,0:T(8,128)(2,1)S(1)} %shard_map.127.staged_ref, bf16[192,1024]{1,0:T(8,128)(2,1)S(1)} %collective-permute-done.10.refs_0_, ...), custom_call_target="tpu_custom_call" | custom-call | flops 402653184 | bytes 3538944 | tf_op jit(solution)/shard_map/pallas_call | solution.py:416
  58.1 1.6 %collective-permute-start.12 = (bf16[4,128,128]{2,1,0:T(8,128)(2,1)S(1)}, bf16[4,128,128]{2,1,0:T(8,128)(2,1)S(1)}, u32[]{:S(2)}, u32[]{:S(2)}) collective-permute-start(bf16[4,128,128]{2,1,0:T(8,128)(2,1)S(1)} %get-tuple-element.28), channel_id=1, source_target_pairs={{0,1},{1,0},{2,3},{3,2},{4,5},{5,4},{6,7},{7,6},{8,9},{9,8},{10,11... | collective-permute-start | bytes 393224 | tf_op jit(solution)/shard_map/ppermute | solution.py:444
  59.8 1.0 %shard_map.137 = (f32[2,112,128]{2,1,0:T(8,128)S(1)}, f32[2,112,128]{2,1,0:T(8,128)S(1)}) custom-call(f32[4,112,128]{2,1,0:T(8,128)S(1)} %copy-done.4, f32[4,112,128]{2,1,0:T(8,128)} %collective-permute-done.15.recv_ref), custom_call_target="tpu_custom_call" | custom-call | bytes 458752 | tf_op jit(solution)/shard_map/pallas_call | solution.py:416
  60.8 1.7 %collective-permute-start.16 = (f32[2,112,128]{2,1,0:T(8,128)S(1)}, f32[2,112,128]{2,1,0:T(8,128)S(1)}, u32[]{:S(2)}, u32[]{:S(2)}) collective-permute-start(f32[2,112,128]{2,1,0:T(8,128)S(1)} %get-tuple-element.34), channel_id=1, source_target_pairs={{0,8},{1,9},{2,10},{3,11},{4,12},{5,13},{6,14},{7,15},{8,0},{9,1},... | collective-permute-start | bytes 344072 | tf_op jit(solution)/shard_map/ppermute | solution.py:444
  62.5 1.2 %collective-permute-done.12.recv_ref = bf16[4,128,128]{2,1,0:T(8,128)(2,1)S(1)} collective-permute-done((bf16[4,128,128]{2,1,0:T(8,128)(2,1)S(1)}, bf16[4,128,128]{2,1,0:T(8,128)(2,1)S(1)}, u32[]{:S(2)}, u32[]{:S(2)}) %collective-permute-start.12) | collective-permute-done | bytes 131104 | tf_op jit(solution)/shard_map/ppermute | solution.py:444
  63.7 2.7 %collective-permute-start.13 = (bf16[4,128,128]{2,1,0:T(8,128)(2,1)S(1)}, bf16[4,128,128]{2,1,0:T(8,128)(2,1)S(1)}, u32[]{:S(2)}, u32[]{:S(2)}) collective-permute-start(bf16[4,128,128]{2,1,0:T(8,128)(2,1)S(1)} %shard_map.129.own_ref), channel_id=1, source_target_pairs={{0,2},{1,3},{2,0},{3,1},{4,6},{5,7},{6,4},{7,5},{8,10},{9,11},{10,... | collective-permute-start | bytes 393224 | tf_op jit(solution)/shard_map/ppermute | solution.py:444
  66.3 2.1 %collective-permute-start.17 = (f32[1,112,128]{2,1,0:T(8,128)S(1)}, f32[1,112,128]{2,1,0:T(8,128)S(1)}, u32[]{:S(2)}, u32[]{:S(2)}) collective-permute-start(f32[1,112,128]{2,1,0:T(8,128)S(1)} %get-tuple-element.36), channel_id=1, source_target_pairs={{0,16},{1,17},{2,18},{3,19},{4,20},{5,21},{6,22},{7,23},{8,24},{9,... | collective-permute-start | bytes 172040 | tf_op jit(solution)/shard_map/ppermute | solution.py:444
  68.4 3.6 %collective-permute-done.13.recv_ref = bf16[4,128,128]{2,1,0:T(8,128)(2,1)S(1)} collective-permute-done((bf16[4,128,128]{2,1,0:T(8,128)(2,1)S(1)}, bf16[4,128,128]{2,1,0:T(8,128)(2,1)S(1)}, u32[]{:S(2)}, u32[]{:S(2)}) %collective-permute-start.13) | collective-permute-done | bytes 131104 | tf_op jit(solution)/shard_map/ppermute | solution.py:444
  72.0 0.7 collective-permute-start.14
  72.8 1.4 %collective-permute-start.18 = (f32[1,112,128]{2,1,0:T(8,128)S(1)}, f32[1,112,128]{2,1,0:T(8,128)S(1)}, u32[]{:S(2)}, u32[]{:S(2)}) collective-permute-start(f32[1,112,128]{2,1,0:T(8,128)S(1)} %shard_map.139.own_ref), channel_id=1, source_target_pairs={{0,1},{1,0},{2,3},{3,2},{4,5},{5,4},{6,7},{7,6},{8,9},{9,8},{10,11... | collective-permute-start | bytes 172040 | tf_op jit(solution)/shard_map/ppermute | solution.py:444
  74.2 3.5 %collective-permute-done.18.recv_ref = f32[1,112,128]{2,1,0:T(8,128)S(1)} collective-permute-done((f32[1,112,128]{2,1,0:T(8,128)S(1)}, f32[1,112,128]{2,1,0:T(8,128)S(1)}, u32[]{:S(2)}, u32[]{:S(2)}) %collective-permute-start.18) | collective-permute-done | bytes 57376 | tf_op jit(solution)/shard_map/ppermute | solution.py:444
  77.7 3.1 %collective-permute-start.19 = (f32[1,112,128]{2,1,0:T(8,128)S(1)}, f32[1,112,128]{2,1,0:T(8,128)S(1)}, u32[]{:S(2)}, u32[]{:S(2)}) collective-permute-start(f32[1,112,128]{2,1,0:T(8,128)S(1)} %shard_map.140.lags_ref), channel_id=1, source_target_pairs={{0,2},{1,3},{2,0},{3,1},{4,6},{5,7},{6,4},{7,5},{8,10},{9,11},{10,... | collective-permute-start | bytes 172040 | tf_op jit(solution)/shard_map/ppermute | solution.py:444
  80.8 2.7 %shard_map.126 = bf16[6,32,1024]{2,1,0:T(8,128)(2,1)} custom-call(bf16[8,192,128]{2,1,0:T(8,128)(2,1)} %shard_map.125.hid_ref, bf16[1024,1024]{1,0:T(8,128)(2,1)S(1)} %copy-done.1), custom_call_target="tpu_custom_call" | custom-call | bytes 2490368 | tf_op jit(solution)/shard_map/pallas_call | solution.py:416
  83.5 0.9 %shard_map.142 = (f32[128,1024]{1,0:T(8,128)}, f32[32,128]{1,0:T(8,128)}, f32[8,128]{1,0:T(8,128)}, f32[8,128]{1,0:T(8,128)}) custom-call(bf16[4,128,128]{2,1,0:T(8,128)(2,1)S(1)} %shard_map.130.own_ref, bf16[4,128,128]{2,1,0:T(8,128)(2,1)S(1)} %collective-permute-done.14.recv_ref, f32[1,112,128]{2,1,0:T(8,128)S(1)} %shard_map.140.lags_ref, ...), custom_call_target="tpu_custom_call" | custom-call | bytes 377856 | tf_op jit(solution)/shard_map/pallas_call | solution.py:416
  (28 shorter events, 0.2 us)
Async XLA Ops:
  0.6 12.5 %collective-permute-start.5 = (bf16[192,1024]{1,0:T(8,128)(2,1)}, bf16[192,1024]{1,0:T(8,128)(2,1)}, u32[]{:S(2)}, u32[]{:S(2)}) collective-permute-start(bf16[192,1024]{1,0:T(8,128)(2,1)} %bitcast.5), channel_id=1, source_target_pairs={{0,8},{1,9},{2,10},{3,11},{4,12},{5,13},{6,14},{7,15},{8,0},{9,1},... | collective-permute-start | bytes 1179656 | tf_op jit(solution)/shard_map/ppermute | solution.py:444
  3.7 11.7 %collective-permute-start.6 = (bf16[192,1024]{1,0:T(8,128)(2,1)}, bf16[192,1024]{1,0:T(8,128)(2,1)}, u32[]{:S(2)}, u32[]{:S(2)}) collective-permute-start(bf16[192,1024]{1,0:T(8,128)(2,1)} %bitcast.6), channel_id=1, source_target_pairs={{0,16},{1,17},{2,18},{3,19},{4,20},{5,21},{6,22},{7,23},{8,24},{9,... | collective-permute-start | bytes 1179656 | tf_op jit(solution)/shard_map/ppermute | solution.py:444
  13.1 10.5 %collective-permute-start.10 = (bf16[192,1024]{1,0:T(8,128)(2,1)}, bf16[192,1024]{1,0:T(8,128)(2,1)S(1)}, u32[]{:S(2)}, u32[]{:S(2)}) collective-permute-start(bf16[192,1024]{1,0:T(8,128)(2,1)} %collective-permute-done.5.refs_1_), channel_id=1, source_target_pairs={{0,16},{1,17},{2,18},{3,19},{4,20},{5,21},{6,22},{7,23},{8,24},{9,... | collective-permute-start | bytes 1179656 | tf_op jit(solution)/shard_map/ppermute | solution.py:444
  14.9 39.6 %collective-permute-start.7 = (bf16[192,1024]{1,0:T(8,128)(2,1)}, bf16[192,1024]{1,0:T(8,128)(2,1)}, u32[]{:S(2)}, u32[]{:S(2)}) collective-permute-start(bf16[192,1024]{1,0:T(8,128)(2,1)} %bitcast.7), channel_id=1, source_target_pairs={{0,4},{1,5},{2,6},{3,7},{4,0},{5,1},{6,2},{7,3},{8,12},{9,13},{10,... | collective-permute-start | bytes 1179656 | tf_op jit(solution)/shard_map/ppermute | solution.py:444
  14.9 39.6 %collective-permute-start.8 = (bf16[192,1024]{1,0:T(8,128)(2,1)}, bf16[192,1024]{1,0:T(8,128)(2,1)}, u32[]{:S(2)}, u32[]{:S(2)}) collective-permute-start(bf16[192,1024]{1,0:T(8,128)(2,1)} %collective-permute-done.5.refs_1_), channel_id=1, source_target_pairs={{0,4},{1,5},{2,6},{3,7},{4,0},{5,1},{6,2},{7,3},{8,12},{9,13},{10,... | collective-permute-start | bytes 1179656 | tf_op jit(solution)/shard_map/ppermute | solution.py:444
  15.4 39.1 %collective-permute-start.9 = (bf16[192,1024]{1,0:T(8,128)(2,1)}, bf16[192,1024]{1,0:T(8,128)(2,1)}, u32[]{:S(2)}, u32[]{:S(2)}) collective-permute-start(bf16[192,1024]{1,0:T(8,128)(2,1)} %collective-permute-done.6.refs_2_), channel_id=1, source_target_pairs={{0,4},{1,5},{2,6},{3,7},{4,0},{5,1},{6,2},{7,3},{8,12},{9,13},{10,... | collective-permute-start | bytes 1179656 | tf_op jit(solution)/shard_map/ppermute | solution.py:444
  23.6 32.6 %collective-permute-start.11 = (bf16[192,1024]{1,0:T(8,128)(2,1)S(1)}, bf16[192,1024]{1,0:T(8,128)(2,1)}, u32[]{:S(2)}, u32[]{:S(2)}) collective-permute-start(bf16[192,1024]{1,0:T(8,128)(2,1)S(1)} %collective-permute-done.10.refs_0_), channel_id=1, source_target_pairs={{0,4},{1,5},{2,6},{3,7},{4,0},{5,1},{6,2},{7,3},{8,12},{9,13},{10,... | collective-permute-start | bytes 1179656 | tf_op jit(solution)/shard_map/ppermute | solution.py:444
  26.8 3.2 %collective-permute-start = (f32[2,1152]{1,0:T(2,128)S(1)}, f32[2,1152]{1,0:T(2,128)S(1)}, u32[]{:S(2)}, u32[]{:S(2)}) collective-permute-start(f32[2,1152]{1,0:T(2,128)S(1)} %get-tuple-element.23.own_ref), channel_id=1, source_target_pairs={{0,5},{1,4},{2,7},{3,6},{4,1},{5,0},{6,3},{7,2},{8,13},{9,12},{10,... | collective-permute-start | bytes 27656 | tf_op jit(solution)/shard_map/ppermute | solution.py:444
  29.9 4.0 %collective-permute-start.1 = (f32[2,1152]{1,0:T(2,128)S(1)}, f32[2,1152]{1,0:T(2,128)S(1)}, u32[]{:S(2)}, u32[]{:S(2)}) collective-permute-start(f32[2,1152]{1,0:T(2,128)S(1)} %shard_map.120.own_ref), channel_id=1, source_target_pairs={{0,6},{1,7},{2,4},{3,5},{4,2},{5,3},{6,0},{7,1},{8,14},{9,15},{10,... | collective-permute-start | bytes 27656 | tf_op jit(solution)/shard_map/ppermute | solution.py:444
  34.0 3.1 %collective-permute-start.2 = (f32[2,1152]{1,0:T(2,128)S(1)}, f32[2,1152]{1,0:T(2,128)S(1)}, u32[]{:S(2)}, u32[]{:S(2)}) collective-permute-start(f32[2,1152]{1,0:T(2,128)S(1)} %shard_map.121.own_ref), channel_id=1, source_target_pairs={{0,12},{1,13},{2,14},{3,15},{4,8},{5,9},{6,10},{7,11},{8,4},{9,5},... | collective-permute-start | bytes 27656 | tf_op jit(solution)/shard_map/ppermute | solution.py:444
  37.1 3.1 %collective-permute-start.3 = (f32[2,1152]{1,0:T(2,128)S(1)}, f32[2,1152]{1,0:T(2,128)S(1)}, u32[]{:S(2)}, u32[]{:S(2)}) collective-permute-start(f32[2,1152]{1,0:T(2,128)S(1)} %shard_map.122.own_ref), channel_id=1, source_target_pairs={{0,20},{1,21},{2,22},{3,23},{4,16},{5,17},{6,18},{7,19},{8,28},{9,... | collective-permute-start | bytes 27656 | tf_op jit(solution)/shard_map/ppermute | solution.py:444
  40.2 1.3 %collective-permute-start.4 = (f32[2,1152]{1,0:T(2,128)S(1)}, f32[2,1152]{1,0:T(2,128)S(1)}, u32[]{:S(2)}, u32[]{:S(2)}) collective-permute-start(f32[2,1152]{1,0:T(2,128)S(1)} %shard_map.123.own_ref), channel_id=1, source_target_pairs={{0,4},{1,5},{2,6},{3,7},{4,0},{5,1},{6,2},{7,3},{8,12},{9,13},{10,... | collective-permute-start | bytes 27656 | tf_op jit(solution)/shard_map/ppermute | solution.py:444
  42.6 13.6 %all-to-all-start = ((bf16[8,192,128]{2,1,0:T(8,128)(2,1)}), bf16[8,192,128]{2,1,0:T(8,128)(2,1)S(1)}, u32[]{:S(2)}, u32[]{:S(2)}) async-start(bf16[8,192,128]{2,1,0:T(8,128)(2,1)} %shard_map.125.hid_ref), calls=%async_computation | async-start | bytes 786432 | tf_op jit(solution)/shard_map/all_to_all | solution.py:515
  47.6 1.6 %copy-start = (bf16[1024,1024]{1,0:T(8,128)(2,1)S(1)}, bf16[1024,1024]{1,0:T(8,128)(2,1)}, u32[]{:S(2)}) copy-start(bf16[1024,1024]{1,0:T(8,128)(2,1)} %w_ref.3) | copy-start | bytes 6291460
  47.7 1.6 %copy-start.2 = (bf16[6,32,1024]{2,1,0:T(8,128)(2,1)S(1)}, bf16[6,32,1024]{2,1,0:T(8,128)(2,1)}, u32[]{:S(2)}) copy-start(bf16[6,32,1024]{2,1,0:T(8,128)(2,1)} %param.9) | copy-start | bytes 1179652
  53.3 0.7 copy-start.3
  54.0 5.8 %collective-permute-start.15 = (f32[4,112,128]{2,1,0:T(8,128)}, f32[4,112,128]{2,1,0:T(8,128)}, u32[]{:S(2)}, u32[]{:S(2)}) collective-permute-start(f32[4,112,128]{2,1,0:T(8,128)} %get-tuple-element.32), channel_id=1, source_target_pairs={{0,4},{1,5},{2,6},{3,7},{4,0},{5,1},{6,2},{7,3},{8,12},{9,13},{10,... | collective-permute-start | bytes 688136 | tf_op jit(solution)/shard_map/ppermute | solution.py:444
  56.2 3.6 %copy-start.4 = (f32[4,112,128]{2,1,0:T(8,128)S(1)}, f32[4,112,128]{2,1,0:T(8,128)}, u32[]{:S(2)}) copy-start(f32[4,112,128]{2,1,0:T(8,128)} %copy-done.3) | copy-start | bytes 688132
  56.2 24.6 %copy-start.1 = (bf16[1024,1024]{1,0:T(8,128)(2,1)S(1)}, bf16[1024,1024]{1,0:T(8,128)(2,1)}, u32[]{:S(2)}) copy-start(bf16[1024,1024]{1,0:T(8,128)(2,1)} %w_ref.3) | copy-start | bytes 6291460
  58.1 5.5 %collective-permute-start.12 = (bf16[4,128,128]{2,1,0:T(8,128)(2,1)S(1)}, bf16[4,128,128]{2,1,0:T(8,128)(2,1)S(1)}, u32[]{:S(2)}, u32[]{:S(2)}) collective-permute-start(bf16[4,128,128]{2,1,0:T(8,128)(2,1)S(1)} %get-tuple-element.28), channel_id=1, source_target_pairs={{0,1},{1,0},{2,3},{3,2},{4,5},{5,4},{6,7},{7,6},{8,9},{9,8},{10,11... | collective-permute-start | bytes 393224 | tf_op jit(solution)/shard_map/ppermute | solution.py:444
  60.8 5.6 %collective-permute-start.16 = (f32[2,112,128]{2,1,0:T(8,128)S(1)}, f32[2,112,128]{2,1,0:T(8,128)S(1)}, u32[]{:S(2)}, u32[]{:S(2)}) collective-permute-start(f32[2,112,128]{2,1,0:T(8,128)S(1)} %get-tuple-element.34), channel_id=1, source_target_pairs={{0,8},{1,9},{2,10},{3,11},{4,12},{5,13},{6,14},{7,15},{8,0},{9,1},... | collective-permute-start | bytes 344072 | tf_op jit(solution)/shard_map/ppermute | solution.py:444
  63.7 8.3 %collective-permute-start.13 = (bf16[4,128,128]{2,1,0:T(8,128)(2,1)S(1)}, bf16[4,128,128]{2,1,0:T(8,128)(2,1)S(1)}, u32[]{:S(2)}, u32[]{:S(2)}) collective-permute-start(bf16[4,128,128]{2,1,0:T(8,128)(2,1)S(1)} %shard_map.129.own_ref), channel_id=1, source_target_pairs={{0,2},{1,3},{2,0},{3,1},{4,6},{5,7},{6,4},{7,5},{8,10},{9,11},{10,... | collective-permute-start | bytes 393224 | tf_op jit(solution)/shard_map/ppermute | solution.py:444
  66.3 6.4 %collective-permute-start.17 = (f32[1,112,128]{2,1,0:T(8,128)S(1)}, f32[1,112,128]{2,1,0:T(8,128)S(1)}, u32[]{:S(2)}, u32[]{:S(2)}) collective-permute-start(f32[1,112,128]{2,1,0:T(8,128)S(1)} %get-tuple-element.36), channel_id=1, source_target_pairs={{0,16},{1,17},{2,18},{3,19},{4,20},{5,21},{6,22},{7,23},{8,24},{9,... | collective-permute-start | bytes 172040 | tf_op jit(solution)/shard_map/ppermute | solution.py:444
  72.0 11.5 %collective-permute-start.14 = (bf16[4,128,128]{2,1,0:T(8,128)(2,1)S(1)}, bf16[4,128,128]{2,1,0:T(8,128)(2,1)S(1)}, u32[]{:S(2)}, u32[]{:S(2)}) collective-permute-start(bf16[4,128,128]{2,1,0:T(8,128)(2,1)S(1)} %shard_map.130.own_ref), channel_id=1, source_target_pairs={{0,1},{1,0},{2,3},{3,2},{4,5},{5,4},{6,7},{7,6},{8,9},{9,8},{10,11... | collective-permute-start | bytes 393224 | tf_op jit(solution)/shard_map/ppermute | solution.py:444
  72.8 4.9 %collective-permute-start.18 = (f32[1,112,128]{2,1,0:T(8,128)S(1)}, f32[1,112,128]{2,1,0:T(8,128)S(1)}, u32[]{:S(2)}, u32[]{:S(2)}) collective-permute-start(f32[1,112,128]{2,1,0:T(8,128)S(1)} %shard_map.139.own_ref), channel_id=1, source_target_pairs={{0,1},{1,0},{2,3},{3,2},{4,5},{5,4},{6,7},{7,6},{8,9},{9,8},{10,11... | collective-permute-start | bytes 172040 | tf_op jit(solution)/shard_map/ppermute | solution.py:444
  77.7 5.8 %collective-permute-start.19 = (f32[1,112,128]{2,1,0:T(8,128)S(1)}, f32[1,112,128]{2,1,0:T(8,128)S(1)}, u32[]{:S(2)}, u32[]{:S(2)}) collective-permute-start(f32[1,112,128]{2,1,0:T(8,128)S(1)} %shard_map.140.lags_ref), channel_id=1, source_target_pairs={{0,2},{1,3},{2,0},{3,1},{4,6},{5,7},{6,4},{7,5},{8,10},{9,11},{10,... | collective-permute-start | bytes 172040 | tf_op jit(solution)/shard_map/ppermute | solution.py:444

commit v8 on v7

--- a/solution.py
+++ b/solution.py
@@ -452,12 +452,12 @@
 
     flat_cotan = cotan.reshape(tokens, width)
     pieces = [(0, flat_cotan)]
-    for bit in dp_bits[1:] + dp_bits[:1]:
+    for bit in dp_bits[:0:-1] + dp_bits[:1]:
         pieces += [(m | bit, swap(v, bit, 0)) for m, v in pieces]
     late_bits = dp_bits[-1] | dp_bits[-2]
     pieces.sort(key=lambda piece: piece[0] & late_bits == late_bits)
     masks, values = tuple(m for m, _ in pieces), [v for _, v in pieces]
-    early = sum(m & late_bits != late_bits for m in masks)
+    early = n_dp - 1
 
     gated, conv_out, stats, valid, inside, gains = call(
         conv_body,
@@ -484,7 +484,8 @@
         in_specs=[HBM] * 6,
     )
 
-    hops = [(1, m) for m in grp_bits] + [(m | 1, 0) for m in dp_bits[1:]] + [(1, 0)]
+    hops = [(m | 1, 0) for m in dp_bits[1:2]] + [(1, m) for m in grp_bits]
+    hops += [(1, 0)] + [(m | 1, 0) for m in dp_bits[2:]]
     for dp_mask, grp_mask in hops:
         stats = plus(stats, swap(stats, dp_mask, grp_mask))
 

time: 84.8 us -> 84.5 us (level)
  transfers between devices with their start and end apart: 21 -> 21, of which waited for: 10 -> 10; matrix products, arithmetic and copies ran while one was open for 0% -> 0% of each run, Pallas kernels for 22% -> 21%
where the time goes in v8:
time: 84.5 us; the launch traced here: 84.1 us
  starting transfers between devices  32 us (38%)
  waiting for transfers between devices  31.5 us (37%)
  Pallas kernels  18.7 us (22%)
  local copies, waits for them, and re-layouts  1.01 us (1%)
    ppermute x20, waiting for transfers between devices, swap(): return lax.ppermute(value, ('dp', 'grp'), pairs)  31.5 us
    ppermute x20, starting transfers between devices, swap(): return lax.ppermute(value, ('dp', 'grp'), pairs)  28.4 us
    pallas_call x24, Pallas kernels, call(): pl.pallas_call(body, in_specs=more.pop('in_specs', None) or [SMEM] * len(...  18.7 us
    all_to_all x1, starting transfers between devices, local_fast(): received = lax.all_to_all(hidden, 'dp', 0, 0, tiled=True)  3.66 us
  transfers between devices with their start and end apart: 21, of which 10 were waited for; matrix products, arithmetic and copies ran while one was open for 0% of the time, Pallas kernels for 21%

profile of v8, /device:TPU:0, one launch (start us, length us, event | category | flops | bytes accessed | tf_op | source)
XLA Modules:
  0.0 84.1 jit_solution(15484619245466817382)
XLA Ops:
  0.6 3.1 %collective-permute-start.5 = (bf16[192,1024]{1,0:T(8,128)(2,1)}, bf16[192,1024]{1,0:T(8,128)(2,1)}, u32[]{:S(2)}, u32[]{:S(2)}) collective-permute-start(bf16[192,1024]{1,0:T(8,128)(2,1)} %bitcast.5), channel_id=1, source_target_pairs={{0,16},{1,17},{2,18},{3,19},{4,20},{5,21},{6,22},{7,23},{8,24},{9,... | collective-permute-start | bytes 1179656 | tf_op jit(solution)/shard_map/ppermute | solution.py:444
  3.7 1.5 %collective-permute-start.6 = (bf16[192,1024]{1,0:T(8,128)(2,1)}, bf16[192,1024]{1,0:T(8,128)(2,1)}, u32[]{:S(2)}, u32[]{:S(2)}) collective-permute-start(bf16[192,1024]{1,0:T(8,128)(2,1)} %bitcast.6), channel_id=1, source_target_pairs={{0,8},{1,9},{2,10},{3,11},{4,12},{5,13},{6,14},{7,15},{8,0},{9,1},... | collective-permute-start | bytes 1179656 | tf_op jit(solution)/shard_map/ppermute | solution.py:444
  5.2 7.9 %collective-permute-done.5.refs_1_ = bf16[192,1024]{1,0:T(8,128)(2,1)} collective-permute-done((bf16[192,1024]{1,0:T(8,128)(2,1)}, bf16[192,1024]{1,0:T(8,128)(2,1)}, u32[]{:S(2)}, u32[]{:S(2)}) %collective-permute-start.5) | collective-permute-done | bytes 393248 | tf_op jit(solution)/shard_map/ppermute | solution.py:444
  13.1 1.7 %collective-permute-start.10 = (bf16[192,1024]{1,0:T(8,128)(2,1)}, bf16[192,1024]{1,0:T(8,128)(2,1)}, u32[]{:S(2)}, u32[]{:S(2)}) collective-permute-start(bf16[192,1024]{1,0:T(8,128)(2,1)} %collective-permute-done.5.refs_1_), channel_id=1, source_target_pairs={{0,8},{1,9},{2,10},{3,11},{4,12},{5,13},{6,14},{7,15},{8,0},{9,1},... | collective-permute-start | bytes 1179656 | tf_op jit(solution)/shard_map/ppermute | solution.py:444
  14.8 0.5 collective-permute-start.8
  15.4 8.4 %collective-permute-done.10.refs_6_ = bf16[192,1024]{1,0:T(8,128)(2,1)} collective-permute-done((bf16[192,1024]{1,0:T(8,128)(2,1)}, bf16[192,1024]{1,0:T(8,128)(2,1)}, u32[]{:S(2)}, u32[]{:S(2)}) %collective-permute-start.10) | collective-permute-done | bytes 393248 | tf_op jit(solution)/shard_map/ppermute | solution.py:444
  23.7 3.2 %shard_map.119 = (f32[8,6,64,128]{3,2,1,0:T(8,128)S(1)}, f32[8,6,32,128]{3,2,1,0:T(8,128)S(1)}, f32[2,1152]{1,0:T(2,128)S(1)}, f32[6,32,128]{2,1,0:T(8,128)S(1)}...) custom-call(s32[6]{0:T(128)} %len_hbm.1, s32[6]{0:T(128)} %off_hbm.1, bf16[6,32,2048]{2,1,0:T(8,128)(2,1)} %acts_hbm.1, ...), custom_call_target="tpu_custom_call" | custom-call | flops 25165824 | bytes 925744 | tf_op jit(solution)/shard_map/pallas_call | solution.py:416
  26.9 0.0 copy-start.5
  26.9 1.6 %collective-permute-start = (f32[2,1152]{1,0:T(2,128)S(1)}, f32[2,1152]{1,0:T(2,128)S(1)}, u32[]{:S(2)}, u32[]{:S(2)}) collective-permute-start(f32[2,1152]{1,0:T(2,128)S(1)} %get-tuple-element.23.own_ref), channel_id=1, source_target_pairs={{0,12},{1,13},{2,14},{3,15},{4,8},{5,9},{6,10},{7,11},{8,4},{9,5},... | collective-permute-start | bytes 27656 | tf_op jit(solution)/shard_map/ppermute | solution.py:444
  28.5 1.5 %collective-permute-done.recv_ref = f32[2,1152]{1,0:T(2,128)S(1)} collective-permute-done((f32[2,1152]{1,0:T(2,128)S(1)}, f32[2,1152]{1,0:T(2,128)S(1)}, u32[]{:S(2)}, u32[]{:S(2)}) %collective-permute-start) | collective-permute-done | bytes 9248 | tf_op jit(solution)/shard_map/ppermute | solution.py:444
  30.1 1.6 %collective-permute-start.1 = (f32[2,1152]{1,0:T(2,128)S(1)}, f32[2,1152]{1,0:T(2,128)S(1)}, u32[]{:S(2)}, u32[]{:S(2)}) collective-permute-start(f32[2,1152]{1,0:T(2,128)S(1)} %shard_map.120.own_ref), channel_id=1, source_target_pairs={{0,5},{1,4},{2,7},{3,6},{4,1},{5,0},{6,3},{7,2},{8,13},{9,12},{10,... | collective-permute-start | bytes 27656 | tf_op jit(solution)/shard_map/ppermute | solution.py:444
  31.7 1.5 %collective-permute-done.1.recv_ref = f32[2,1152]{1,0:T(2,128)S(1)} collective-permute-done((f32[2,1152]{1,0:T(2,128)S(1)}, f32[2,1152]{1,0:T(2,128)S(1)}, u32[]{:S(2)}, u32[]{:S(2)}) %collective-permute-start.1) | collective-permute-done | bytes 9248 | tf_op jit(solution)/shard_map/ppermute | solution.py:444
  33.2 2.6 %collective-permute-start.2 = (f32[2,1152]{1,0:T(2,128)S(1)}, f32[2,1152]{1,0:T(2,128)S(1)}, u32[]{:S(2)}, u32[]{:S(2)}) collective-permute-start(f32[2,1152]{1,0:T(2,128)S(1)} %shard_map.121.own_ref), channel_id=1, source_target_pairs={{0,6},{1,7},{2,4},{3,5},{4,2},{5,3},{6,0},{7,1},{8,14},{9,15},{10,... | collective-permute-start | bytes 27656 | tf_op jit(solution)/shard_map/ppermute | solution.py:444
  35.8 1.4 %collective-permute-done.2.recv_ref = f32[2,1152]{1,0:T(2,128)S(1)} collective-permute-done((f32[2,1152]{1,0:T(2,128)S(1)}, f32[2,1152]{1,0:T(2,128)S(1)}, u32[]{:S(2)}, u32[]{:S(2)}) %collective-permute-start.2) | collective-permute-done | bytes 9248 | tf_op jit(solution)/shard_map/ppermute | solution.py:444
  37.2 0.5 collective-permute-start.3
  37.7 0.8 collective-permute-done.3.recv_ref
  38.5 1.4 %collective-permute-start.4 = (f32[2,1152]{1,0:T(2,128)S(1)}, f32[2,1152]{1,0:T(2,128)S(1)}, u32[]{:S(2)}, u32[]{:S(2)}) collective-permute-start(f32[2,1152]{1,0:T(2,128)S(1)} %shard_map.123.own_ref), channel_id=1, source_target_pairs={{0,20},{1,21},{2,22},{3,23},{4,16},{5,17},{6,18},{7,19},{8,28},{9,... | collective-permute-start | bytes 27656 | tf_op jit(solution)/shard_map/ppermute | solution.py:444
  39.9 1.7 %collective-permute-done.4.recv_ref = f32[2,1152]{1,0:T(2,128)S(1)} collective-permute-done((f32[2,1152]{1,0:T(2,128)S(1)}, f32[2,1152]{1,0:T(2,128)S(1)}, u32[]{:S(2)}, u32[]{:S(2)}) %collective-permute-start.4) | collective-permute-done | bytes 9248 | tf_op jit(solution)/shard_map/ppermute | solution.py:444
  41.6 1.2 %shard_map.125.hid_ref = bf16[8,192,128]{2,1,0:T(8,128)(2,1)} custom-call(f32[2,1152]{1,0:T(2,128)S(1)} %shard_map.124.st_ref, f32[2,8,128]{2,1,0:T(8,128)S(1)} %get-tuple-element.24.gb_ref, f32[6,32,128]{2,1,0:T(8,128)S(1)} %get-tuple-element.25.ok_ref, f32[8,6,32,128]{3,2,1,0:T(8,128)S(1)} %get-tuple-element.26.cv_ref), custom_call_target="tpu_custom_call" | custom-call | bytes 902144 | tf_op jit(solution)/shard_map/pallas_call | solution.py:416
  42.7 3.7 %all-to-all-start = ((bf16[8,192,128]{2,1,0:T(8,128)(2,1)}), bf16[8,192,128]{2,1,0:T(8,128)(2,1)S(1)}, u32[]{:S(2)}, u32[]{:S(2)}) async-start(bf16[8,192,128]{2,1,0:T(8,128)(2,1)} %shard_map.125.hid_ref), calls=%async_computation | async-start | bytes 786432 | tf_op jit(solution)/shard_map/all_to_all | solution.py:516
  46.4 0.7 shard_map.132.refs_0_
  47.1 0.7 shard_map.133.refs_1_
  47.8 0.0 copy-start
  47.8 0.0 copy-start.2
  47.8 0.7 shard_map.134.refs_2_
  48.5 0.7 shard_map.135.refs_3_
  49.1 0.2 copy-done
  49.4 0.0 copy-done.2
  49.4 1.0 %shard_map.131.bk_ref = f32[8,192,128]{2,1,0:T(8,128)S(1)} custom-call(bf16[192,1024]{1,0:T(8,128)(2,1)S(1)} %bitcast.8, bf16[1024,1024]{1,0:T(8,128)(2,1)S(1)} %copy-done), custom_call_target="tpu_custom_call" | custom-call | flops 402653184 | bytes 2490368 | tf_op jit(solution)/shard_map/pallas_call | solution.py:416
  50.4 3.0 %shard_map.136 = (f32[4,112,128]{2,1,0:T(8,128)}, f32[4,112,128]{2,1,0:T(8,128)S(1)}) custom-call(f32[2,1152]{1,0:T(2,128)S(1)} %shard_map.124.st_ref, f32[2,8,128]{2,1,0:T(8,128)S(1)} %get-tuple-element.24.gb_ref, f32[6,32,128]{2,1,0:T(8,128)S(1)} %get-tuple-element.25.ok_ref, f32[8,6,64,128]{3,2,1,0:T(8,128)S(1)} %get-tuple-element.29.gp_ref, ...), custom_call_target="tpu_custom_call" | custom-call | flops 25165824 | bytes 3523584 | tf_op jit(solution)/shard_map/pallas_call | solution.py:416
  53.4 0.7 copy-done.3
  54.1 0.5 collective-permute-start.15
  54.6 1.8 %shard_map.127.staged_ref = bf16[7,192,1024]{2,1,0:T(8,128)(2,1)S(1)} custom-call(bf16[192,1024]{1,0:T(8,128)(2,1)S(1)} %bitcast.9, bf16[192,1024]{1,0:T(8,128)(2,1)} %collective-permute-done.5.refs_1_, bf16[192,1024]{1,0:T(8,128)(2,1)} %collective-permute-done.6.refs_2_, bf16[192,1024]{1,0:T(8,128)(2,1)} %collective-permute-done.7.refs_3_, ...), custom_call_target="tpu_custom_call" | custom-call | bytes 2752512 | tf_op jit(solution)/shard_map/pallas_call | solution.py:416
  56.5 0.0 copy-start.1
  56.5 1.2 %shard_map.128 = (bf16[4,128,128]{2,1,0:T(8,128)(2,1)S(1)}, bf16[4,128,128]{2,1,0:T(8,128)(2,1)S(1)}) custom-call(bf16[8,192,128]{2,1,0:T(8,128)(2,1)S(1)} %all-to-all-done.recv_hbm, bf16[7,192,1024]{2,1,0:T(8,128)(2,1)S(1)} %shard_map.127.staged_ref, bf16[192,1024]{1,0:T(8,128)(2,1)S(1)} %collective-permute-done.11.refs_0_), custom_call_target="tpu_custom_call" | custom-call | flops 402653184 | bytes 3538944 | tf_op jit(solution)/shard_map/pallas_call | solution.py:416
  57.8 1.6 %collective-permute-start.12 = (bf16[4,128,128]{2,1,0:T(8,128)(2,1)S(1)}, bf16[4,128,128]{2,1,0:T(8,128)(2,1)S(1)}, u32[]{:S(2)}, u32[]{:S(2)}) collective-permute-start(bf16[4,128,128]{2,1,0:T(8,128)(2,1)S(1)} %get-tuple-element.28), channel_id=1, source_target_pairs={{0,1},{1,0},{2,3},{3,2},{4,5},{5,4},{6,7},{7,6},{8,9},{9,8},{10,11... | collective-permute-start | bytes 393224 | tf_op jit(solution)/shard_map/ppermute | solution.py:444
  59.4 1.0 %shard_map.137 = (f32[2,112,128]{2,1,0:T(8,128)S(1)}, f32[2,112,128]{2,1,0:T(8,128)S(1)}) custom-call(f32[4,112,128]{2,1,0:T(8,128)S(1)} %copy-done.4, f32[4,112,128]{2,1,0:T(8,128)} %collective-permute-done.15.recv_ref), custom_call_target="tpu_custom_call" | custom-call | bytes 458752 | tf_op jit(solution)/shard_map/pallas_call | solution.py:416
  60.4 1.7 %collective-permute-start.16 = (f32[2,112,128]{2,1,0:T(8,128)S(1)}, f32[2,112,128]{2,1,0:T(8,128)S(1)}, u32[]{:S(2)}, u32[]{:S(2)}) collective-permute-start(f32[2,112,128]{2,1,0:T(8,128)S(1)} %get-tuple-element.34), channel_id=1, source_target_pairs={{0,8},{1,9},{2,10},{3,11},{4,12},{5,13},{6,14},{7,15},{8,0},{9,1},... | collective-permute-start | bytes 344072 | tf_op jit(solution)/shard_map/ppermute | solution.py:444
  62.1 1.2 %collective-permute-done.12.recv_ref = bf16[4,128,128]{2,1,0:T(8,128)(2,1)S(1)} collective-permute-done((bf16[4,128,128]{2,1,0:T(8,128)(2,1)S(1)}, bf16[4,128,128]{2,1,0:T(8,128)(2,1)S(1)}, u32[]{:S(2)}, u32[]{:S(2)}) %collective-permute-start.12) | collective-permute-done | bytes 131104 | tf_op jit(solution)/shard_map/ppermute | solution.py:444
  63.3 2.7 %collective-permute-start.13 = (bf16[4,128,128]{2,1,0:T(8,128)(2,1)S(1)}, bf16[4,128,128]{2,1,0:T(8,128)(2,1)S(1)}, u32[]{:S(2)}, u32[]{:S(2)}) collective-permute-start(bf16[4,128,128]{2,1,0:T(8,128)(2,1)S(1)} %shard_map.129.own_ref), channel_id=1, source_target_pairs={{0,2},{1,3},{2,0},{3,1},{4,6},{5,7},{6,4},{7,5},{8,10},{9,11},{10,... | collective-permute-start | bytes 393224 | tf_op jit(solution)/shard_map/ppermute | solution.py:444
  66.0 2.1 %collective-permute-start.17 = (f32[1,112,128]{2,1,0:T(8,128)S(1)}, f32[1,112,128]{2,1,0:T(8,128)S(1)}, u32[]{:S(2)}, u32[]{:S(2)}) collective-permute-start(f32[1,112,128]{2,1,0:T(8,128)S(1)} %get-tuple-element.36), channel_id=1, source_target_pairs={{0,16},{1,17},{2,18},{3,19},{4,20},{5,21},{6,22},{7,23},{8,24},{9,... | collective-permute-start | bytes 172040 | tf_op jit(solution)/shard_map/ppermute | solution.py:444
  68.0 3.6 %collective-permute-done.13.recv_ref = bf16[4,128,128]{2,1,0:T(8,128)(2,1)S(1)} collective-permute-done((bf16[4,128,128]{2,1,0:T(8,128)(2,1)S(1)}, bf16[4,128,128]{2,1,0:T(8,128)(2,1)S(1)}, u32[]{:S(2)}, u32[]{:S(2)}) %collective-permute-start.13) | collective-permute-done | bytes 131104 | tf_op jit(solution)/shard_map/ppermute | solution.py:444
  71.7 0.7 collective-permute-start.14
  72.4 1.4 %collective-permute-start.18 = (f32[1,112,128]{2,1,0:T(8,128)S(1)}, f32[1,112,128]{2,1,0:T(8,128)S(1)}, u32[]{:S(2)}, u32[]{:S(2)}) collective-permute-start(f32[1,112,128]{2,1,0:T(8,128)S(1)} %shard_map.139.own_ref), channel_id=1, source_target_pairs={{0,1},{1,0},{2,3},{3,2},{4,5},{5,4},{6,7},{7,6},{8,9},{9,8},{10,11... | collective-permute-start | bytes 172040 | tf_op jit(solution)/shard_map/ppermute | solution.py:444
  73.8 3.5 %collective-permute-done.18.recv_ref = f32[1,112,128]{2,1,0:T(8,128)S(1)} collective-permute-done((f32[1,112,128]{2,1,0:T(8,128)S(1)}, f32[1,112,128]{2,1,0:T(8,128)S(1)}, u32[]{:S(2)}, u32[]{:S(2)}) %collective-permute-start.18) | collective-permute-done | bytes 57376 | tf_op jit(solution)/shard_map/ppermute | solution.py:444
  77.4 3.1 %collective-permute-start.19 = (f32[1,112,128]{2,1,0:T(8,128)S(1)}, f32[1,112,128]{2,1,0:T(8,128)S(1)}, u32[]{:S(2)}, u32[]{:S(2)}) collective-permute-start(f32[1,112,128]{2,1,0:T(8,128)S(1)} %shard_map.140.lags_ref), channel_id=1, source_target_pairs={{0,2},{1,3},{2,0},{3,1},{4,6},{5,7},{6,4},{7,5},{8,10},{9,11},{10,... | collective-permute-start | bytes 172040 | tf_op jit(solution)/shard_map/ppermute | solution.py:444
  80.5 2.7 %shard_map.126 = bf16[6,32,1024]{2,1,0:T(8,128)(2,1)} custom-call(bf16[8,192,128]{2,1,0:T(8,128)(2,1)} %shard_map.125.hid_ref, bf16[1024,1024]{1,0:T(8,128)(2,1)S(1)} %copy-done.1), custom_call_target="tpu_custom_call" | custom-call | bytes 2490368 | tf_op jit(solution)/shard_map/pallas_call | solution.py:416
  83.2 0.9 %shard_map.142 = (f32[128,1024]{1,0:T(8,128)}, f32[32,128]{1,0:T(8,128)}, f32[8,128]{1,0:T(8,128)}, f32[8,128]{1,0:T(8,128)}) custom-call(bf16[4,128,128]{2,1,0:T(8,128)(2,1)S(1)} %shard_map.130.own_ref, bf16[4,128,128]{2,1,0:T(8,128)(2,1)S(1)} %collective-permute-done.14.recv_ref, f32[1,112,128]{2,1,0:T(8,128)S(1)} %shard_map.140.lags_ref, ...), custom_call_target="tpu_custom_call" | custom-call | bytes 377856 | tf_op jit(solution)/shard_map/pallas_call | solution.py:416
  (32 shorter events, 0.2 us)
Async XLA Ops:
  0.6 12.5 %collective-permute-start.5 = (bf16[192,1024]{1,0:T(8,128)(2,1)}, bf16[192,1024]{1,0:T(8,128)(2,1)}, u32[]{:S(2)}, u32[]{:S(2)}) collective-permute-start(bf16[192,1024]{1,0:T(8,128)(2,1)} %bitcast.5), channel_id=1, source_target_pairs={{0,16},{1,17},{2,18},{3,19},{4,20},{5,21},{6,22},{7,23},{8,24},{9,... | collective-permute-start | bytes 1179656 | tf_op jit(solution)/shard_map/ppermute | solution.py:444
  3.7 11.7 %collective-permute-start.6 = (bf16[192,1024]{1,0:T(8,128)(2,1)}, bf16[192,1024]{1,0:T(8,128)(2,1)}, u32[]{:S(2)}, u32[]{:S(2)}) collective-permute-start(bf16[192,1024]{1,0:T(8,128)(2,1)} %bitcast.6), channel_id=1, source_target_pairs={{0,8},{1,9},{2,10},{3,11},{4,12},{5,13},{6,14},{7,15},{8,0},{9,1},... | collective-permute-start | bytes 1179656 | tf_op jit(solution)/shard_map/ppermute | solution.py:444
  13.1 10.6 %collective-permute-start.10 = (bf16[192,1024]{1,0:T(8,128)(2,1)}, bf16[192,1024]{1,0:T(8,128)(2,1)}, u32[]{:S(2)}, u32[]{:S(2)}) collective-permute-start(bf16[192,1024]{1,0:T(8,128)(2,1)} %collective-permute-done.5.refs_1_), channel_id=1, source_target_pairs={{0,8},{1,9},{2,10},{3,11},{4,12},{5,13},{6,14},{7,15},{8,0},{9,1},... | collective-permute-start | bytes 1179656 | tf_op jit(solution)/shard_map/ppermute | solution.py:444
  14.8 39.8 %collective-permute-start.7 = (bf16[192,1024]{1,0:T(8,128)(2,1)}, bf16[192,1024]{1,0:T(8,128)(2,1)}, u32[]{:S(2)}, u32[]{:S(2)}) collective-permute-start(bf16[192,1024]{1,0:T(8,128)(2,1)} %bitcast.7), channel_id=1, source_target_pairs={{0,4},{1,5},{2,6},{3,7},{4,0},{5,1},{6,2},{7,3},{8,12},{9,13},{10,... | collective-permute-start | bytes 1179656 | tf_op jit(solution)/shard_map/ppermute | solution.py:444
  14.8 39.8 %collective-permute-start.8 = (bf16[192,1024]{1,0:T(8,128)(2,1)}, bf16[192,1024]{1,0:T(8,128)(2,1)}, u32[]{:S(2)}, u32[]{:S(2)}) collective-permute-start(bf16[192,1024]{1,0:T(8,128)(2,1)} %collective-permute-done.5.refs_1_), channel_id=1, source_target_pairs={{0,4},{1,5},{2,6},{3,7},{4,0},{5,1},{6,2},{7,3},{8,12},{9,13},{10,... | collective-permute-start | bytes 1179656 | tf_op jit(solution)/shard_map/ppermute | solution.py:444
  15.4 39.3 %collective-permute-start.9 = (bf16[192,1024]{1,0:T(8,128)(2,1)}, bf16[192,1024]{1,0:T(8,128)(2,1)}, u32[]{:S(2)}, u32[]{:S(2)}) collective-permute-start(bf16[192,1024]{1,0:T(8,128)(2,1)} %collective-permute-done.6.refs_2_), channel_id=1, source_target_pairs={{0,4},{1,5},{2,6},{3,7},{4,0},{5,1},{6,2},{7,3},{8,12},{9,13},{10,... | collective-permute-start | bytes 1179656 | tf_op jit(solution)/shard_map/ppermute | solution.py:444
  23.7 32.8 %collective-permute-start.11 = (bf16[192,1024]{1,0:T(8,128)(2,1)}, bf16[192,1024]{1,0:T(8,128)(2,1)S(1)}, u32[]{:S(2)}, u32[]{:S(2)}) collective-permute-start(bf16[192,1024]{1,0:T(8,128)(2,1)} %collective-permute-done.10.refs_6_), channel_id=1, source_target_pairs={{0,4},{1,5},{2,6},{3,7},{4,0},{5,1},{6,2},{7,3},{8,12},{9,13},{10,... | collective-permute-start | bytes 1179656 | tf_op jit(solution)/shard_map/ppermute | solution.py:444
  26.9 23.5 %copy-start.5 = (f32[2,8,128]{2,1,0:T(8,128)}, f32[2,8,128]{2,1,0:T(8,128)S(1)}, u32[]{:S(2)}) copy-start(f32[2,8,128]{2,1,0:T(8,128)S(1)} %get-tuple-element.24.gb_ref) | copy-start | bytes 24580
  26.9 3.2 %collective-permute-start = (f32[2,1152]{1,0:T(2,128)S(1)}, f32[2,1152]{1,0:T(2,128)S(1)}, u32[]{:S(2)}, u32[]{:S(2)}) collective-permute-start(f32[2,1152]{1,0:T(2,128)S(1)} %get-tuple-element.23.own_ref), channel_id=1, source_target_pairs={{0,12},{1,13},{2,14},{3,15},{4,8},{5,9},{6,10},{7,11},{8,4},{9,5},... | collective-permute-start | bytes 27656 | tf_op jit(solution)/shard_map/ppermute | solution.py:444
  30.1 3.1 %collective-permute-start.1 = (f32[2,1152]{1,0:T(2,128)S(1)}, f32[2,1152]{1,0:T(2,128)S(1)}, u32[]{:S(2)}, u32[]{:S(2)}) collective-permute-start(f32[2,1152]{1,0:T(2,128)S(1)} %shard_map.120.own_ref), channel_id=1, source_target_pairs={{0,5},{1,4},{2,7},{3,6},{4,1},{5,0},{6,3},{7,2},{8,13},{9,12},{10,... | collective-permute-start | bytes 27656 | tf_op jit(solution)/shard_map/ppermute | solution.py:444
  33.2 4.0 %collective-permute-start.2 = (f32[2,1152]{1,0:T(2,128)S(1)}, f32[2,1152]{1,0:T(2,128)S(1)}, u32[]{:S(2)}, u32[]{:S(2)}) collective-permute-start(f32[2,1152]{1,0:T(2,128)S(1)} %shard_map.121.own_ref), channel_id=1, source_target_pairs={{0,6},{1,7},{2,4},{3,5},{4,2},{5,3},{6,0},{7,1},{8,14},{9,15},{10,... | collective-permute-start | bytes 27656 | tf_op jit(solution)/shard_map/ppermute | solution.py:444
  37.2 1.3 %collective-permute-start.3 = (f32[2,1152]{1,0:T(2,128)S(1)}, f32[2,1152]{1,0:T(2,128)S(1)}, u32[]{:S(2)}, u32[]{:S(2)}) collective-permute-start(f32[2,1152]{1,0:T(2,128)S(1)} %shard_map.122.own_ref), channel_id=1, source_target_pairs={{0,4},{1,5},{2,6},{3,7},{4,0},{5,1},{6,2},{7,3},{8,12},{9,13},{10,... | collective-permute-start | bytes 27656 | tf_op jit(solution)/shard_map/ppermute | solution.py:444
  38.5 3.1 %collective-permute-start.4 = (f32[2,1152]{1,0:T(2,128)S(1)}, f32[2,1152]{1,0:T(2,128)S(1)}, u32[]{:S(2)}, u32[]{:S(2)}) collective-permute-start(f32[2,1152]{1,0:T(2,128)S(1)} %shard_map.123.own_ref), channel_id=1, source_target_pairs={{0,20},{1,21},{2,22},{3,23},{4,16},{5,17},{6,18},{7,19},{8,28},{9,... | collective-permute-start | bytes 27656 | tf_op jit(solution)/shard_map/ppermute | solution.py:444
  42.7 13.7 %all-to-all-start = ((bf16[8,192,128]{2,1,0:T(8,128)(2,1)}), bf16[8,192,128]{2,1,0:T(8,128)(2,1)S(1)}, u32[]{:S(2)}, u32[]{:S(2)}) async-start(bf16[8,192,128]{2,1,0:T(8,128)(2,1)} %shard_map.125.hid_ref), calls=%async_computation | async-start | bytes 786432 | tf_op jit(solution)/shard_map/all_to_all | solution.py:516
  47.8 1.6 %copy-start = (bf16[1024,1024]{1,0:T(8,128)(2,1)S(1)}, bf16[1024,1024]{1,0:T(8,128)(2,1)}, u32[]{:S(2)}) copy-start(bf16[1024,1024]{1,0:T(8,128)(2,1)} %w_ref.3) | copy-start | bytes 6291460
  47.8 1.6 %copy-start.2 = (bf16[6,32,1024]{2,1,0:T(8,128)(2,1)S(1)}, bf16[6,32,1024]{2,1,0:T(8,128)(2,1)}, u32[]{:S(2)}) copy-start(bf16[6,32,1024]{2,1,0:T(8,128)(2,1)} %param.9) | copy-start | bytes 1179652
  53.4 0.7 copy-start.3
  54.1 5.3 %collective-permute-start.15 = (f32[4,112,128]{2,1,0:T(8,128)}, f32[4,112,128]{2,1,0:T(8,128)}, u32[]{:S(2)}, u32[]{:S(2)}) collective-permute-start(f32[4,112,128]{2,1,0:T(8,128)} %get-tuple-element.32), channel_id=1, source_target_pairs={{0,4},{1,5},{2,6},{3,7},{4,0},{5,1},{6,2},{7,3},{8,12},{9,13},{10,... | collective-permute-start | bytes 688136 | tf_op jit(solution)/shard_map/ppermute | solution.py:444
  56.5 2.9 %copy-start.4 = (f32[4,112,128]{2,1,0:T(8,128)S(1)}, f32[4,112,128]{2,1,0:T(8,128)}, u32[]{:S(2)}) copy-start(f32[4,112,128]{2,1,0:T(8,128)} %copy-done.3) | copy-start | bytes 688132
  56.5 24.0 %copy-start.6 = (f32[2,8,128]{2,1,0:T(8,128)S(1)}, f32[2,8,128]{2,1,0:T(8,128)}, u32[]{:S(2)}) copy-start(f32[2,8,128]{2,1,0:T(8,128)} %copy-done.5) | copy-start | bytes 24580
  56.5 24.0 %copy-start.1 = (bf16[1024,1024]{1,0:T(8,128)(2,1)S(1)}, bf16[1024,1024]{1,0:T(8,128)(2,1)}, u32[]{:S(2)}) copy-start(bf16[1024,1024]{1,0:T(8,128)(2,1)} %w_ref.3) | copy-start | bytes 6291460
  57.8 5.5 %collective-permute-start.12 = (bf16[4,128,128]{2,1,0:T(8,128)(2,1)S(1)}, bf16[4,128,128]{2,1,0:T(8,128)(2,1)S(1)}, u32[]{:S(2)}, u32[]{:S(2)}) collective-permute-start(bf16[4,128,128]{2,1,0:T(8,128)(2,1)S(1)} %get-tuple-element.28), channel_id=1, source_target_pairs={{0,1},{1,0},{2,3},{3,2},{4,5},{5,4},{6,7},{7,6},{8,9},{9,8},{10,11... | collective-permute-start | bytes 393224 | tf_op jit(solution)/shard_map/ppermute | solution.py:444
  60.4 5.6 %collective-permute-start.16 = (f32[2,112,128]{2,1,0:T(8,128)S(1)}, f32[2,112,128]{2,1,0:T(8,128)S(1)}, u32[]{:S(2)}, u32[]{:S(2)}) collective-permute-start(f32[2,112,128]{2,1,0:T(8,128)S(1)} %get-tuple-element.34), channel_id=1, source_target_pairs={{0,8},{1,9},{2,10},{3,11},{4,12},{5,13},{6,14},{7,15},{8,0},{9,1},... | collective-permute-start | bytes 344072 | tf_op jit(solution)/shard_map/ppermute | solution.py:444
  63.3 8.3 %collective-permute-start.13 = (bf16[4,128,128]{2,1,0:T(8,128)(2,1)S(1)}, bf16[4,128,128]{2,1,0:T(8,128)(2,1)S(1)}, u32[]{:S(2)}, u32[]{:S(2)}) collective-permute-start(bf16[4,128,128]{2,1,0:T(8,128)(2,1)S(1)} %shard_map.129.own_ref), channel_id=1, source_target_pairs={{0,2},{1,3},{2,0},{3,1},{4,6},{5,7},{6,4},{7,5},{8,10},{9,11},{10,... | collective-permute-start | bytes 393224 | tf_op jit(solution)/shard_map/ppermute | solution.py:444
  66.0 6.5 %collective-permute-start.17 = (f32[1,112,128]{2,1,0:T(8,128)S(1)}, f32[1,112,128]{2,1,0:T(8,128)S(1)}, u32[]{:S(2)}, u32[]{:S(2)}) collective-permute-start(f32[1,112,128]{2,1,0:T(8,128)S(1)} %get-tuple-element.36), channel_id=1, source_target_pairs={{0,16},{1,17},{2,18},{3,19},{4,20},{5,21},{6,22},{7,23},{8,24},{9,... | collective-permute-start | bytes 172040 | tf_op jit(solution)/shard_map/ppermute | solution.py:444
  71.7 11.6 %collective-permute-start.14 = (bf16[4,128,128]{2,1,0:T(8,128)(2,1)S(1)}, bf16[4,128,128]{2,1,0:T(8,128)(2,1)S(1)}, u32[]{:S(2)}, u32[]{:S(2)}) collective-permute-start(bf16[4,128,128]{2,1,0:T(8,128)(2,1)S(1)} %shard_map.130.own_ref), channel_id=1, source_target_pairs={{0,1},{1,0},{2,3},{3,2},{4,5},{5,4},{6,7},{7,6},{8,9},{9,8},{10,11... | collective-permute-start | bytes 393224 | tf_op jit(solution)/shard_map/ppermute | solution.py:444
  72.4 4.9 %collective-permute-start.18 = (f32[1,112,128]{2,1,0:T(8,128)S(1)}, f32[1,112,128]{2,1,0:T(8,128)S(1)}, u32[]{:S(2)}, u32[]{:S(2)}) collective-permute-start(f32[1,112,128]{2,1,0:T(8,128)S(1)} %shard_map.139.own_ref), channel_id=1, source_target_pairs={{0,1},{1,0},{2,3},{3,2},{4,5},{5,4},{6,7},{7,6},{8,9},{9,8},{10,11... | collective-permute-start | bytes 172040 | tf_op jit(solution)/shard_map/ppermute | solution.py:444
  77.4 5.8 %collective-permute-start.19 = (f32[1,112,128]{2,1,0:T(8,128)S(1)}, f32[1,112,128]{2,1,0:T(8,128)S(1)}, u32[]{:S(2)}, u32[]{:S(2)}) collective-permute-start(f32[1,112,128]{2,1,0:T(8,128)S(1)} %shard_map.140.lags_ref), channel_id=1, source_target_pairs={{0,2},{1,3},{2,0},{3,1},{4,6},{5,7},{6,4},{7,5},{8,10},{9,11},{10,... | collective-permute-start | bytes 172040 | tf_op jit(solution)/shard_map/ppermute | solution.py:444
